TPU v7x, 32 devices: a whole 2x2x4 slice. The times are simulated.
32 devices in a mesh: dp: 4 (over z), expert: 8 (over y, x, core).
Axes of the slice: x: 2, y: 2, z: 4, core: 2. Of those that a mesh axis runs over, the one named last changes fastest.
Arguments:
- tokens: bfloat16 [8192, 2048], P(('dp', 'expert')), may hold values from -6 to 6
- cotangent: bfloat16 [8192, 2048], P(('dp', 'expert')), may hold values from -6 to 6
- lengths: int32 [32], P(('dp', 'expert')), may hold values from 64 to 256, as said below
- deal_order: int32 [8, 4], replicated, may hold values from 0 to 3, each once within a row
- routes: int32 [8192, 8], P(('dp', 'expert')), may hold values from 0 to 15, all different within a row; in each aligned block of 256 rows (0 to 255, 256 to 511, ...) at most 144 rows name the same one
- balance_coef: float32 [1], replicated, may hold values from 0.5 to 2
- w_query: bfloat16 [2048, 2048], P('expert'), may hold values from -0.125 to 0.125
- w_key: bfloat16 [2048, 2048], P('expert'), may hold values from -0.125 to 0.125
- w_value: bfloat16 [2048, 2048], P('expert'), may hold values from -0.125 to 0.125
- w_out: bfloat16 [2048, 2048], P('expert'), may hold values from -1.5 to 1.5
- w_router: bfloat16 [2048, 16], P('expert'), may hold values from -0.0625 to 0.0625
- attn_gain: bfloat16 [2048], P('expert'), may hold values from 0.099609375 to 1.8984375
- mlp_gain: bfloat16 [2048], P('expert'), may hold values from 0.099609375 to 1.8984375
- query_gain: bfloat16 [128], P('expert'), may hold values from 0.099609375 to 1.8984375
- key_gain: bfloat16 [128], P('expert'), may hold values from 0.099609375 to 1.8984375
- w_gate: bfloat16 [16, 2048, 1024], P('expert'), may hold values from -0.125 to 0.125
- w_up: bfloat16 [16, 2048, 1024], P('expert'), may hold values from -0.125 to 0.125
- w_down: bfloat16 [16, 1024, 2048], P('expert'), may hold values from -0.75 to 0.75
Outputs:
- output: bfloat16 [8192, 2048], P(('dp', 'expert'))
- balance_loss: float32 [1], replicated
- grad_input: float32 [8192, 2048], P(('dp', 'expert'))
- grad_query: float32 [2048, 2048], P('expert')
- grad_key: float32 [2048, 2048], P('expert')
- grad_value: float32 [2048, 2048], P('expert')
- grad_out: float32 [2048, 2048], P('expert')
- grad_router: float32 [2048, 16], P('expert')
- grad_attn_gain: float32 [2048], P('expert')
- grad_mlp_gain: float32 [2048], P('expert')
- grad_query_gain: float32 [128], P('expert')
- grad_key_gain: float32 [128], P('expert')
- grad_gate: float32 [16, 2048, 1024], P('expert', 'dp')
- grad_up: float32 [16, 2048, 1024], P('expert', 'dp')
- grad_down: float32 [16, 1024, 2048], P('expert', 'dp')
Inputs may be any that keep to these rules, and one draw needn't show every extreme that they name: Each sequence's live tokens are its first lengths[s] rows; the rest are padding. The first sequence has 64 live tokens and the last is full. Each row of deal_order names every dp index once. Within the rows of one sequence no expert is named by more than 144 routes; some expert reaches 144. A token names 8 different experts.
All inputs are finite; a program needn't handle non-finite values.
Results may differ from a plain program's by a relative error of at most 0.022.
Values may be sent and summed in bfloat16 or wider, within the bound.
A program may use at most 320 MiB of HBM per device.

v0:
```python
import math

import jax
import jax.numpy as jnp
from jax import lax
from jax.sharding import PartitionSpec as P

norm_eps = 1e-06
rope_base = 50000.0
big_negative = -1e30


def norm_fwd(values, scales):
    inverse = lax.rsqrt(jnp.mean(values * values, axis=-1, keepdims=True) + norm_eps)
    return (values * inverse * scales, inverse)


def norm_back(values, inverse, scales, grad_out, sum_axes):
    scaled = grad_out * scales
    grad_in = inverse * (
        scaled - values * inverse * inverse * jnp.mean(scaled * values, axis=-1, keepdims=True)
    )
    grad_scale = jnp.sum(grad_out * values * inverse, axis=sum_axes)
    return (grad_in, grad_scale)


def rotary_tables(tok_rows, head_dim):
    half_dim = head_dim // 2
    positions = jnp.arange(tok_rows, dtype=jnp.int32).astype(jnp.float32)
    frequency = rope_base ** (
        -jnp.arange(half_dim, dtype=jnp.int32).astype(jnp.float32) * 2.0 / head_dim
    )
    angles = positions[:, None] * frequency[None, :]
    cosine = jnp.concatenate([jnp.cos(angles), jnp.cos(angles)], axis=-1)[:, None, :]
    sine_table = jnp.concatenate([jnp.sin(angles), jnp.sin(angles)], axis=-1)[:, None, :]
    return (cosine, sine_table)


def turn_half(values):
    half_dim = values.shape[-1] // 2
    return jnp.concatenate([-values[..., half_dim:], values[..., :half_dim]], axis=-1)


def rotary(values, cosine, sine_table):
    return values * cosine + turn_half(values) * sine_table


def rotary_back(grad_out, cosine, sine_table):
    return grad_out * cosine - turn_half(grad_out * sine_table)


def masked_scores(q_rot, k_rot, key_live, score_scale):
    scores = (
        jnp.einsum("thd,uhd->htu", q_rot, k_rot, preferred_element_type=jnp.float32) * score_scale
    )
    return jnp.where(key_live[None, None, :], scores, big_negative)


def body(
    tokens,
    cotangent,
    lengths,
    deal_order,
    routes,
    balance_coef,
    w_query,
    w_key,
    w_value,
    w_out,
    w_router,
    attn_gain,
    mlp_gain,
    query_gain,
    key_gain,
    w_gate,
    w_up,
    w_down,
):
    groups = lax.axis_size("expert")
    replicas = lax.axis_size("dp")
    tok_rows, model_width = tokens.shape
    block_rows = tok_rows // replicas
    total_slots = float(tok_rows * replicas * groups)
    order_row = lax.dynamic_index_in_dim(deal_order, lax.axis_index("expert"), 0, keepdims=False)
    matched = (order_row[:, None] == jnp.arange(replicas, dtype=jnp.int32)[None, :]).astype(
        jnp.int32
    )
    inverse_order = jnp.sum(matched * jnp.arange(replicas, dtype=jnp.int32)[:, None], axis=0)
    send_tokens = tokens.reshape(replicas, block_rows, model_width)[inverse_order]
    send_cot = cotangent.reshape(replicas, block_rows, model_width)[inverse_order]
    seq_tokens, seq_cot = (
        lax.all_to_all(send_tokens, "dp", split_axis=0, concat_axis=0, tiled=True),
        lax.all_to_all(send_cot, "dp", split_axis=0, concat_axis=0, tiled=True),
    )
    seq_tokens = seq_tokens.reshape(tok_rows, model_width)
    seq_cot = seq_cot.reshape(tok_rows, model_width)
    (
        wq_full,
        wk_full,
        wv_full,
        wo_full,
        router_full,
        attn_scale,
        mlp_scale,
        query_scale,
        key_scale,
    ) = (
        lax.all_gather(w_query, "expert", axis=0, tiled=True),
        lax.all_gather(w_key, "expert", axis=0, tiled=True),
        lax.all_gather(w_value, "expert", axis=0, tiled=True),
        lax.all_gather(w_out, "expert", axis=0, tiled=True),
        lax.all_gather(w_router, "expert", axis=0, tiled=True),
        lax.all_gather(attn_gain, "expert", axis=0, tiled=True),
        lax.all_gather(mlp_gain, "expert", axis=0, tiled=True),
        lax.all_gather(query_gain, "expert", axis=0, tiled=True),
        lax.all_gather(key_gain, "expert", axis=0, tiled=True),
    )
    head_dim = query_scale.shape[0]
    head_count = wq_full.shape[1] // head_dim
    all_heads = head_count * head_dim
    local_experts = w_gate.shape[0]
    experts = local_experts * groups
    top_k = routes.shape[1]
    capacity = tok_rows * top_k * 9 // (8 * experts)
    n_slots = experts * capacity
    score_scale = 1.0 / math.sqrt(head_dim)
    zero_low = jnp.zeros((), jnp.bfloat16)
    attn_g = attn_scale.astype(jnp.float32)
    mlp_g = mlp_scale.astype(jnp.float32)
    query_g = query_scale.astype(jnp.float32)
    key_g = key_scale.astype(jnp.float32)
    inputs = seq_tokens.astype(jnp.float32)
    live_rows = (jnp.arange(tok_rows, dtype=jnp.int32) < lengths[0]).astype(jnp.float32)
    key_live = live_rows > 0.5
    normed, inv_first = norm_fwd(inputs, attn_g)
    attn_in = normed.astype(jnp.bfloat16)
    q_lin = jnp.dot(attn_in, wq_full, preferred_element_type=jnp.float32).reshape(
        tok_rows, head_count, head_dim
    )
    k_lin = jnp.dot(attn_in, wk_full, preferred_element_type=jnp.float32).reshape(
        tok_rows, head_count, head_dim
    )
    v_heads = (
        jnp.dot(attn_in, wv_full, preferred_element_type=jnp.float32)
        .astype(jnp.bfloat16)
        .reshape(tok_rows, head_count, head_dim)
    )
    cosine, sine_table = rotary_tables(tok_rows, head_dim)
    q_normed, q_inverse = norm_fwd(q_lin, query_g)
    k_normed, k_inverse = norm_fwd(k_lin, key_g)
    q_rot = rotary(q_normed, cosine, sine_table).astype(jnp.bfloat16)
    k_rot = rotary(k_normed, cosine, sine_table).astype(jnp.bfloat16)
    masked = masked_scores(q_rot, k_rot, key_live, score_scale)
    row_max = jnp.max(masked, axis=-1, keepdims=True)
    log_total = row_max + jnp.log(jnp.sum(jnp.exp(masked - row_max), axis=-1, keepdims=True))
    attn_probs = jnp.exp(masked - log_total)
    probs_low = attn_probs.astype(jnp.bfloat16)
    mixed_heads = (
        jnp.einsum("htu,uhd->thd", probs_low, v_heads, preferred_element_type=jnp.float32)
        .astype(jnp.bfloat16)
        .reshape(tok_rows, all_heads)
    )
    hidden = inputs + jnp.dot(mixed_heads, wo_full, preferred_element_type=jnp.float32)
    mlp_normed, inv_second = norm_fwd(hidden, mlp_g)
    mlp_in = mlp_normed.astype(jnp.bfloat16)
    logits = jnp.dot(mlp_in, router_full, preferred_element_type=jnp.float32)
    router = jax.nn.softmax(logits, axis=-1)
    picked = (routes[:, :, None] == jnp.arange(experts, dtype=jnp.int32)[None, None, :]).astype(
        jnp.float32
    )
    chosen = jnp.sum(picked * router[:, None, :], axis=-1)
    chosen_sum = jnp.sum(chosen, axis=1, keepdims=True)
    route_gates = chosen / chosen_sum
    counts = jnp.sum(picked * live_rows[:, None, None], axis=(0, 1))
    prob_sums = jnp.sum(router * live_rows[:, None], axis=0)
    live_count = jnp.sum(live_rows)[None]
    counts, prob_sums, live_count = lax.psum((counts, prob_sums, live_count), ("dp", "expert"))
    fraction = counts / (live_count * top_k)
    balance_loss = balance_coef * (experts * jnp.sum(fraction * prob_sums / total_slots))
    flat_pick = picked.reshape(tok_rows * top_k, experts)
    slot_rank = jnp.sum((jnp.cumsum(flat_pick, axis=0) - flat_pick) * flat_pick, axis=-1)
    slot_of_route = routes.reshape(tok_rows * top_k) * capacity + slot_rank.astype(jnp.int32)
    route_index = jnp.arange(tok_rows * top_k, dtype=jnp.int32)
    slot_route = jnp.zeros((n_slots,), jnp.int32).at[slot_of_route].set(route_index)
    slot_live = jnp.zeros((n_slots,), jnp.bool_).at[slot_of_route].set(True)
    slot_token = slot_route // top_k
    send_rows = jnp.where(slot_live[:, None], mlp_in[slot_token], zero_low).reshape(
        groups, local_experts * capacity, model_width
    )
    recv_rows = lax.all_to_all(send_rows, "expert", split_axis=0, concat_axis=0, tiled=True)
    expert_in = recv_rows.reshape(groups, local_experts, capacity, model_width)
    gate_in = jnp.einsum("sjcd,jdf->sjcf", expert_in, w_gate, preferred_element_type=jnp.float32)
    up_in = jnp.einsum("sjcd,jdf->sjcf", expert_in, w_up, preferred_element_type=jnp.float32)
    sigmoid_gate = jax.nn.sigmoid(gate_in)
    activated = gate_in * sigmoid_gate
    act_low = (activated * up_in).astype(jnp.bfloat16)
    expert_out = (
        jnp.einsum("sjcf,jfd->sjcd", act_low, w_down, preferred_element_type=jnp.float32)
        .astype(jnp.bfloat16)
        .reshape(groups, local_experts * capacity, model_width)
    )
    returned = lax.all_to_all(
        expert_out, "expert", split_axis=0, concat_axis=0, tiled=True
    ).reshape(n_slots, model_width)
    route_out = returned[slot_of_route].reshape(tok_rows, top_k, model_width)
    expert_sum = jnp.einsum(
        "tk,tkd->td", route_gates, route_out, preferred_element_type=jnp.float32
    )
    out_seq = (live_rows[:, None] * (hidden + expert_sum)).astype(jnp.bfloat16)
    out_back = lax.all_to_all(
        out_seq.reshape(replicas, block_rows, model_width),
        "dp",
        split_axis=0,
        concat_axis=0,
        tiled=True,
    )
    output = out_back[order_row].reshape(tok_rows, model_width)
    grad_output = seq_cot.astype(jnp.float32) * live_rows[:, None]
    grad_gates = jnp.einsum(
        "td,tkd->tk", grad_output, route_out, preferred_element_type=jnp.float32
    )
    grad_route = (
        (route_gates[:, :, None] * grad_output[:, None, :])
        .astype(jnp.bfloat16)
        .reshape(tok_rows * top_k, model_width)
    )
    grad_send = jnp.where(slot_live[:, None], grad_route[slot_route], zero_low).reshape(
        groups, local_experts * capacity, model_width
    )
    grad_recv = lax.all_to_all(
        grad_send, "expert", split_axis=0, concat_axis=0, tiled=True
    ).reshape(groups, local_experts, capacity, model_width)
    grad_act = jnp.einsum("sjcd,jfd->sjcf", grad_recv, w_down, preferred_element_type=jnp.float32)
    grad_down_w = jnp.einsum(
        "sjcf,sjcd->jfd", act_low, grad_recv, preferred_element_type=jnp.float32
    )
    grad_up_in = (grad_act * activated).astype(jnp.bfloat16)
    grad_gate_in = (
        grad_act * up_in * sigmoid_gate * (1.0 + gate_in * (1.0 - sigmoid_gate))
    ).astype(jnp.bfloat16)
    grad_gate_w = jnp.einsum(
        "sjcd,sjcf->jdf", expert_in, grad_gate_in, preferred_element_type=jnp.float32
    )
    grad_up_w = jnp.einsum(
        "sjcd,sjcf->jdf", expert_in, grad_up_in, preferred_element_type=jnp.float32
    )
    grad_rows = (
        (
            jnp.einsum("sjcf,jdf->sjcd", grad_gate_in, w_gate, preferred_element_type=jnp.float32)
            + jnp.einsum("sjcf,jdf->sjcd", grad_up_in, w_up, preferred_element_type=jnp.float32)
        )
        .astype(jnp.bfloat16)
        .reshape(groups, local_experts * capacity, model_width)
    )
    grad_back = lax.all_to_all(
        grad_rows, "expert", split_axis=0, concat_axis=0, tiled=True
    ).reshape(n_slots, model_width)
    grad_mlp_in = jnp.sum(
        grad_back[slot_of_route].reshape(tok_rows, top_k, model_width), axis=1, dtype=jnp.float32
    )
    grad_chosen = (
        grad_gates / chosen_sum
        - jnp.sum(grad_gates * route_gates, axis=1, keepdims=True) / chosen_sum
    )
    grad_prob = (
        jnp.einsum("tk,tke->te", grad_chosen, picked)
        + live_rows[:, None] * (balance_coef * experts / total_slots) * fraction[None, :]
    )
    grad_logits = (
        router * (grad_prob - jnp.sum(router * grad_prob, axis=-1, keepdims=True))
    ).astype(jnp.bfloat16)
    grad_router_w = jnp.einsum("td,te->de", mlp_in, grad_logits, preferred_element_type=jnp.float32)
    grad_mlp_in = grad_mlp_in + jnp.einsum(
        "te,de->td", grad_logits, router_full, preferred_element_type=jnp.float32
    )
    grad_hidden_norm, grad_mlp_g = norm_back(hidden, inv_second, mlp_g, grad_mlp_in, 0)
    grad_hidden = grad_output + grad_hidden_norm
    grad_hidden_low = grad_hidden.astype(jnp.bfloat16)
    grad_out_w = jnp.einsum(
        "tm,td->md", mixed_heads, grad_hidden_low, preferred_element_type=jnp.float32
    )
    grad_mixed = (
        jnp.einsum("td,md->tm", grad_hidden_low, wo_full, preferred_element_type=jnp.float32)
        .astype(jnp.bfloat16)
        .reshape(tok_rows, head_count, head_dim)
    )
    again_probs = jnp.exp(masked_scores(q_rot, k_rot, key_live, score_scale) - log_total)
    grad_probs = jnp.einsum("thd,uhd->htu", grad_mixed, v_heads, preferred_element_type=jnp.float32)
    grad_scores = (
        again_probs * (grad_probs - jnp.sum(again_probs * grad_probs, axis=-1, keepdims=True))
    ).astype(jnp.bfloat16)
    grad_q_rot = (
        jnp.einsum("htu,uhd->thd", grad_scores, k_rot, preferred_element_type=jnp.float32)
        * score_scale
    )
    grad_k_rot = (
        jnp.einsum("htu,thd->uhd", grad_scores, q_rot, preferred_element_type=jnp.float32)
        * score_scale
    )
    grad_values = (
        jnp.einsum(
            "htu,thd->uhd",
            again_probs.astype(jnp.bfloat16),
            grad_mixed,
            preferred_element_type=jnp.float32,
        )
        .astype(jnp.bfloat16)
        .reshape(tok_rows, all_heads)
    )
    grad_q_lin, grad_query_g = norm_back(
        q_lin, q_inverse, query_g, rotary_back(grad_q_rot, cosine, sine_table), (0, 1)
    )
    grad_k_lin, grad_key_g = norm_back(
        k_lin, k_inverse, key_g, rotary_back(grad_k_rot, cosine, sine_table), (0, 1)
    )
    grad_q_low = grad_q_lin.astype(jnp.bfloat16).reshape(tok_rows, all_heads)
    grad_k_low = grad_k_lin.astype(jnp.bfloat16).reshape(tok_rows, all_heads)
    grad_query_w = jnp.einsum("td,tm->dm", attn_in, grad_q_low, preferred_element_type=jnp.float32)
    grad_key_w = jnp.einsum("td,tm->dm", attn_in, grad_k_low, preferred_element_type=jnp.float32)
    grad_value_w = jnp.einsum("td,tm->dm", attn_in, grad_values, preferred_element_type=jnp.float32)
    grad_attn_in = (
        jnp.einsum("tm,dm->td", grad_q_low, wq_full, preferred_element_type=jnp.float32)
        + jnp.einsum("tm,dm->td", grad_k_low, wk_full, preferred_element_type=jnp.float32)
        + jnp.einsum("tm,dm->td", grad_values, wv_full, preferred_element_type=jnp.float32)
    )
    grad_input_norm, grad_attn_g = norm_back(inputs, inv_first, attn_g, grad_attn_in, 0)
    grad_seq = grad_hidden + grad_input_norm
    grad_home = lax.all_to_all(
        grad_seq.reshape(replicas, block_rows, model_width).astype(jnp.bfloat16),
        "dp",
        split_axis=0,
        concat_axis=0,
        tiled=True,
    ).astype(jnp.float32)
    grad_input = grad_home[order_row].reshape(tok_rows, model_width)
    part_q, part_k, part_v, part_o, part_r, part_ga, part_gm, part_gq, part_gk = (
        lax.psum_scatter(
            grad_query_w.astype(jnp.bfloat16), "expert", scatter_dimension=0, tiled=True
        ).astype(jnp.float32),
        lax.psum_scatter(
            grad_key_w.astype(jnp.bfloat16), "expert", scatter_dimension=0, tiled=True
        ).astype(jnp.float32),
        lax.psum_scatter(
            grad_value_w.astype(jnp.bfloat16), "expert", scatter_dimension=0, tiled=True
        ).astype(jnp.float32),
        lax.psum_scatter(
            grad_out_w.astype(jnp.bfloat16), "expert", scatter_dimension=0, tiled=True
        ).astype(jnp.float32),
        lax.psum_scatter(
            grad_router_w.astype(jnp.bfloat16), "expert", scatter_dimension=0, tiled=True
        ).astype(jnp.float32),
        lax.psum_scatter(
            grad_attn_g.astype(jnp.bfloat16), "expert", scatter_dimension=0, tiled=True
        ).astype(jnp.float32),
        lax.psum_scatter(
            grad_mlp_g.astype(jnp.bfloat16), "expert", scatter_dimension=0, tiled=True
        ).astype(jnp.float32),
        lax.psum_scatter(
            grad_query_g.astype(jnp.bfloat16), "expert", scatter_dimension=0, tiled=True
        ).astype(jnp.float32),
        lax.psum_scatter(
            grad_key_g.astype(jnp.bfloat16), "expert", scatter_dimension=0, tiled=True
        ).astype(jnp.float32),
    )
    sum_q, sum_k, sum_v, sum_o, sum_r, sum_ga, sum_gm, sum_gq, sum_gk = (
        lax.psum(part_q.astype(jnp.bfloat16), "dp").astype(jnp.float32),
        lax.psum(part_k.astype(jnp.bfloat16), "dp").astype(jnp.float32),
        lax.psum(part_v.astype(jnp.bfloat16), "dp").astype(jnp.float32),
        lax.psum(part_o.astype(jnp.bfloat16), "dp").astype(jnp.float32),
        lax.psum(part_r.astype(jnp.bfloat16), "dp").astype(jnp.float32),
        lax.psum(part_ga.astype(jnp.bfloat16), "dp").astype(jnp.float32),
        lax.psum(part_gm.astype(jnp.bfloat16), "dp").astype(jnp.float32),
        lax.psum(part_gq.astype(jnp.bfloat16), "dp").astype(jnp.float32),
        lax.psum(part_gk.astype(jnp.bfloat16), "dp").astype(jnp.float32),
    )
    total_gate, total_up, total_down = (
        lax.psum_scatter(
            grad_gate_w.astype(jnp.bfloat16), "dp", scatter_dimension=1, tiled=True
        ).astype(jnp.float32),
        lax.psum_scatter(
            grad_up_w.astype(jnp.bfloat16), "dp", scatter_dimension=1, tiled=True
        ).astype(jnp.float32),
        lax.psum_scatter(
            grad_down_w.astype(jnp.bfloat16), "dp", scatter_dimension=1, tiled=True
        ).astype(jnp.float32),
    )
    return (
        output,
        balance_loss,
        grad_input,
        sum_q,
        sum_k,
        sum_v,
        sum_o,
        sum_r,
        sum_ga,
        sum_gm,
        sum_gq,
        sum_gk,
        total_gate,
        total_up,
        total_down,
    )


def solution(mesh):
    return jax.shard_map(
        body,
        mesh=mesh,
        in_specs=(
            P(("dp", "expert"), None),
            P(("dp", "expert"), None),
            P(("dp", "expert")),
            P(),
            P(("dp", "expert"), None),
            P(),
            P("expert", None),
            P("expert", None),
            P("expert", None),
            P("expert", None),
            P("expert", None),
            P("expert"),
            P("expert"),
            P("expert"),
            P("expert"),
            P("expert", None, None),
            P("expert", None, None),
            P("expert", None, None),
        ),
        out_specs=(
            P(("dp", "expert"), None),
            P(),
            P(("dp", "expert"), None),
            P("expert", None),
            P("expert", None),
            P("expert", None),
            P("expert", None),
            P("expert", None),
            P("expert"),
            P("expert"),
            P("expert"),
            P("expert"),
            P("expert", "dp", None),
            P("expert", "dp", None),
            P("expert", "dp", None),
        ),
        check_vma=False,
    )
```

profile of v0, /device:TPU:0, one launch (start us, length us, event | category | flops | bytes accessed | tf_op | source)
XLA Modules:
  0.0 1978.7 jit_solution(11527842721548710693)
XLA Ops:
  12.0 6.3 all-to-all-start
  21.1 14.0 all-reduce.8
  35.2 7.8 all-gather.1
  43.1 9.0 all-gather
  52.3 4.5 reduce-window.6
  57.5 9.1 scatter_custom_fusion
  66.7 8.1 scatter_custom_fusion.1
  78.7 12.7 copy.98
  91.3 32.3 %all-gather.9.cloned.1.call-done = bf16[2048,2048]{1,0:T(8,128)(2,1)} async-done(((bf16[256,2048]{1,0:T(8,128)(2,1)}), bf16[2048,2048]{1,0:T(8,128)(2,1)}) %all-gather.9.cloned.1.call-update) | async-done | bytes 8388624 | tf_op jit(solution)/shard_map/all_gather | solution.py:108
  123.6 12.6 copy.97
  136.3 6.0 multiply_reduce_fusion.8
  151.7 28.2 %all-gather.7.cloned.1.call-done = bf16[2048,2048]{1,0:T(8,128)(2,1)} async-done(((bf16[256,2048]{1,0:T(8,128)(2,1)}), bf16[2048,2048]{1,0:T(8,128)(2,1)}) %all-gather.7.cloned.1.call-update) | async-done | bytes 8388624 | tf_op jit(solution)/shard_map/all_gather | solution.py:110
  180.0 5.9 fusion.63
  188.1 48.0 %all-gather.13.cloned.1.call-done = bf16[2048,2048]{1,0:T(8,128)(2,1)} async-done(((bf16[256,2048]{1,0:T(8,128)(2,1)}), bf16[2048,2048]{1,0:T(8,128)(2,1)}) %all-gather.13.cloned.1.call-update) | async-done | bytes 8388624 | tf_op jit(solution)/shard_map/all_gather | solution.py:111
  236.1 17.0 multiply_reduce_fusion.7
  254.7 9.9 gather_fusion.1
  264.6 8.1 broadcast_select_fusion.1
  272.6 5.2 all-to-all-start.1
  279.4 103.7 %all-to-all-done.1 = bf16[8,288,2048]{2,1,0:T(8,128)(2,1)} async-done(((bf16[8,288,2048]{2,1,0:T(8,128)(2,1)}), bf16[8,288,2048]{2,1,0:T(8,128)(2,1)}, u32[]{:S(2)}, u32[]{:S(2)}) %all-to-all-start.1) | async-done | bytes 9437216 | tf_op jit(solution)/shard_map/all_to_all | solution.py:190
  383.1 4.6 all-to-all-start.4
  387.7 17.1 fusion.17
  404.9 19.0 fusion.6
  426.0 15.4 convert_bitcast_fusion
  441.4 9.2 copy.108
  450.7 5.2 all-to-all-start.2
  456.0 108.4 %all_gather.35 = bf16[2048,16]{0,1:T(8,128)(2,1)S(1)} all-gather(bf16[256,16]{0,1:T(8,128)(2,1)S(1)} %copy-done.77), channel_id=1, replica_groups=mesh['dp'=4,'expert'=8] {'expert'}, dimensions={0}, use_global_device_ids=true | all-gather | bytes 73728 | tf_op jit(solution)/shard_map/all_gather | solution.py:112
  567.7 21.4 %gather_fusion.2 = bf16[2048,2048]{1,0:T(8,128)(2,1)} fusion(bf16[2304,2048]{1,0:T(8,128)(2,1)} %bitcast.33, s32[2048]{0:T(1024)S(1)} %broadcast_clamp_fusion), kind=kCustom, calls=%fused_computation.2 | custom fusion | bytes 16785408 | tf_op jit(solution)/shard_map/gather | solution.py:205
  589.1 8.7 fusion.23
  598.1 4.2 fusion
  602.3 22.8 %gather_fusion.5 = bf16[2304,2048]{1,0:T(8,128)(2,1)} fusion(bf16[2048,2048]{1,0:T(8,128)(2,1)} %fusion, s32[3072]{0:T(1024)S(1)} %pad_clamp_fusion), kind=kCustom, calls=%fused_computation.5 | custom fusion | bytes 18883584 | tf_op jit(solution)/shard_map/gather | solution.py:227
  625.1 8.0 broadcast_select_fusion
  633.1 111.5 %all_to_all.40 = bf16[8,288,2048]{2,1,0:T(8,128)(2,1)} all-to-all(bf16[8,288,2048]{2,1,0:T(8,128)(2,1)} %broadcast_select_fusion), channel_id=1, replica_groups=mesh['dp'=4,'expert'=8] {'expert'}, dimensions={0} | all-to-all | bytes 18874368 | tf_op jit(solution)/shard_map/all_to_all | solution.py:230
  744.6 21.1 %fusion.4 = (bf16[8,2,144,1024]{3,2,0,1:T(8,128)(2,1)}, bf16[8,2,144,1024]{3,2,0,1:T(8,128)(2,1)}) fusion(f32[2,8,144,1024]{3,2,1,0:T(8,128)} %get-tuple-element.88, f32[2,8,144,1024]{3,2,1,0:T(8,128)} %fusion.17, bf16[2,1024,2048]{2,1,0:T(8,128)(2,1)} %param.35, bf16[8,2,144,2048]{3,2,1,0:T(8,128)(2,1)} %bitcast.285), kind=kOutput, calls=%fused_computation.22 | convolution fusion | flops 9694347264 | bytes 46137344 | tf_op jit(solution)/shard_map/sjcd,jfd->sjcf/dot_general | solution.py:233
  765.7 17.5 fusion.11
  783.2 18.8 fusion.1
  802.0 9.2 copy.111
  811.2 5.2 all-to-all-start.6
  818.0 137.4 %all-reduce.6 = (f32[16]{0:T(128)S(1)}, f32[1]{0:T(128)}) all-reduce(f32[16]{0:T(128)S(1)} %get-tuple-element.28, f32[1]{0:T(128)} %bitcast.39), channel_id=1, replica_groups=mesh['dp'=4,'expert'=8] {'dp','expert'}, use_global_device_ids=true, to_apply=%region_17.18 | all-reduce | flops 17 | bytes 136 | tf_op jit(solution)/shard_map/psum | solution.py:177
  956.9 7.0 fusion.25
  963.9 21.7 %gather_fusion.6 = bf16[2048,2048]{1,0:T(8,128)(2,1)} fusion(bf16[2304,2048]{1,0:T(8,128)(2,1)} %bitcast.53, s32[2048]{0:T(1024)S(1)} %copy-done.62), kind=kCustom, calls=%fused_computation.6 | custom fusion | bytes 16785408 | tf_op jit(solution)/shard_map/gather | solution.py:259
  985.6 11.4 convert_reduce_fusion
  1004.6 5.6 convolution_convert_fusion
  1011.7 6.9 convolution_convert_fusion.4
  1025.4 5.7 convolution_convert_fusion.1
  1048.0 5.7 convolution_convert_fusion.2
  1056.9 5.8 convolution_convert_fusion.3
  1065.3 18.2 bitcast_convert_fusion
  1083.6 17.0 bitcast_convert_fusion.2
  1100.9 17.3 bitcast_convert_fusion.1
  1119.5 6.0 fusion.96
  1125.6 7.2 convolution_add_fusion.2
  1132.8 22.9 %reduce-scatter.13.cloned.1.call-done = bf16[256,2048]{1,0:T(8,128)(2,1)} async-done(((bf16[2048,2048]{1,0:T(8,128)(2,1)}), bf16[256,2048]{1,0:T(8,128)(2,1)}) %reduce-scatter.13.cloned.1.call-update) | async-done | bytes 1048592 | tf_op jit(solution)/shard_map/reduce_scatter | solution.py:343
  1155.8 74.7 %reduce-scatter.11.cloned.1.call-done = bf16[256,2048]{1,0:T(8,128)(2,1)} async-done(((bf16[2048,2048]{1,0:T(8,128)(2,1)}), bf16[256,2048]{1,0:T(8,128)(2,1)}) %reduce-scatter.11.cloned.1.call-update) | async-done | bytes 1048592 | tf_op jit(solution)/shard_map/reduce_scatter | solution.py:340
  1230.5 75.1 %reduce-scatter.9.cloned.1.call-done = bf16[256,2048]{1,0:T(8,128)(2,1)} async-done(((bf16[2048,2048]{1,0:T(8,128)(2,1)}), bf16[256,2048]{1,0:T(8,128)(2,1)}) %reduce-scatter.9.cloned.1.call-update) | async-done | bytes 1048592 | tf_op jit(solution)/shard_map/reduce_scatter | solution.py:337
  1305.7 7.0 fusion.61
  1313.5 30.1 %all_to_all.41 = bf16[4,64,2048]{2,1,0:T(8,128)(2,1)S(1)} all-to-all(bf16[4,64,2048]{2,1,0:T(8,128)(2,1)S(1)} %bitcast.294), channel_id=1, replica_groups=mesh['dp'=4,'expert'=8] {'dp'}, dimensions={0} | all-to-all | bytes 2097152 | tf_op jit(solution)/shard_map/all_to_all | solution.py:328
  1343.7 4.3 all-to-all-start.3
  1349.3 72.6 %psum.86 = f32[16]{0:T(128)S(1)} all-reduce(f32[16]{0:T(128)S(1)} %copy-done.88), channel_id=1, replica_groups=mesh['dp'=4,'expert'=8] {'dp','expert'}, use_global_device_ids=true, to_apply=%region_21.22 | all-reduce | flops 16 | bytes 128 | tf_op jit(solution)/shard_map/psum | solution.py:177
  1423.2 13.7 all-reduce.7
  1437.2 19.2 all-reduce.9
  1464.3 39.7 %reduce-scatter.23.cloned.1.call-done = bf16[2,256,2048]{2,1,0:T(8,128)(2,1)} async-done(((bf16[2,1024,2048]{2,1,0:T(8,128)(2,1)}), bf16[2,256,2048]{2,1,0:T(8,128)(2,1)}) %reduce-scatter.23.cloned.1.call-update) | async-done | bytes 2097168 | tf_op jit(solution)/shard_map/reduce_scatter | solution.py:383
  1508.1 146.6 %reduce-scatter.19.cloned.1.call-done = bf16[2,512,1024]{2,1,0:T(8,128)(2,1)} async-done(((bf16[2,2048,1024]{2,1,0:T(8,128)(2,1)}), bf16[2,512,1024]{2,1,0:T(8,128)(2,1)}) %reduce-scatter.19.cloned.1.call-update) | async-done | bytes 2097168 | tf_op jit(solution)/shard_map/reduce_scatter | solution.py:377
  1658.8 143.5 %reduce-scatter.21.cloned.1.call-done = bf16[2,512,1024]{2,1,0:T(8,128)(2,1)} async-done(((bf16[2,2048,1024]{2,1,0:T(8,128)(2,1)}), bf16[2,512,1024]{2,1,0:T(8,128)(2,1)}) %reduce-scatter.21.cloned.1.call-update) | async-done | bytes 2097168 | tf_op jit(solution)/shard_map/reduce_scatter | solution.py:380
  1806.3 155.5 %all-reduce.13.cloned.1.call-done = (bf16[256,2048]{1,0:T(8,128)(2,1)}, bf16[256,2048]{1,0:T(8,128)(2,1)}, bf16[256,2048]{1,0:T(8,128)(2,1)}, bf16[256,2048]{1,0:T(8,128)(2,1)}) async-done(((bf16[256,2048]{1,0:T(8,128)(2,1)}, bf16[256,2048]{1,0:T(8,128)(2,1)}, bf16[256,2048]{1,0:T(8,128)(2,1)}, bf16[256,2048]{1,0:T(8,128)(2,1)}), (bf16[256,2048]{1,0:T(8,128)(2,1)}, bf16[256,2048]{1,0:T(8,128)(2,1)}, ...) | async-done | bytes 4194320 | tf_op jit(solution)/shard_map/psum | solution.py:366
  (351 shorter events, 103.5 us)
Async XLA Ops:
  7.2 12.1 copy-start.86
  7.2 11.1 copy-start.56
  7.2 13.3 copy-start.93
  7.2 13.6 copy-start.94
  7.3 27.9 %copy-start.95 = (bf16[256]{0:T(256)(128)(2,1)S(1)}, bf16[256]{0:T(256)(128)(2,1)}, u32[]{:S(2)}) copy-start(bf16[256]{0:T(256)(128)(2,1)} %param.29) | copy-start | bytes 1540
  7.3 27.9 %copy-start.96 = (bf16[256]{0:T(256)(128)(2,1)S(1)}, bf16[256]{0:T(256)(128)(2,1)}, u32[]{:S(2)}) copy-start(bf16[256]{0:T(256)(128)(2,1)} %param.30) | copy-start | bytes 1540
  7.3 71.4 %all-gather.11.cloned.1.call-start = ((), (), s32[]{:S(2)}) async-start(), calls=%async_computation.18 | async-start | bytes 9437184 | tf_op jit(solution)/shard_map/all_gather | solution.py:109
  8.0 115.6 %all-gather.9.cloned.1.call-start = ((), (), s32[]{:S(2)}) async-start(), calls=%async_computation.17 | async-start | bytes 9437184 | tf_op jit(solution)/shard_map/all_gather | solution.py:108
  8.8 171.2 %all-gather.7.cloned.1.call-start = ((), (), s32[]{:S(2)}) async-start(), calls=%async_computation.16 | async-start | bytes 9437184 | tf_op jit(solution)/shard_map/all_gather | solution.py:110
  9.5 226.6 %all-gather.13.cloned.1.call-start = ((), (), s32[]{:S(2)}) async-start(), calls=%async_computation.19 | async-start | bytes 9437184 | tf_op jit(solution)/shard_map/all_gather | solution.py:111
  12.0 65.1 %all-to-all-start = ((bf16[4,64,2048]{2,1,0:T(8,128)(2,1)}), bf16[4,64,2048]{2,1,0:T(8,128)(2,1)S(1)}, u32[]{:S(2)}, u32[]{:S(2)}) async-start(bf16[4,64,2048]{2,1,0:T(8,128)(2,1)} %gather_fusion), calls=%async_computation | async-start | bytes 2097152 | tf_op jit(solution)/shard_map/all_to_all | solution.py:92
  35.1 109.6 %copy-start.80 = (f32[128]{0:T(128)}, f32[128]{0:T(128)S(1)}, u32[]{:S(2)}) copy-start(f32[128]{0:T(128)S(1)} %convert_element_type.300) | copy-start | bytes 1540
  35.2 109.6 %copy-start.82 = (f32[128]{0:T(128)}, f32[128]{0:T(128)S(1)}, u32[]{:S(2)}) copy-start(f32[128]{0:T(128)S(1)} %convert_element_type.304) | copy-start | bytes 1540
  43.1 210.1 %copy-start.59 = (f32[8,1,256]{2,1,0:T(1,128)}, f32[8,1,256]{2,1,0:T(1,128)S(1)}, u32[]{:S(2)}) copy-start(f32[8,1,256]{2,1,0:T(1,128)S(1)} %convert_element_type.367) | copy-start | bytes 24580
  52.0 39.3 %copy-start.54 = (f32[8,1,256]{2,1,0:T(1,128)}, f32[8,1,256]{2,1,0:T(1,128)S(1)}, u32[]{:S(2)}) copy-start(f32[8,1,256]{2,1,0:T(1,128)S(1)} %convert_element_type.366) | copy-start | bytes 24580
  57.5 17.3 copy-start.64
  74.8 111.0 %copy-start.78 = (pred[256]{0:T(512)(128)(4,1)}, pred[256]{0:T(512)(128)(4,1)S(1)}, u32[]{:S(2)}) copy-start(pred[256]{0:T(512)(128)(4,1)S(1)} %fusion.88) | copy-start | bytes 772
  77.1 159.0 %copy-start.7 = (bf16[4,64,2048]{2,1,0:T(8,128)(2,1)}, bf16[4,64,2048]{2,1,0:T(8,128)(2,1)S(1)}, u32[]{:S(2)}) copy-start(bf16[4,64,2048]{2,1,0:T(8,128)(2,1)S(1)} %all-to-all-done) | copy-start | bytes 3145732
  78.6 63.6 %copy-start.11 = (bf16[4,64,2048]{2,1,0:T(8,128)(2,1)}, bf16[4,64,2048]{2,1,0:T(8,128)(2,1)S(1)}, u32[]{:S(2)}) copy-start(bf16[4,64,2048]{2,1,0:T(8,128)(2,1)S(1)} %fusion.58) | copy-start | bytes 3145732
  151.7 34.1 %copy-start.52 = (f32[16,256]{1,0:T(8,128)}, f32[16,256]{1,0:T(8,128)S(1)}, u32[]{:S(2)}) copy-start(f32[16,256]{1,0:T(8,128)S(1)} %log_add_fusion) | copy-start | bytes 49156
  188.1 65.1 %copy-start.29 = (bf16[16,128,256]{2,1,0:T(8,128)(2,1)}, bf16[16,128,256]{2,1,0:T(8,128)(2,1)S(1)}, u32[]{:S(2)}) copy-start(bf16[16,128,256]{2,1,0:T(8,128)(2,1)S(1)} %convolution_convert_fusion.8) | copy-start | bytes 3145732
  254.7 311.9 %copy-start.2 = (bf16[256,2048]{1,0:T(8,128)(2,1)}, bf16[256,2048]{1,0:T(8,128)(2,1)S(1)}, u32[]{:S(2)}) copy-start(bf16[256,2048]{1,0:T(8,128)(2,1)S(1)} %multiply_convert_fusion.3) | copy-start | bytes 3145732
  272.6 110.5 %all-to-all-start.1 = ((bf16[8,288,2048]{2,1,0:T(8,128)(2,1)}), bf16[8,288,2048]{2,1,0:T(8,128)(2,1)}, u32[]{:S(2)}, u32[]{:S(2)}) async-start(bf16[8,288,2048]{2,1,0:T(8,128)(2,1)} %broadcast_select_fusion.1), calls=%async_computation.1 | async-start | bytes 18874368 | tf_op jit(solution)/shard_map/all_to_all | solution.py:190
  383.1 67.5 %all-to-all-start.4 = ((bf16[4,64,2048]{2,1,0:T(8,128)(2,1)}), bf16[4,64,2048]{2,1,0:T(8,128)(2,1)S(1)}, u32[]{:S(2)}, u32[]{:S(2)}) async-start(bf16[4,64,2048]{2,1,0:T(8,128)(2,1)} %gather_fusion.4), calls=%async_computation.4 | async-start | bytes 2097152 | tf_op jit(solution)/shard_map/all_to_all | solution.py:93
  450.7 113.8 %copy-start.24 = (bf16[4,64,2048]{2,1,0:T(8,128)(2,1)}, bf16[4,64,2048]{2,1,0:T(8,128)(2,1)S(1)}, u32[]{:S(2)}) copy-start(bf16[4,64,2048]{2,1,0:T(8,128)(2,1)S(1)} %all-to-all-done.4) | copy-start | bytes 3145732
  450.7 113.7 %copy-start.63 = (s32[2304]{0:T(1024)S(1)}, s32[2304]{0:T(1024)}, u32[]{:S(2)}) copy-start(s32[2304]{0:T(1024)} %get-tuple-element.73) | copy-start | bytes 27652
  450.7 113.8 %copy-start.65 = (s32[2048,1]{0,1:T(1,128)S(1)}, s32[2048,1]{0,1:T(1,128)}, u32[]{:S(2)}) copy-start(s32[2048,1]{0,1:T(1,128)} %copy-done.64) | copy-start | bytes 24580
  450.7 117.0 %all-to-all-start.2 = ((bf16[8,288,2048]{2,1,0:T(8,128)(2,1)}), bf16[8,288,2048]{2,1,0:T(8,128)(2,1)}, u32[]{:S(2)}, u32[]{:S(2)}) async-start(bf16[8,288,2048]{2,1,0:T(8,128)(2,1)} %bitcast.277), calls=%async_computation.2 | async-start | bytes 18874368 | tf_op jit(solution)/shard_map/all_to_all | solution.py:202
  456.0 111.6 %copy-start.57 = (s32[256,8]{0,1:T(8,128)S(1)}, s32[256,8]{0,1:T(8,128)}, u32[]{:S(2)}) copy-start(s32[256,8]{0,1:T(8,128)} %param.22) | copy-start | bytes 24580
  565.0 24.1 %copy-start.61 = (s32[2048]{0:T(1024)}, s32[2048]{0:T(1024)S(1)}, u32[]{:S(2)}) copy-start(s32[2048]{0:T(1024)S(1)} %broadcast_clamp_fusion) | copy-start | bytes 24580
  567.0 22.1 %copy-start.66 = (f32[256]{0:T(256)}, f32[256]{0:T(256)S(1)}, u32[]{:S(2)}) copy-start(f32[256]{0:T(256)S(1)} %get-tuple-element.89) | copy-start | bytes 3076
  567.6 21.5 %copy-start.69 = (f32[256]{0:T(256)}, f32[256]{0:T(256)S(1)}, u32[]{:S(2)}) copy-start(f32[256]{0:T(256)S(1)} %fusion.76) | copy-start | bytes 3076
  567.7 21.4 %copy-start.27 = (f32[256,2048]{1,0:T(8,128)S(1)}, f32[256,2048]{1,0:T(8,128)}, u32[]{:S(2)}) copy-start(f32[256,2048]{1,0:T(8,128)} %convert_multiply_fusion) | copy-start | bytes 6291460
  811.2 144.9 %copy-start.47 = (f32[256,16]{0,1:T(8,128)S(1)}, f32[256,16]{0,1:T(8,128)}, u32[]{:S(2)}) copy-start(f32[256,16]{0,1:T(8,128)} %copy-done.46) | copy-start | bytes 49156
  811.2 144.9 %copy-start.67 = (f32[256]{0:T(256)S(1)}, f32[256]{0:T(256)}, u32[]{:S(2)}) copy-start(f32[256]{0:T(256)} %copy-done.66) | copy-start | bytes 3076
  811.2 144.9 %copy-start.70 = (f32[256]{0:T(256)S(1)}, f32[256]{0:T(256)}, u32[]{:S(2)}) copy-start(f32[256]{0:T(256)} %copy-done.69) | copy-start | bytes 3076
  811.2 152.7 %all-to-all-start.6 = ((bf16[8,288,2048]{2,1,0:T(8,128)(2,1)}), bf16[8,288,2048]{2,1,0:T(8,128)(2,1)}, u32[]{:S(2)}, u32[]{:S(2)}) async-start(bf16[8,288,2048]{2,1,0:T(8,128)(2,1)} %bitcast.276), calls=%async_computation.6 | async-start | bytes 18874368 | tf_op jit(solution)/shard_map/all_to_all | solution.py:255
  816.5 316.3 %reduce-scatter.15.cloned.1.call-start = ((), (), s32[]{:S(2)}) async-start(), calls=%async_computation.23 | async-start | bytes 9437184 | tf_op jit(solution)/shard_map/reduce_scatter | solution.py:346
  955.3 8.6 copy-start.91
  985.6 11.5 copy-start.10
  985.6 11.5 copy-start.43
  985.6 11.5 copy-start.60
  985.6 11.4 copy-start.72
  1010.2 10.1 copy-start.53
  1010.2 10.1 copy-start.79
  1010.2 145.6 %reduce-scatter.13.cloned.1.call-start = ((), (), s32[]{:S(2)}) async-start(), calls=%async_computation.22 | async-start | bytes 9437184 | tf_op jit(solution)/shard_map/reduce_scatter | solution.py:343
  1031.2 199.3 %reduce-scatter.11.cloned.1.call-start = ((), (), s32[]{:S(2)}) async-start(), calls=%async_computation.21 | async-start | bytes 9437184 | tf_op jit(solution)/shard_map/reduce_scatter | solution.py:340
  1053.7 251.9 %reduce-scatter.9.cloned.1.call-start = ((), (), s32[]{:S(2)}) async-start(), calls=%async_computation.20 | async-start | bytes 9437184 | tf_op jit(solution)/shard_map/reduce_scatter | solution.py:337
  1062.7 374.5 %reduce-scatter.17.cloned.1.call-start = ((), (), s32[]{:S(2)}) async-start(), calls=%async_computation.24 | async-start | bytes 73728 | tf_op jit(solution)/shard_map/reduce_scatter | solution.py:349
  1064.8 439.2 %reduce-scatter.23.cloned.1.call-start = ((), (), s32[]{:S(2)}) async-start(), calls=%async_computation.27 | async-start | bytes 10485760 | tf_op jit(solution)/shard_map/reduce_scatter | solution.py:383
  1083.6 571.2 %reduce-scatter.19.cloned.1.call-start = ((), (), s32[]{:S(2)}) async-start(), calls=%async_computation.25 | async-start | bytes 10485760 | tf_op jit(solution)/shard_map/reduce_scatter | solution.py:377
  1100.7 701.6 %reduce-scatter.21.cloned.1.call-start = ((), (), s32[]{:S(2)}) async-start(), calls=%async_computation.26 | async-start | bytes 10485760 | tf_op jit(solution)/shard_map/reduce_scatter | solution.py:380
  1118.2 843.6 %all-reduce.13.cloned.1.call-start = ((), (), s32[]{:S(2)}) async-start(), calls=%async_computation.28 | async-start | bytes 8388608 | tf_op jit(solution)/shard_map/psum | solution.py:366
  1132.8 172.9 %copy-start.8 = (bf16[4,64,2048]{2,1,0:T(8,128)(2,1)S(1)}, bf16[4,64,2048]{2,1,0:T(8,128)(2,1)}, u32[]{:S(2)}) copy-start(bf16[4,64,2048]{2,1,0:T(8,128)(2,1)} %copy-done.7) | copy-start | bytes 3145732
  1132.8 172.9 %copy-start.41 = (bf16[16,128,256]{2,1,0:T(8,128)(2,1)S(1)}, bf16[16,128,256]{2,1,0:T(8,128)(2,1)}, u32[]{:S(2)}) copy-start(bf16[16,128,256]{2,1,0:T(8,128)(2,1)} %copy-done.40) | copy-start | bytes 3145732
  1132.8 172.9 %copy-start.55 = (f32[8,1,256]{2,1,0:T(1,128)S(1)}, f32[8,1,256]{2,1,0:T(1,128)}, u32[]{:S(2)}) copy-start(f32[8,1,256]{2,1,0:T(1,128)} %copy-done.54) | copy-start | bytes 24580
  1132.8 172.9 %copy-start.76 = (f32[256]{0:T(256)S(1)}, f32[256]{0:T(256)}, u32[]{:S(2)}) copy-start(f32[256]{0:T(256)} %copy-done.75) | copy-start | bytes 3076
  1312.7 36.5 %copy-start.90 = (s32[4]{0:T(128)S(1)}, s32[4]{0:T(128)}, u32[]{:S(2)}) copy-start(s32[4]{0:T(128)} %copy-done.89) | copy-start | bytes 52
  1312.8 36.5 %copy-start.88 = (f32[16]{0:T(128)S(1)}, f32[16]{0:T(128)}, u32[]{:S(2)}) copy-start(f32[16]{0:T(128)} %get-tuple-element.26) | copy-start | bytes 196
  1312.8 109.1 %copy-start.92 = (f32[16]{0:T(128)S(1)}, f32[16]{0:T(128)}, u32[]{:S(2)}) copy-start(f32[16]{0:T(128)} %copy-done.91) | copy-start | bytes 196
  1312.8 110.4 %copy-start.68 = (bf16[2048]{0:T(1024)(128)(2,1)S(1)}, bf16[2048]{0:T(1024)(128)(2,1)}, u32[]{:S(2)}) copy-start(bf16[2048]{0:T(1024)(128)(2,1)} %get-tuple-element.19) | copy-start | bytes 12292
  1312.8 110.4 %copy-start.84 = (bf16[128]{0:T(256)(128)(2,1)S(1)}, bf16[128]{0:T(256)(128)(2,1)}, u32[]{:S(2)}) copy-start(bf16[128]{0:T(256)(128)(2,1)} %get-tuple-element.15) | copy-start | bytes 772
  1312.8 110.4 %copy-start.85 = (bf16[128]{0:T(256)(128)(2,1)S(1)}, bf16[128]{0:T(256)(128)(2,1)}, u32[]{:S(2)}) copy-start(bf16[128]{0:T(256)(128)(2,1)} %get-tuple-element.65) | copy-start | bytes 772
  1343.7 117.8 %all-to-all-start.3 = ((bf16[4,64,2048]{2,1,0:T(8,128)(2,1)}), bf16[4,64,2048]{2,1,0:T(8,128)(2,1)}, u32[]{:S(2)}, u32[]{:S(2)}) async-start(bf16[4,64,2048]{2,1,0:T(8,128)(2,1)} %bitcast.36), calls=%async_computation.3 | async-start | bytes 2097152 | tf_op jit(solution)/shard_map/all_to_all | solution.py:210
  (53 other events, 171.0 us)
Sparse Core Ops, SparseCore 0:
  10.0 57.2 all-gather.10
  69.2 54.4 all-gather.8
  125.5 54.3 all-gather.6
  181.7 54.3 all-gather.12
  1010.3 70.4 reduce-scatter.14
  1084.5 71.2 reduce-scatter.12
  1159.2 71.2 reduce-scatter.10
  1234.4 71.2 reduce-scatter.8
  1309.2 31.4 reduce-scatter.16
  1343.0 160.9 reduce-scatter.22
  1506.5 148.1 reduce-scatter.18
  1657.0 145.1 reduce-scatter.20
  1805.0 156.7 all-reduce.12
where the time goes:
time: 1980 us
  waiting for transfers between devices  873 us (44%)
  blocking collectives  524 us (26%)
  matrix products  274 us (14%)
  local copies, waits for them, and re-layouts  170 us (9%)
  other arithmetic  83.2 us (4%)
  starting transfers between devices  32.1 us (2%)
  between operations  21.4 us (1%)
    psum x2, blocking collectives, body(): lax.psum((counts, prob_sums, live_count), ('dp', 'expert'))  210 us
    psum x1, waiting for transfers between devices, body(): lax.psum(part_q.astype(jnp.bfloat16), 'dp').astype(jnp.float32)  155 us
    reduce_scatter x1, waiting for transfers between devices, body(): lax.psum_scatter(grad_gate_w.astype(jnp.bfloat16), 'dp', scatter_dimensio...  147 us
    reduce_scatter x1, waiting for transfers between devices, body(): lax.psum_scatter(grad_up_w.astype(jnp.bfloat16), 'dp', scatter_dimension=...  143 us
    all_to_all x1, blocking collectives, body(): lax.all_to_all(grad_send, 'expert', split_axis=0, concat_axis=0, tiled=True)  111 us
    all_gather x1, blocking collectives, body(): lax.all_gather(w_router, 'expert', axis=0, tiled=True)  108 us
    all_to_all x1, waiting for transfers between devices, body(): lax.all_to_all(send_rows, 'expert', split_axis=0, concat_axis=0, tiled=True)  104 us
    reduce_scatter x1, waiting for transfers between devices, body(): lax.psum_scatter(grad_query_w.astype(jnp.bfloat16), 'expert', scatter_dim...  75.1 us
  transfers between devices with their start and end apart: 19, of which 11 were waited for; matrix products, arithmetic and copies ran while one was open for 14% of the time, Pallas kernels for 0%

commit v1 on v0

v1 whole, which is shorter than its diff:
```python
import math

import jax
import jax.numpy as jnp
from jax import lax
from jax.sharding import PartitionSpec as P

norm_eps = 1e-06
rope_base = 50000.0
big_negative = -1e30
bf16 = jnp.bfloat16
f32 = jnp.float32


def norm_fwd(values, scales):
    inverse = lax.rsqrt(jnp.mean(values * values, axis=-1, keepdims=True) + norm_eps)
    return (values * inverse * scales, inverse)


def norm_back(values, inverse, scales, grad_out, sum_axes):
    scaled = grad_out * scales
    grad_in = inverse * (
        scaled - values * inverse * inverse * jnp.mean(scaled * values, axis=-1, keepdims=True)
    )
    grad_scale = jnp.sum(grad_out * values * inverse, axis=sum_axes)
    return (grad_in, grad_scale)


def rotary_tables(tok_rows, head_dim):
    half_dim = head_dim // 2
    positions = jnp.arange(tok_rows, dtype=jnp.int32).astype(f32)
    frequency = rope_base ** (-jnp.arange(half_dim, dtype=jnp.int32).astype(f32) * 2.0 / head_dim)
    angles = positions[:, None] * frequency[None, :]
    cosine = jnp.concatenate([jnp.cos(angles), jnp.cos(angles)], axis=-1)[:, None, :]
    sine_table = jnp.concatenate([jnp.sin(angles), jnp.sin(angles)], axis=-1)[:, None, :]
    return (cosine, sine_table)


def turn_half(values):
    half_dim = values.shape[-1] // 2
    return jnp.concatenate([-values[..., half_dim:], values[..., :half_dim]], axis=-1)


def rotary(values, cosine, sine_table):
    return values * cosine + turn_half(values) * sine_table


def rotary_back(grad_out, cosine, sine_table):
    return grad_out * cosine - turn_half(grad_out * sine_table)


def einf(spec, left, right):
    return jnp.einsum(spec, left, right, preferred_element_type=f32)


def body(
    tokens,
    cotangent,
    lengths,
    deal_order,
    routes,
    balance_coef,
    w_query,
    w_key,
    w_value,
    w_out,
    w_router,
    attn_gain,
    mlp_gain,
    query_gain,
    key_gain,
    w_gate,
    w_up,
    w_down,
):
    groups = lax.axis_size("expert")
    replicas = lax.axis_size("dp")
    me = lax.axis_index("expert")
    tok_rows, width = tokens.shape
    block_rows = tok_rows // replicas
    total_slots = float(tok_rows * replicas * groups)
    shard_rows = w_query.shape[0]
    local_experts = w_gate.shape[0]
    experts = local_experts * groups
    top_k = routes.shape[1]
    capacity = tok_rows * top_k * 9 // (8 * experts)

    order_row = lax.dynamic_index_in_dim(deal_order, me, 0, keepdims=False)
    dp_ids = jnp.arange(replicas, dtype=jnp.int32)
    matched = (order_row[:, None] == dp_ids[None, :]).astype(jnp.int32)
    inverse_order = jnp.sum(matched * dp_ids[:, None], axis=0)

    def deal(values):
        blocks = values.reshape(replicas, block_rows, width)[inverse_order]
        return lax.all_to_all(blocks, "dp", split_axis=0, concat_axis=0, tiled=True).reshape(
            tok_rows, width
        )

    def undeal(values):
        back = lax.all_to_all(
            values.reshape(replicas, block_rows, width), "dp", split_axis=0, concat_axis=0, tiled=True
        )
        return back[order_row].reshape(tok_rows, width)

    seq_tokens = deal(tokens)
    seq_cot = deal(cotangent)

    small = jnp.concatenate(
        [w_router.reshape(-1), attn_gain, mlp_gain, query_gain, key_gain]
    )
    small_all = lax.all_gather(small, "expert", axis=0, tiled=False)
    n_router = shard_rows * experts
    cuts = [0, n_router]
    for gain in (attn_gain, mlp_gain, query_gain, key_gain):
        cuts.append(cuts[-1] + gain.shape[0])
    router_full = small_all[:, :n_router].reshape(width, experts)
    attn_g, mlp_g, query_g, key_g = (
        small_all[:, cuts[i] : cuts[i + 1]].reshape(-1).astype(f32) for i in range(1, 5)
    )
    head_dim = query_g.shape[0]
    local_width = w_query.shape[1] // groups
    local_heads = local_width // head_dim
    score_scale = 1.0 / math.sqrt(head_dim)

    ints = jnp.concatenate([routes.reshape(-1), jnp.broadcast_to(lengths, (top_k,))])
    ints_all = lax.all_gather(ints, "expert", axis=0, tiled=False)
    routes_all = ints_all[:, : tok_rows * top_k].reshape(groups, tok_rows, top_k)
    lengths_all = ints_all[:, tok_rows * top_k]
    positions = jnp.arange(tok_rows, dtype=jnp.int32)
    live_all = (positions[None, :] < lengths_all[:, None]).astype(f32)
    live_rows = (positions < lengths[0]).astype(f32)

    def columns(weight):
        return weight.reshape(shard_rows, groups, local_width).transpose(1, 0, 2)

    w_send = jnp.concatenate([columns(w_query), columns(w_key), columns(w_value)], axis=2)
    w_qkv = lax.all_to_all(w_send, "expert", split_axis=0, concat_axis=0, tiled=True).reshape(
        width, 3 * local_width
    )
    wo_full = lax.all_gather(w_out, "expert", axis=0, tiled=True)

    inputs = seq_tokens.astype(f32)
    normed, inv_first = norm_fwd(inputs, attn_g)
    attn_in = normed.astype(bf16)
    attn_all = lax.all_gather(attn_in, "expert", axis=0, tiled=True)
    grad_output = seq_cot.astype(f32) * live_rows[:, None]
    cot_all = lax.all_gather(grad_output.astype(bf16), "expert", axis=0, tiled=False)

    qkv = jnp.dot(attn_all, w_qkv, preferred_element_type=f32)
    heads_shape = (groups, tok_rows, local_heads, head_dim)
    q_lin = qkv[:, :local_width].reshape(heads_shape)
    k_lin = qkv[:, local_width : 2 * local_width].reshape(heads_shape)
    v_heads = qkv[:, 2 * local_width :].astype(bf16).reshape(heads_shape)
    cosine, sine_table = rotary_tables(tok_rows, head_dim)
    q_normed, q_inverse = norm_fwd(q_lin, query_g)
    k_normed, k_inverse = norm_fwd(k_lin, key_g)
    q_rot = rotary(q_normed, cosine, sine_table).astype(bf16)
    k_rot = rotary(k_normed, cosine, sine_table).astype(bf16)
    scores = einf("sthd,suhd->shtu", q_rot, k_rot) * score_scale
    masked = jnp.where(live_all[:, None, None, :] > 0.5, scores, big_negative)
    row_max = jnp.max(masked, axis=-1, keepdims=True)
    raised = jnp.exp(masked - row_max)
    attn_probs = raised / jnp.sum(raised, axis=-1, keepdims=True)
    probs_low = attn_probs.astype(bf16)
    mixed = (
        einf("shtu,suhd->sthd", probs_low, v_heads).astype(bf16).reshape(groups, tok_rows, local_width)
    )
    mixed_here = lax.all_to_all(mixed, "expert", split_axis=0, concat_axis=0, tiled=True)
    hidden = inputs + einf("xtm,xmd->td", mixed_here, wo_full.reshape(groups, local_width, width))
    mlp_normed, inv_second = norm_fwd(hidden, mlp_g)
    mlp_in = mlp_normed.astype(bf16)
    mlp_all = lax.all_gather(mlp_in, "expert", axis=0, tiled=False)

    logits = einf("std,de->ste", mlp_all, router_full)
    router = jax.nn.softmax(logits, axis=-1)
    expert_ids = jnp.arange(experts, dtype=jnp.int32)
    picked = jnp.sum(
        (routes_all[:, :, :, None] == expert_ids).astype(f32), axis=2
    )
    chosen_sum = jnp.sum(picked * router, axis=-1, keepdims=True)
    gates = picked * router / chosen_sum
    counts = jnp.sum(picked * live_all[:, :, None], axis=(0, 1))
    prob_sums = jnp.sum(router * live_all[:, :, None], axis=(0, 1))
    live_count = jnp.sum(live_all)[None]
    sums = lax.psum(jnp.concatenate([counts, prob_sums, live_count]), "dp")
    counts, prob_sums, live_count = sums[:experts], sums[experts : 2 * experts], sums[2 * experts :]
    fraction = counts / (live_count * top_k)
    balance_loss = balance_coef * (experts * jnp.sum(fraction * prob_sums / total_slots))

    first = me * local_experts
    own_picked = lax.dynamic_slice_in_dim(picked, first, local_experts, 2)
    own_gates = lax.dynamic_slice_in_dim(gates, first, local_experts, 2)
    before = (positions[:, None] > positions[None, :]).astype(bf16)
    rank = einf("tu,suj->jst", before, own_picked.astype(bf16))
    own_picked = own_picked.transpose(2, 0, 1)
    own_gates = own_gates.transpose(2, 0, 1)
    slot_of = jnp.where(own_picked > 0.5, rank.astype(jnp.int32), -1)
    slot_ids = jnp.arange(capacity, dtype=jnp.int32)
    is_slot = slot_of[:, :, None, :] == slot_ids[None, None, :, None]
    one_hot = is_slot.astype(bf16)
    slot_gate = jnp.sum(jnp.where(is_slot, own_gates[:, :, None, :], 0.0), axis=-1)
    n_slots = groups * capacity

    expert_in = einf("jsct,std->jscd", one_hot, mlp_all).astype(bf16).reshape(
        local_experts, n_slots, width
    )
    gate_in = einf("jrd,jdf->jrf", expert_in, w_gate)
    up_in = einf("jrd,jdf->jrf", expert_in, w_up)
    sigmoid_gate = jax.nn.sigmoid(gate_in)
    activated = gate_in * sigmoid_gate
    act_low = (activated * up_in).astype(bf16)
    cot_slots = einf("jsct,std->jscd", one_hot, cot_all).astype(bf16)
    grad_recv = (
        (slot_gate[..., None] * cot_slots.astype(f32)).astype(bf16).reshape(local_experts, n_slots, width)
    )
    grad_down_w = einf("jrf,jrd->jfd", act_low, grad_recv)
    total_down = lax.psum_scatter(
        grad_down_w.astype(bf16), "dp", scatter_dimension=1, tiled=True
    ).astype(f32)

    expert_out = einf("jrf,jfd->jrd", act_low, w_down).astype(bf16).reshape(
        local_experts, groups, capacity, width
    )
    grad_gate_slot = jnp.sum(cot_slots.astype(f32) * expert_out.astype(f32), axis=-1)
    own_grad_gates = jnp.sum(jnp.where(is_slot, grad_gate_slot[..., None], 0.0), axis=2)
    weighted = (slot_gate[..., None] * expert_out.astype(f32)).astype(bf16)
    sum_part = einf("jsct,jscd->std", one_hot, weighted).astype(bf16)

    grad_act = einf("jrd,jfd->jrf", grad_recv, w_down)
    grad_up_in = (grad_act * activated).astype(bf16)
    grad_gate_in = (
        grad_act * up_in * sigmoid_gate * (1.0 + gate_in * (1.0 - sigmoid_gate))
    ).astype(bf16)
    grad_rows = (
        (einf("jrf,jdf->jrd", grad_gate_in, w_gate) + einf("jrf,jdf->jrd", grad_up_in, w_up))
        .astype(bf16)
        .reshape(local_experts, groups, capacity, width)
    )
    grad_part = einf("jsct,jscd->std", one_hot, grad_rows).astype(bf16)
    grad_mlp_in = lax.psum_scatter(grad_part, "expert", scatter_dimension=0, tiled=True).astype(f32)
    grad_mlp_in = grad_mlp_in.reshape(tok_rows, width)

    grad_gate_w = einf("jrd,jrf->jdf", expert_in, grad_gate_in)
    grad_up_w = einf("jrd,jrf->jdf", expert_in, grad_up_in)
    total_gate, total_up = (
        lax.psum_scatter(value.astype(bf16), "dp", scatter_dimension=1, tiled=True).astype(f32)
        for value in (grad_gate_w, grad_up_w)
    )

    gate_back = lax.all_to_all(
        own_grad_gates.transpose(1, 0, 2), "expert", split_axis=0, concat_axis=0, tiled=True
    )
    grad_gates = gate_back.reshape(experts, tok_rows).T
    my_router = lax.dynamic_index_in_dim(router, me, 0, keepdims=False)
    my_picked = lax.dynamic_index_in_dim(picked, me, 0, keepdims=False)
    my_gates = lax.dynamic_index_in_dim(gates, me, 0, keepdims=False)
    my_sum = lax.dynamic_index_in_dim(chosen_sum, me, 0, keepdims=False)
    grad_prob = (
        my_picked * (grad_gates - jnp.sum(grad_gates * my_gates, axis=1, keepdims=True)) / my_sum
        + live_rows[:, None] * (balance_coef * experts / total_slots) * fraction[None, :]
    )
    grad_logits = (
        my_router * (grad_prob - jnp.sum(my_router * grad_prob, axis=-1, keepdims=True))
    ).astype(bf16)
    grad_router_w = einf("td,te->de", mlp_in, grad_logits)
    grad_mlp_in = grad_mlp_in + einf("te,de->td", grad_logits, router_full)

    grad_hidden_norm, grad_mlp_g = norm_back(hidden, inv_second, mlp_g, grad_mlp_in, 0)
    grad_hidden = grad_output + grad_hidden_norm
    grad_hidden_low = grad_hidden.astype(bf16)
    hidden_all = lax.all_gather(grad_hidden_low, "expert", axis=0, tiled=True)

    grad_out_w = einf("rm,rd->md", mixed.reshape(groups * tok_rows, local_width), hidden_all)
    grad_mixed = einf("rd,md->rm", hidden_all, w_out).astype(bf16).reshape(heads_shape)
    grad_probs = einf("sthd,suhd->shtu", grad_mixed, v_heads)
    grad_scores = (
        attn_probs * (grad_probs - jnp.sum(attn_probs * grad_probs, axis=-1, keepdims=True))
    ).astype(bf16)
    grad_q_rot = einf("shtu,suhd->sthd", grad_scores, k_rot) * score_scale
    grad_k_rot = einf("shtu,sthd->suhd", grad_scores, q_rot) * score_scale
    grad_values = einf("shtu,sthd->suhd", probs_low, grad_mixed).astype(bf16)
    grad_q_lin, grad_query_g = norm_back(
        q_lin, q_inverse, query_g, rotary_back(grad_q_rot, cosine, sine_table), (0, 1, 2)
    )
    grad_k_lin, grad_key_g = norm_back(
        k_lin, k_inverse, key_g, rotary_back(grad_k_rot, cosine, sine_table), (0, 1, 2)
    )
    flat = (groups * tok_rows, local_width)
    grad_qkv = jnp.concatenate(
        [
            grad_q_lin.astype(bf16).reshape(flat),
            grad_k_lin.astype(bf16).reshape(flat),
            grad_values.reshape(flat),
        ],
        axis=1,
    )
    grad_attn_part = einf("rm,dm->rd", grad_qkv, w_qkv).astype(bf16)
    grad_attn_in = lax.psum_scatter(
        grad_attn_part, "expert", scatter_dimension=0, tiled=True
    ).astype(f32)
    grad_qkv_w = einf("rd,rm->dm", attn_all, grad_qkv).astype(bf16)
    w_back = lax.all_to_all(
        grad_qkv_w.reshape(groups, shard_rows, 3 * local_width),
        "expert",
        split_axis=0,
        concat_axis=0,
        tiled=True,
    )
    attn_w = jnp.concatenate(
        [
            w_back[:, :, i * local_width : (i + 1) * local_width]
            .transpose(1, 0, 2)
            .reshape(shard_rows, groups * local_width)
            for i in range(3)
        ]
        + [grad_out_w.astype(bf16)],
        axis=0,
    )
    attn_sum = lax.psum(attn_w, "dp").astype(f32)
    sum_q, sum_k, sum_v, sum_o = (
        attn_sum[i * shard_rows : (i + 1) * shard_rows] for i in range(4)
    )

    grad_input_norm, grad_attn_g = norm_back(inputs, inv_first, attn_g, grad_attn_in, 0)
    grad_input = undeal((grad_hidden + grad_input_norm).astype(bf16)).astype(f32)

    expert_sum = lax.psum_scatter(sum_part, "expert", scatter_dimension=0, tiled=True)
    expert_sum = expert_sum.reshape(tok_rows, width).astype(f32)
    output = undeal((live_rows[:, None] * (hidden + expert_sum)).astype(bf16))

    pieces = [grad_router_w.astype(bf16).reshape(groups, n_router)] + [
        value.astype(bf16).reshape(groups, -1)
        for value in (grad_attn_g, grad_mlp_g, grad_query_g, grad_key_g)
    ]
    part_small = lax.psum_scatter(
        jnp.concatenate(pieces, axis=1), "expert", scatter_dimension=0, tiled=True
    )
    sum_small = lax.psum(part_small.reshape(-1), "dp").astype(f32)
    sum_r = sum_small[:n_router].reshape(shard_rows, experts)
    sum_ga, sum_gm, sum_gq, sum_gk = (sum_small[cuts[i] : cuts[i + 1]] for i in range(1, 5))
    return (
        output,
        balance_loss,
        grad_input,
        sum_q,
        sum_k,
        sum_v,
        sum_o,
        sum_r,
        sum_ga,
        sum_gm,
        sum_gq,
        sum_gk,
        total_gate,
        total_up,
        total_down,
    )


def solution(mesh):
    rows = P(("dp", "expert"), None)
    weight = P("expert", None)
    gain = P("expert")
    cube = P("expert", None, None)
    cube_out = P("expert", "dp", None)
    return jax.shard_map(
        body,
        mesh=mesh,
        in_specs=(
            (rows, rows, P(("dp", "expert")), P(), rows, P())
            + (weight,) * 5
            + (gain,) * 4
            + (cube,) * 3
        ),
        out_specs=(
            (rows, P(), rows) + (weight,) * 5 + (gain,) * 4 + (cube_out,) * 3
        ),
        check_vma=False,
    )
```

time: 1980 us -> 1550 us (0.78)
  blocking collectives: 524 us -> 30.4 us
  waiting for transfers between devices: 873 us -> 1010 us
  local copies, waits for them, and re-layouts: 170 us -> 99.1 us
    psum x3 -> x2, blocking collectives: 229 us -> 30.4 us  [the longest x1 18.7 us: body(): sum_small = lax.psum(part_small.reshape(-1), 'dp').astype(f32)]
    all_to_all x2 -> x0, blocking collectives: 142 us -> none  [the longest x1 111 us: body(): lax.all_to_all(grad_send, 'expert', split_axis=0, concat_axis=0, tiled=True)]
    unnamed x13 -> x18, waiting for transfers between devices: 2.73 us -> 140 us
    all_gather x3 -> x0, blocking collectives: 125 us -> none  [the longest x1 108 us: body(): lax.all_gather(w_router, 'expert', axis=0, tiled=True)]
    gather x8 -> x4, local copies, waits for them, and re-layouts: 83.6 us -> 6.74 us  [the longest x2 3.46 us: undeal(): return back[order_row].reshape(tok_rows, width)]
    reduce_scatter x8 -> x6, waiting for transfers between devices: 503 us -> 471 us  [the longest x2 291 us: body(): lax.psum_scatter(value.astype(bf16), 'dp', scatter_dimension=1, tiled=True)]
    unnamed x2 -> x0, blocking collectives: 27.8 us -> none
    dot_general x3 -> x0, local copies, waits for them, and re-layouts: 25.4 us -> none  [the longest x1 12.7 us: body(): jnp.dot(attn_in, wk_full, preferred_element_type=jnp.float32)]
  transfers between devices with their start and end apart: 19 -> 23, of which waited for: 11 -> 17; matrix products, arithmetic and copies ran while one was open for 14% -> 19% of each run, Pallas kernels for 0% -> 0%
where the time goes in v1:
time: 1550 us; the launch traced here: 1540 us
  waiting for transfers between devices  1010 us (65%)
  matrix products  277 us (18%)
  local copies, waits for them, and re-layouts  99.1 us (6%)
  other arithmetic  68.9 us (4%)
  starting transfers between devices  40 us (3%)
  blocking collectives  30.4 us (2%)
  between operations  20.8 us (1%)
    reduce_scatter x2, waiting for transfers between devices, body(): lax.psum_scatter(value.astype(bf16), 'dp', scatter_dimension=1, tiled=True)  291 us
    dot_general x26, matrix products, einf(): return jnp.einsum(spec, left, right, preferred_element_type=f32)  257 us
    psum x1, waiting for transfers between devices, body(): attn_sum = lax.psum(attn_w, 'dp').astype(f32)  153 us
    unnamed x18, waiting for transfers between devices  140 us
    reduce_scatter x1, waiting for transfers between devices, body(): lax.psum_scatter(grad_down_w.astype(bf16), 'dp', scatter_dimension=1, til...  74.7 us
    reduce_scatter x1, waiting for transfers between devices, body(): lax.psum_scatter(sum_part, 'expert', scatter_dimension=0, tiled=True)  71 us
    all_gather x1, waiting for transfers between devices, body(): hidden_all = lax.all_gather(grad_hidden_low, 'expert', axis=0, tiled=True)  54.5 us
    all_gather x1, waiting for transfers between devices, body(): attn_all = lax.all_gather(attn_in, 'expert', axis=0, tiled=True)  49.9 us
  transfers between devices with their start and end apart: 23, of which 17 were waited for; matrix products, arithmetic and copies ran while one was open for 19% of the time, Pallas kernels for 0%

profile of v1, /device:TPU:0, one launch (start us, length us, event | category | flops | bytes accessed | tf_op | source)
XLA Modules:
  0.0 1543.7 jit_solution(17593628085989760064)
XLA Ops:
  10.0 6.3 all-to-all-start
  21.5 50.8 %all-reduce.11.cloned.1.call-done = bf16[37120]{0:T(1024)(128)(2,1)} async-done(((bf16[37120]{0:T(1024)(128)(2,1)}), bf16[37120]{0:T(1024)(128)(2,1)}) %all-reduce.11.cloned.1.call-update) | async-done | bytes 74256
  83.3 4.7 all-to-all-start.1
  89.1 42.5 %all-reduce.13.cloned.1.call-done = s32[16448]{0:T(1024)} async-done(((s32[16448]{0:T(1024)}), s32[16448]{0:T(1024)}) %all-reduce.13.cloned.1.call-update) | async-done | bytes 65808
  135.2 4.6 copy.295
  139.9 49.9 %all-gather.9.cloned.1.call-done = bf16[2048,2048]{1,0:T(8,128)(2,1)} async-done(((bf16[256,2048]{1,0:T(8,128)(2,1)}), bf16[2048,2048]{1,0:T(8,128)(2,1)}) %all-gather.9.cloned.1.call-update) | async-done | bytes 8388624 | tf_op jit(solution)/shard_map/all_gather | solution.py:145
  189.7 10.0 fusion.91
  203.7 4.5 fusion.80
  212.8 3.2 multiply_reduce_fusion.8
  218.3 3.4 reshape.428
  224.4 5.6 multiply_reduce_fusion.9
  236.7 4.3 fusion.85
  241.6 3.1 convolution_convert_fusion.10
  246.1 3.6 all-to-all-start.2
  249.8 15.2 all-to-all-done.2
  265.0 5.8 multiply_reduce_fusion.7
  275.1 4.4 all-to-all-start.4
  279.6 22.8 %all-to-all-done.4 = bf16[4,64,2048]{2,1,0:T(8,128)(2,1)S(1)} async-done(((bf16[4,64,2048]{2,1,0:T(8,128)(2,1)}), bf16[4,64,2048]{2,1,0:T(8,128)(2,1)S(1)}, u32[]{:S(2)}, u32[]{:S(2)}) %all-to-all-start.4) | async-done | bytes 1048608 | tf_op jit(solution)/shard_map/all_to_all | solution.py:95
  305.6 21.3 %all-gather.17.cloned.1.call-done = bf16[2048,2048]{1,0:T(8,128)(2,1)} async-done(((bf16[256,2048]{1,0:T(8,128)(2,1)}), bf16[2048,2048]{1,0:T(8,128)(2,1)}) %all-gather.17.cloned.1.call-update) | async-done | bytes 8388624 | tf_op jit(solution)/shard_map/all_gather | solution.py:172
  326.9 8.4 convert_bitcast_fusion
  335.3 10.1 copy.312
  345.5 5.7 fusion.86
  352.0 17.8 %fusion.92 = f32[2,1152,1024]{2,1,0:T(8,128)} fusion(bf16[2,1152,2048]{2,1,0:T(8,128)(2,1)} %bitcast.265, bf16[2,2048,1024]{2,1,0:T(8,128)(2,1)} %param.33), kind=kOutput, calls=%fused_computation.211 | convolution fusion | flops 9663676416 | bytes 27262976 | tf_op jit(solution)/shard_map/jrd,jdf->jrf/dot_general | solution.py:53
  369.9 17.9 %multiply_convert_fusion.4 = (bf16[2,1152,1024]{2,1,0:T(8,128)(2,1)}, f32[2,1152,1024]{2,1,0:T(8,128)}) fusion(f32[2,1152,1024]{2,1,0:T(8,128)} %fusion.92, bf16[2,1152,2048]{2,1,0:T(8,128)(2,1)S(1)} %bitcast.270, bf16[2,2048,1024]{2,1,0:T(8,128)(2,1)} %param.34), kind=kOutput, calls=%fused_computation.20 | convolution fusion | flops 9677832192 | bytes 41418752 | tf_op jit(solution)/shard_map/jrd,jdf->jrf/dot_general | solution.py:53
  387.8 16.5 %convolution_convert_fusion = bf16[2,1152,2048]{2,1,0:T(8,128)(2,1)} fusion(bf16[2,1152,1024]{2,1,0:T(8,128)(2,1)} %get-tuple-element.177, bf16[2,1024,2048]{2,1,0:T(8,128)(2,1)} %param.35), kind=kOutput, calls=%fused_computation.14 | convolution fusion | flops 9668395008 | bytes 22544384 | tf_op jit(solution)/shard_map/jrf,jfd->jrd/dot_general | solution.py:53
  404.3 10.1 fusion.3
  415.7 8.8 fusion.2
  424.5 9.3 copy.314
  433.8 21.4 %multiply_convert_fusion.2 = (bf16[2,1152,1024]{2,1,0:T(8,128)(2,1)}, bf16[2,1152,1024]{2,1,0:T(8,128)(2,1)}) fusion(f32[2,1152,1024]{2,1,0:T(8,128)} %fusion.92, f32[2,1152,1024]{2,1,0:T(8,128)} %get-tuple-element.178, bf16[2,1152,2048]{2,1,0:T(8,128)(2,1)} %bitcast.271, bf16[2,1024,2048]{2,1,0:T(8,128)(2,1)} %param.35), kind=kOutput, calls=%fused_computation.18 | convolution fusion | flops 9694347264 | bytes 46137344 | tf_op jit(solution)/shard_map/jrd,jfd->jrf/dot_general | solution.py:53
  455.1 17.4 %fusion.93 = f32[2,1152,2048]{2,1,0:T(8,128)} fusion(bf16[2,1152,1024]{2,1,0:T(8,128)(2,1)} %get-tuple-element.127, bf16[2,2048,1024]{2,1,0:T(8,128)(2,1)} %param.33), kind=kOutput, calls=%fused_computation.212 | convolution fusion | flops 9663676416 | bytes 31981568 | tf_op jit(solution)/shard_map/jrf,jdf->jrd/dot_general | solution.py:53
  472.5 18.6 %add_convert_fusion = bf16[2,1152,2048]{2,1,0:T(8,128)(2,1)} fusion(f32[2,1152,2048]{2,1,0:T(8,128)} %fusion.93, bf16[2,1152,1024]{2,1,0:T(8,128)(2,1)} %get-tuple-element.126, bf16[2,2048,1024]{2,1,0:T(8,128)(2,1)} %param.34), kind=kOutput, calls=%fused_computation.10 | convolution fusion | flops 9673113600 | bytes 41418752 | tf_op jit(solution)/shard_map/jrf,jdf->jrd/dot_general | solution.py:53
  491.1 10.9 bitcast_convert_fusion
  502.0 13.0 bitcast_convert_fusion.1
  517.4 11.7 psum.21
  529.7 3.3 all-to-all-start.5
  539.5 34.1 %reduce-scatter.9.cloned.1.call-done = bf16[1,256,2048]{2,1,0:T(8,128)(2,1)} async-done(((bf16[8,256,2048]{2,1,0:T(8,128)(2,1)}), bf16[1,256,2048]{2,1,0:T(8,128)(2,1)}) %reduce-scatter.9.cloned.1.call-update) | async-done | bytes 1048592 | tf_op jit(solution)/shard_map/reduce_scatter | solution.py:240
  573.6 4.2 multiply_reduce_fusion.3
  577.8 71.0 %reduce-scatter.7.cloned.1.call-done = bf16[1,256,2048]{2,1,0:T(8,128)(2,1)} async-done(((bf16[8,256,2048]{2,1,0:T(8,128)(2,1)}), bf16[1,256,2048]{2,1,0:T(8,128)(2,1)}) %reduce-scatter.7.cloned.1.call-update) | async-done | bytes 1048592 | tf_op jit(solution)/shard_map/reduce_scatter | solution.py:327
  648.8 4.8 fusion.77
  653.7 54.5 %all-gather.15.cloned.1.call-done = bf16[2048,2048]{1,0:T(8,128)(2,1)} async-done(((bf16[256,2048]{1,0:T(8,128)(2,1)}), bf16[2048,2048]{1,0:T(8,128)(2,1)}) %all-gather.15.cloned.1.call-update) | async-done | bytes 8388624 | tf_op jit(solution)/shard_map/all_gather | solution.py:271
  708.2 6.0 convolution_convert_fusion.7
  715.4 3.2 fusion.42
  735.3 9.3 convolution_convert_fusion.1
  744.7 17.8 %convolution_convert_fusion.2 = bf16[2,1024,2048]{2,1,0:T(8,128)(2,1)} fusion(bf16[2,1152,1024]{2,1,0:T(8,128)(2,1)} %get-tuple-element.177, bf16[2,1152,2048]{2,1,0:T(8,128)(2,1)} %bitcast.272), kind=kOutput, calls=%fused_computation.29 | convolution fusion | flops 9667870720 | bytes 22544384 | tf_op jit(solution)/shard_map/jrf,jrd->jfd/dot_general | solution.py:53
  762.6 17.3 %convolution_convert_fusion.3 = bf16[2,2048,1024]{2,1,0:T(8,128)(2,1)} fusion(bf16[2,1152,2048]{2,1,0:T(8,128)(2,1)} %bitcast.266, bf16[2,1152,1024]{2,1,0:T(8,128)(2,1)} %get-tuple-element.126), kind=kOutput, calls=%fused_computation.30 | convolution fusion | flops 9667870720 | bytes 22544384 | tf_op jit(solution)/shard_map/jrd,jrf->jdf/dot_general | solution.py:53
  779.9 17.8 %convolution_convert_fusion.4 = bf16[2,2048,1024]{2,1,0:T(8,128)(2,1)} fusion(bf16[2,1152,2048]{2,1,0:T(8,128)(2,1)} %bitcast.267, bf16[2,1152,1024]{2,1,0:T(8,128)(2,1)} %get-tuple-element.127), kind=kOutput, calls=%fused_computation.31 | convolution fusion | flops 9667870720 | bytes 22544384 | tf_op jit(solution)/shard_map/jrd,jrf->jdf/dot_general | solution.py:53
  797.8 11.3 convolution_convert_fusion.5
  809.1 4.6 all-to-all-start.7
  814.9 5.8 convolution_convert_fusion.6
  820.7 30.9 %all-to-all-done.7 = bf16[8,256,768]{2,1,0:T(8,128)(2,1)} async-done(((bf16[8,256,768]{2,1,0:T(8,128)(2,1)}), bf16[8,256,768]{2,1,0:T(8,128)(2,1)}, u32[]{:S(2)}, u32[]{:S(2)}) %all-to-all-start.7) | async-done | bytes 3145760 | tf_op jit(solution)/shard_map/all_to_all | solution.py:302
  856.5 4.8 all-to-all-start.3
  863.2 3.6 fusion.23
  866.8 46.0 %all-to-all-done.3 = bf16[4,64,2048]{2,1,0:T(8,128)(2,1)S(1)} async-done(((bf16[4,64,2048]{2,1,0:T(8,128)(2,1)}), bf16[4,64,2048]{2,1,0:T(8,128)(2,1)S(1)}, u32[]{:S(2)}, u32[]{:S(2)}) %all-to-all-start.3) | async-done | bytes 1048608 | tf_op jit(solution)/shard_map/all_to_all | solution.py:100
  913.8 7.7 all-to-all-start.6
  927.2 74.7 %reduce-scatter.17.cloned.1.call-done = bf16[2,256,2048]{2,1,0:T(8,128)(2,1)} async-done(((bf16[2,1024,2048]{2,1,0:T(8,128)(2,1)}), bf16[2,256,2048]{2,1,0:T(8,128)(2,1)}) %reduce-scatter.17.cloned.1.call-update) | async-done | bytes 2097168 | tf_op jit(solution)/shard_map/reduce_scatter | solution.py:217
  1001.9 4.1 convert_element_type.401
  1006.0 147.6 %reduce-scatter.15.cloned.1.call-done = bf16[2,512,1024]{2,1,0:T(8,128)(2,1)} async-done(((bf16[2,2048,1024]{2,1,0:T(8,128)(2,1)}), bf16[2,512,1024]{2,1,0:T(8,128)(2,1)}) %reduce-scatter.15.cloned.1.call-update) | async-done | bytes 2097168 | tf_op jit(solution)/shard_map/reduce_scatter | solution.py:246
  1153.6 4.1 convert_element_type.399
  1157.7 143.6 %reduce-scatter.13.cloned.1.call-done = bf16[2,512,1024]{2,1,0:T(8,128)(2,1)} async-done(((bf16[2,2048,1024]{2,1,0:T(8,128)(2,1)}), bf16[2,512,1024]{2,1,0:T(8,128)(2,1)}) %reduce-scatter.13.cloned.1.call-update) | async-done | bytes 2097168 | tf_op jit(solution)/shard_map/reduce_scatter | solution.py:246
  1301.3 4.1 convert_element_type.397
  1306.3 153.1 %all-reduce.9.cloned.1.call-done = bf16[1024,2048]{1,0:T(8,128)(2,1)} async-done(((bf16[1024,2048]{1,0:T(8,128)(2,1)}), bf16[1024,2048]{1,0:T(8,128)(2,1)}) %all-reduce.9.cloned.1.call-update) | async-done | bytes 4194320 | tf_op jit(solution)/shard_map/psum | solution.py:319
  1459.4 6.0 fusion.81
  1465.4 45.9 %all-reduce.15.cloned.1.call-done = bf16[8,4640]{1,0:T(8,128)(2,1)} async-done(((bf16[8,4640]{1,0:T(8,128)(2,1)}), bf16[8,4640]{1,0:T(8,128)(2,1)}) %all-reduce.15.cloned.1.call-update) | async-done | bytes 74256
  1512.9 18.7 %psum.23 = bf16[4640]{0:T(1024)(128)(2,1)S(1)} all-reduce(bf16[4640]{0:T(1024)(128)(2,1)S(1)} %dynamic-slice_reduce_fusion), channel_id=1, replica_groups=mesh['dp'=4,'expert'=8] {'dp'}, use_global_device_ids=true, to_apply=%region_35.36 | all-reduce | flops 4640 | bytes 18560 | tf_op jit(solution)/shard_map/psum | solution.py:338
  (341 shorter events, 99.3 us)
Async XLA Ops:
  7.2 10.6 copy-start.78
  7.2 10.6 copy-start.77
  7.2 10.6 copy-start.76
  7.3 10.6 copy-start.75
  7.3 13.1 copy-start.64
  8.2 11.5 copy-start.79
  10.0 63.9 %all-to-all-start = ((bf16[4,64,2048]{2,1,0:T(8,128)(2,1)}), bf16[4,64,2048]{2,1,0:T(8,128)(2,1)S(1)}, u32[]{:S(2)}, u32[]{:S(2)}) async-start(bf16[4,64,2048]{2,1,0:T(8,128)(2,1)} %gather_fusion), calls=%async_computation | async-start | bytes 2097152 | tf_op jit(solution)/shard_map/all_to_all | solution.py:95
  16.3 55.9 %all-reduce.11.cloned.1.call-start = ((), (), s32[]{:S(2)}) async-start(), calls=%async_computation.26 | async-start | bytes 151552
  16.3 59.9 %copy-start.25 = (bf16[256,2048]{1,0:T(8,128)(2,1)S(1)}, bf16[256,2048]{1,0:T(8,128)(2,1)}, u32[]{:S(2)}) copy-start(bf16[256,2048]{1,0:T(8,128)(2,1)} %param.24) | copy-start | bytes 3145732
  19.0 112.6 %all-reduce.13.cloned.1.call-start = ((), (), s32[]{:S(2)}) async-start(), calls=%async_computation.27 | async-start | bytes 139264
  21.5 168.3 %all-gather.9.cloned.1.call-start = ((), (), s32[]{:S(2)}) async-start(), calls=%async_computation.14 | async-start | bytes 9437184 | tf_op jit(solution)/shard_map/all_gather | solution.py:145
  73.9 191.1 %copy-start.5 = (bf16[4,64,2048]{2,1,0:T(8,128)(2,1)}, bf16[4,64,2048]{2,1,0:T(8,128)(2,1)S(1)}, u32[]{:S(2)}) copy-start(bf16[4,64,2048]{2,1,0:T(8,128)(2,1)S(1)} %all-to-all-done) | copy-start | bytes 3145732
  75.6 174.1 %all-gather.11.cloned.1.call-start = ((), (), s32[]{:S(2)}) async-start(), calls=%async_computation.15 | async-start | bytes 9437184 | tf_op jit(solution)/shard_map/all_gather | solution.py:140
  83.3 51.9 %all-to-all-start.1 = ((bf16[8,256,768]{1,2,0:T(8,128)(2,1)}), bf16[8,256,768]{1,2,0:T(8,128)(2,1)}, u32[]{:S(2)}, u32[]{:S(2)}) async-start(bf16[8,256,768]{1,2,0:T(8,128)(2,1)} %pad_maximum_fusion.1), calls=%async_computation.1 | async-start | bytes 6291456 | tf_op jit(solution)/shard_map/all_to_all | solution.py:137
  224.4 10.8 copy-start.2
  244.8 26.1 %copy-start.16 = (bf16[8,2,128,256]{3,2,1,0:T(8,128)(2,1)}, bf16[8,2,128,256]{3,2,1,0:T(8,128)(2,1)S(1)}, u32[]{:S(2)}) copy-start(bf16[8,2,128,256]{3,2,1,0:T(8,128)(2,1)S(1)} %convolution_convert_fusion.10) | copy-start | bytes 3145732
  246.1 18.9 %all-to-all-start.2 = ((bf16[8,256,256]{2,1,0:T(8,128)(2,1)}), bf16[8,256,256]{2,1,0:T(8,128)(2,1)S(1)}, u32[]{:S(2)}, u32[]{:S(2)}) async-start(bf16[8,256,256]{2,1,0:T(8,128)(2,1)} %copy.307), calls=%async_computation.2 | async-start | bytes 2097152 | tf_op jit(solution)/shard_map/all_to_all | solution.py:168
  249.6 77.3 %all-gather.17.cloned.1.call-start = ((), (), s32[]{:S(2)}) async-start(), calls=%async_computation.25 | async-start | bytes 9437184 | tf_op jit(solution)/shard_map/all_gather | solution.py:172
  249.7 21.2 %copy-start.41 = (f32[1,2,8,128]{3,1,2,0:T(2,128)}, f32[1,2,8,128]{3,1,2,0:T(2,128)S(1)}, u32[]{:S(2)}) copy-start(f32[1,2,8,128]{3,1,2,0:T(2,128)S(1)} %copy.363) | copy-start | bytes 24580
  275.1 27.3 %all-to-all-start.4 = ((bf16[4,64,2048]{2,1,0:T(8,128)(2,1)}), bf16[4,64,2048]{2,1,0:T(8,128)(2,1)S(1)}, u32[]{:S(2)}, u32[]{:S(2)}) async-start(bf16[4,64,2048]{2,1,0:T(8,128)(2,1)} %gather_fusion.2), calls=%async_computation.5 | async-start | bytes 2097152 | tf_op jit(solution)/shard_map/all_to_all | solution.py:95
  279.6 124.8 %all-gather.13.cloned.1.call-start = ((), (), s32[]{:S(2)}) async-start(), calls=%async_computation.17 | async-start | bytes 9437184 | tf_op jit(solution)/shard_map/all_gather | solution.py:147
  279.6 24.2 %copy-start.68 = (f32[256]{0:T(256)}, f32[256]{0:T(256)S(1)}, u32[]{:S(2)}) copy-start(f32[256]{0:T(256)S(1)} %fusion.72) | copy-start | bytes 3076
  303.9 269.7 %reduce-scatter.9.cloned.1.call-start = ((), (), s32[]{:S(2)}) async-start(), calls=%async_computation.18 | async-start | bytes 9437184 | tf_op jit(solution)/shard_map/reduce_scatter | solution.py:240
  304.9 47.0 %copy-start.23 = (f32[8,256,16]{1,2,0:T(8,128)}, f32[8,256,16]{1,2,0:T(8,128)S(1)}, u32[]{:S(2)}) copy-start(f32[8,256,16]{1,2,0:T(8,128)S(1)} %convert_reduce_fusion) | copy-start | bytes 393220
  305.6 39.9 %copy-start.12 = (bf16[2048,16]{1,0:T(8,128)(2,1)}, bf16[2048,16]{1,0:T(8,128)(2,1)S(1)}, u32[]{:S(2)}) copy-start(bf16[2048,16]{1,0:T(8,128)(2,1)S(1)} %reshape.432) | copy-start | bytes 196612
  351.2 18.6 %slice-start = ((s8[9437184]{0:T(1024)(128)(4,1)}), s8[4194304]{0:T(1024)(128)(4,1)S(1)}, s32[]{:S(2)}) async-start(s8[9437184]{0:T(1024)(128)(4,1)} %bitcast.268), calls=%async_computation.29 | async-start | bytes 8388608
  351.9 17.9 %copy-start.27 = (f32[8,256,16]{1,2,0:T(8,128)}, f32[8,256,16]{1,2,0:T(8,128)S(1)}, u32[]{:S(2)}) copy-start(f32[8,256,16]{1,2,0:T(8,128)S(1)} %get-tuple-element.123) | copy-start | bytes 393220
  351.9 17.9 %copy-start.43 = (f32[8,256]{1,0:T(8,128)}, f32[8,256]{1,0:T(8,128)S(1)}, u32[]{:S(2)}) copy-start(f32[8,256]{1,0:T(8,128)S(1)} %get-tuple-element.124) | copy-start | bytes 24580
  352.0 17.9 %copy-start.38 = (f32[8,256,16]{1,2,0:T(8,128)}, f32[8,256,16]{1,2,0:T(8,128)S(1)}, u32[]{:S(2)}) copy-start(f32[8,256,16]{1,2,0:T(8,128)S(1)} %broadcast_divide_fusion.1) | copy-start | bytes 393220
  352.0 17.8 %slice-start.1 = ((s8[9437184]{0:T(1024)(128)(4,1)}), s8[4194304]{0:T(1024)(128)(4,1)S(1)}, s32[]{:S(2)}) async-start(s8[9437184]{0:T(1024)(128)(4,1)} %bitcast.268), calls=%async_computation.30 | async-start | bytes 8388608
  352.0 17.8 %slice-start.2 = ((s8[9437184]{0:T(1024)(128)(4,1)}), s8[1048576]{0:T(1024)(128)(4,1)S(1)}, s32[]{:S(2)}) async-start(s8[9437184]{0:T(1024)(128)(4,1)} %bitcast.268), calls=%async_computation.31 | async-start | bytes 2097152
  502.0 146.8 %reduce-scatter.7.cloned.1.call-start = ((), (), s32[]{:S(2)}) async-start(), calls=%async_computation.16 | async-start | bytes 9437184 | tf_op jit(solution)/shard_map/reduce_scatter | solution.py:327
  515.0 58.5 %copy-start.8 = (f32[256,2048]{1,0:T(8,128)S(1)}, f32[256,2048]{1,0:T(8,128)}, u32[]{:S(2)}) copy-start(f32[256,2048]{1,0:T(8,128)} %copy-done.7) | copy-start | bytes 6291460
  515.0 58.5 %copy-start.42 = (f32[1,2,8,128]{3,1,2,0:T(2,128)S(1)}, f32[1,2,8,128]{3,1,2,0:T(2,128)}, u32[]{:S(2)}) copy-start(f32[1,2,8,128]{3,1,2,0:T(2,128)} %copy-done.41) | copy-start | bytes 24580
  515.1 58.5 %copy-start.58 = (f32[256]{0:T(256)S(1)}, f32[256]{0:T(256)}, u32[]{:S(2)}) copy-start(f32[256]{0:T(256)} %copy-done.57) | copy-start | bytes 3076
  515.1 133.7 %copy-start.11 = (bf16[4,64,2048]{2,1,0:T(8,128)(2,1)S(1)}, bf16[4,64,2048]{2,1,0:T(8,128)(2,1)}, u32[]{:S(2)}) copy-start(bf16[4,64,2048]{2,1,0:T(8,128)(2,1)} %copy-done.10) | copy-start | bytes 3145732
  515.1 133.7 %copy-start.69 = (f32[256]{0:T(256)S(1)}, f32[256]{0:T(256)}, u32[]{:S(2)}) copy-start(f32[256]{0:T(256)} %copy-done.68) | copy-start | bytes 3076
  516.0 137.6 %copy-start.52 = (f32[256]{0:T(256)}, f32[256]{0:T(256)S(1)}, u32[]{:S(2)}) copy-start(f32[256]{0:T(256)S(1)} %fusion.71) | copy-start | bytes 3076
  529.7 8.2 all-to-all-start.5
  533.0 175.1 %all-gather.15.cloned.1.call-start = ((), (), s32[]{:S(2)}) async-start(), calls=%async_computation.19 | async-start | bytes 9437184 | tf_op jit(solution)/shard_map/all_gather | solution.py:271
  534.5 119.1 %copy-start.61 = (f32[16]{0:T(128)}, f32[16]{0:T(128)S(1)}, u32[]{:S(2)}) copy-start(f32[16]{0:T(128)S(1)} %get-tuple-element.122) | copy-start | bytes 196
  535.2 118.4 %copy-start.54 = (f32[1,256]{1,0:T(1,128)}, f32[1,256]{1,0:T(1,128)S(1)}, u32[]{:S(2)}) copy-start(f32[1,256]{1,0:T(1,128)S(1)} %constant_dynamic-slice_fusion) | copy-start | bytes 3076
  537.9 115.7 %copy-start.30 = (f32[16,256]{1,0:T(8,128)}, f32[16,256]{1,0:T(8,128)S(1)}, u32[]{:S(2)}) copy-start(f32[16,256]{1,0:T(8,128)S(1)} %reshape.441) | copy-start | bytes 49156
  538.6 115.0 %copy-start.50 = (f32[256]{0:T(256)}, f32[256]{0:T(256)S(1)}, u32[]{:S(2)}) copy-start(f32[256]{0:T(256)S(1)} %fusion.62) | copy-start | bytes 3076
  539.5 114.1 %copy-start.59 = (f32[256]{0:T(256)}, f32[256]{0:T(256)S(1)}, u32[]{:S(2)}) copy-start(f32[256]{0:T(256)S(1)} %fusion.66) | copy-start | bytes 3076
  653.6 207.6 %reduce-scatter.11.cloned.1.call-start = ((), (), s32[]{:S(2)}) async-start(), calls=%async_computation.20 | async-start | bytes 9437184 | tf_op jit(solution)/shard_map/reduce_scatter | solution.py:298
  744.7 257.2 %reduce-scatter.17.cloned.1.call-start = ((), (), s32[]{:S(2)}) async-start(), calls=%async_computation.24 | async-start | bytes 10485760 | tf_op jit(solution)/shard_map/reduce_scatter | solution.py:217
  762.5 391.1 %reduce-scatter.15.cloned.1.call-start = ((), (), s32[]{:S(2)}) async-start(), calls=%async_computation.23 | async-start | bytes 10485760 | tf_op jit(solution)/shard_map/reduce_scatter | solution.py:246
  779.9 521.4 %reduce-scatter.13.cloned.1.call-start = ((), (), s32[]{:S(2)}) async-start(), calls=%async_computation.22 | async-start | bytes 10485760 | tf_op jit(solution)/shard_map/reduce_scatter | solution.py:246
  809.1 42.5 %all-to-all-start.7 = ((bf16[8,256,768]{2,1,0:T(8,128)(2,1)}), bf16[8,256,768]{2,1,0:T(8,128)(2,1)}, u32[]{:S(2)}, u32[]{:S(2)}) async-start(bf16[8,256,768]{2,1,0:T(8,128)(2,1)} %bitcast.291), calls=%async_computation.10 | async-start | bytes 6291456 | tf_op jit(solution)/shard_map/all_to_all | solution.py:302
  813.7 645.7 %all-reduce.9.cloned.1.call-start = ((), (), s32[]{:S(2)}) async-start(), calls=%async_computation.21 | async-start | bytes 8388608 | tf_op jit(solution)/shard_map/psum | solution.py:319
  856.5 56.3 %all-to-all-start.3 = ((bf16[4,64,2048]{2,1,0:T(8,128)(2,1)}), bf16[4,64,2048]{2,1,0:T(8,128)(2,1)S(1)}, u32[]{:S(2)}, u32[]{:S(2)}) async-start(bf16[4,64,2048]{2,1,0:T(8,128)(2,1)} %bitcast.32), calls=%async_computation.4 | async-start | bytes 2097152 | tf_op jit(solution)/shard_map/all_to_all | solution.py:100
  863.1 58.3 %copy-start.80 = (s32[4]{0:T(128)S(1)}, s32[4]{0:T(128)}, u32[]{:S(2)}) copy-start(s32[4]{0:T(128)} %copy-done.79) | copy-start | bytes 52
  863.1 59.0 %copy-start.9 = (bf16[256,2048]{1,0:T(8,128)(2,1)S(1)}, bf16[256,2048]{1,0:T(8,128)(2,1)}, u32[]{:S(2)}) copy-start(bf16[256,2048]{1,0:T(8,128)(2,1)} %multiply_convert_fusion.10) | copy-start | bytes 3145732
  863.2 59.0 %copy-start.31 = (f32[16,256]{1,0:T(8,128)S(1)}, f32[16,256]{1,0:T(8,128)}, u32[]{:S(2)}) copy-start(f32[16,256]{1,0:T(8,128)} %copy-done.30) | copy-start | bytes 49156
  863.2 59.0 %copy-start.51 = (f32[256]{0:T(256)S(1)}, f32[256]{0:T(256)}, u32[]{:S(2)}) copy-start(f32[256]{0:T(256)} %copy-done.50) | copy-start | bytes 3076
  863.2 59.0 %copy-start.53 = (f32[256]{0:T(256)S(1)}, f32[256]{0:T(256)}, u32[]{:S(2)}) copy-start(f32[256]{0:T(256)} %copy-done.52) | copy-start | bytes 3076
  863.2 59.0 %copy-start.55 = (f32[1,256]{1,0:T(1,128)S(1)}, f32[1,256]{1,0:T(1,128)}, u32[]{:S(2)}) copy-start(f32[1,256]{1,0:T(1,128)} %copy-done.54) | copy-start | bytes 3076
  863.2 59.0 %copy-start.60 = (f32[256]{0:T(256)S(1)}, f32[256]{0:T(256)}, u32[]{:S(2)}) copy-start(f32[256]{0:T(256)} %copy-done.59) | copy-start | bytes 3076
  863.2 59.0 %copy-start.62 = (f32[16]{0:T(128)S(1)}, f32[16]{0:T(128)}, u32[]{:S(2)}) copy-start(f32[16]{0:T(128)} %copy-done.61) | copy-start | bytes 196
  866.8 57.5 %copy-start.56 = (bf16[2048]{0:T(1024)(128)(2,1)S(1)}, bf16[2048]{0:T(1024)(128)(2,1)}, u32[]{:S(2)}) copy-start(bf16[2048]{0:T(1024)(128)(2,1)} %get-tuple-element.109) | copy-start | bytes 12292
  913.8 619.8 %all-to-all-start.6 = ((bf16[4,64,2048]{2,1,0:T(8,128)(2,1)}), bf16[4,64,2048]{2,1,0:T(8,128)(2,1)S(1)}, u32[]{:S(2)}, u32[]{:S(2)}) async-start(bf16[4,64,2048]{2,1,0:T(8,128)(2,1)} %bitcast.60), calls=%async_computation.9 | async-start | bytes 2097152 | tf_op jit(solution)/shard_map/all_to_all | solution.py:100
  921.5 589.9 %all-reduce.15.cloned.1.call-start = ((), (), s32[]{:S(2)}) async-start(), calls=%async_computation.28 | async-start | bytes 151552
  1459.4 76.4 %copy-start.1 = (bf16[256,2048]{1,0:T(8,128)(2,1)S(1)}, bf16[256,2048]{1,0:T(8,128)(2,1)}, u32[]{:S(2)}) copy-start(bf16[256,2048]{1,0:T(8,128)(2,1)} %param.18) | copy-start | bytes 3145732
  (43 other events, 121.2 us)
Sparse Core Ops, SparseCore 0:
  20.8 51.4 all-reduce.10
  76.2 55.3 all-reduce.12
  134.1 55.5 all-gather.8
  191.5 54.3 all-gather.10
  273.5 53.3 all-gather.16
  329.2 54.3 all-gather.12
  502.1 71.4 reduce-scatter.8
  577.4 71.2 reduce-scatter.6
  653.8 54.3 all-gather.14
  744.8 71.2 reduce-scatter.10
  818.6 183.2 reduce-scatter.16
  1004.2 149.3 reduce-scatter.14
  1156.1 145.1 reduce-scatter.12
  1303.7 155.6 all-reduce.8
  1462.3 48.9 all-reduce.14

commit v2 on v1

--- a/solution.py
+++ b/solution.py
@@ -1,8 +1,11 @@
+import functools
 import math
 
 import jax
 import jax.numpy as jnp
 from jax import lax
+from jax.experimental import pallas as pl
+from jax.experimental.pallas import tpu as pltpu
 from jax.sharding import PartitionSpec as P
 
 norm_eps = 1e-06
@@ -10,6 +13,8 @@
 big_negative = -1e30
 bf16 = jnp.bfloat16
 f32 = jnp.float32
+MESH = pl.DeviceIdType.MESH
+DMA = pltpu.SemaphoreType.DMA
 
 
 def norm_fwd(values, scales):
@@ -31,22 +36,529 @@
     positions = jnp.arange(tok_rows, dtype=jnp.int32).astype(f32)
     frequency = rope_base ** (-jnp.arange(half_dim, dtype=jnp.int32).astype(f32) * 2.0 / head_dim)
     angles = positions[:, None] * frequency[None, :]
-    cosine = jnp.concatenate([jnp.cos(angles), jnp.cos(angles)], axis=-1)[:, None, :]
-    sine_table = jnp.concatenate([jnp.sin(angles), jnp.sin(angles)], axis=-1)[:, None, :]
-    return (cosine, sine_table)
-
-
-def turn_half(values):
-    half_dim = values.shape[-1] // 2
-    return jnp.concatenate([-values[..., half_dim:], values[..., :half_dim]], axis=-1)
-
-
-def rotary(values, cosine, sine_table):
-    return values * cosine + turn_half(values) * sine_table
-
-
-def rotary_back(grad_out, cosine, sine_table):
-    return grad_out * cosine - turn_half(grad_out * sine_table)
+    cosine = jnp.concatenate([jnp.cos(angles), jnp.cos(angles)], axis=-1)
+    signed_sine = jnp.concatenate([-jnp.sin(angles), jnp.sin(angles)], axis=-1)
+    return (cosine, signed_sine)
+
+
+def peer(index):
+    return {"expert": index}
+
+
+def remote(src, dst, send, recv, to):
+    return pltpu.make_async_remote_copy(
+        src_ref=src, dst_ref=dst, send_sem=send, recv_sem=recv, device_id=peer(to), device_id_type=MESH
+    )
+
+
+def greet(n, me):
+    barrier = pltpu.get_barrier_semaphore()
+    for k in range(1, n):
+        pl.semaphore_signal(
+            barrier, inc=1, device_id=peer(lax.rem(me + k, n)), device_id_type=MESH
+        )
+    pl.semaphore_wait(barrier, n - 1)
+
+
+def quad_places(me):
+    core = lax.rem(me, 2)
+    chip = me // 2
+    x = lax.rem(chip, 2)
+    y = chip // 2
+
+    def at(px, py, pc):
+        return (py * 2 + px) * 2 + pc
+
+    spots = ((x, y), (1 - x, y), (x, 1 - y), (1 - x, 1 - y))
+    return [at(px, py, core) for px, py in spots], [at(px, py, 1 - core) for px, py in spots]
+
+
+def any_places(n, me):
+    core = lax.rem(me, 2)
+    chip = me // 2
+    chips = n // 2
+    chip_of = [lax.rem(chip + k, chips) for k in range(chips)]
+    chip_from = [lax.rem(chip - k + chips, chips) for k in range(chips)]
+    return (
+        [c * 2 + core for c in chip_of],
+        [c * 2 + 1 - core for c in chip_of],
+        [c * 2 + core for c in chip_from],
+        [c * 2 + 1 - core for c in chip_from],
+    )
+
+
+def small_kernel(n, *refs):
+    ins, outs, (send_sem, recv_sem) = refs[: len(refs) // 2 - 1], refs[len(refs) // 2 - 1 : -2], refs[-2:]
+    me = lax.axis_index("expert")
+    for src, out in zip(ins, outs):
+        out[me] = src[...]
+    greet(n, me)
+    copies = []
+    for k in range(1, n):
+        for i, (src, out) in enumerate(zip(ins, outs)):
+            copy = remote(
+                src, out.at[me], send_sem.at[i, k], recv_sem.at[i, k], lax.rem(me + k, n)
+            )
+            copy.start()
+            copies.append(copy)
+    for copy in copies:
+        copy.wait()
+
+
+def gather_small(n, collective_id, *values):
+    vmem = pl.BlockSpec(memory_space=pltpu.VMEM)
+    return pl.pallas_call(
+        functools.partial(small_kernel, n),
+        out_shape=[jax.ShapeDtypeStruct((n,) + v.shape, v.dtype) for v in values],
+        in_specs=[vmem] * len(values),
+        out_specs=[vmem] * len(values),
+        scratch_shapes=[DMA((len(values), n)), DMA((len(values), n))],
+        compiler_params=pltpu.CompilerParams(collective_id=collective_id, has_side_effects=True),
+        name="gather_small",
+    )(*values)
+
+
+def quad_gather_kernel(parts, x_ref, o_ref, own_sem, send_sem, recv_sem, pass_sem, pair_send, pair_recv):
+    me = lax.axis_index("expert")
+    same, other = quad_places(me)
+    step = x_ref.shape[0] // parts
+    half = parts // 2
+    own = pltpu.make_async_copy(x_ref, o_ref.at[me], own_sem)
+    own.start()
+    greet(8, me)
+    started = []
+
+    def go(copy):
+        copy.start()
+        started.append(copy)
+
+    def piece(p):
+        return pl.ds(p * step, step)
+
+    low, high = list(range(half)), list(range(half, parts))
+    turns = [(k, seq[i]) for i in range(parts) for k, seq in ((1, high + low), (2, low + high))]
+    for k, p in turns:
+        go(remote(x_ref.at[piece(p)], o_ref.at[me, piece(p)], send_sem.at[k, p], recv_sem.at[k, p], same[k]))
+    for p in range(parts):
+        go(remote(x_ref.at[piece(p)], o_ref.at[me, piece(p)], pair_send.at[0, p], pair_recv.at[0, p], other[0]))
+
+    def arrive(k, p):
+        block = o_ref.at[same[k], piece(p)]
+        remote(block, block, send_sem.at[k, p], recv_sem.at[k, p], other[0]).wait_recv()
+        return block
+
+    for k, p in turns:
+        block = arrive(k, p)
+        if (p >= half) == (k == 1):
+            go(remote(block, block, pass_sem.at[p], recv_sem.at[3, p], same[3 - k]))
+        go(remote(block, block, pair_send.at[k, p], pair_recv.at[k, p], other[0]))
+    for pair in zip(low, high):
+        for p in pair:
+            block = arrive(3, p)
+            go(remote(block, block, pair_send.at[3, p], pair_recv.at[3, p], other[0]))
+    for k in range(4):
+        for p in range(parts):
+            block = o_ref.at[other[k], piece(p)]
+            remote(block, block, pair_send.at[k, p], pair_recv.at[k, p], other[0]).wait_recv()
+    for copy in started:
+        copy.wait_send()
+    own.wait()
+
+
+def any_gather_kernel(n, x_ref, o_ref, own_sem, send_sem, recv_sem, pair_send, pair_recv):
+    me = lax.axis_index("expert")
+    same, other, same_from, other_from = any_places(n, me)
+    own = pltpu.make_async_copy(x_ref, o_ref.at[me], own_sem)
+    own.start()
+    greet(n, me)
+    started = []
+    for k in range(n // 2):
+        if k:
+            copy = remote(x_ref, o_ref.at[me], send_sem.at[k], recv_sem.at[k], same[k])
+        else:
+            copy = remote(x_ref, o_ref.at[me], pair_send.at[0], pair_recv.at[0], other[0])
+        copy.start()
+        started.append(copy)
+    for k in range(1, n // 2):
+        block = o_ref.at[same_from[k]]
+        remote(block, block, send_sem.at[k], recv_sem.at[k], other[0]).wait_recv()
+        copy = remote(block, block, pair_send.at[k], pair_recv.at[k], other[0])
+        copy.start()
+        started.append(copy)
+    for k in range(n // 2):
+        block = o_ref.at[other_from[k]]
+        remote(block, block, pair_send.at[k], pair_recv.at[k], other[0]).wait_recv()
+    for copy in started:
+        copy.wait_send()
+    own.wait()
+
+
+def gather_rows(x, n, collective_id, parts=4):
+    chips = n // 2
+    if n == 8:
+        kernel = functools.partial(quad_gather_kernel, parts)
+        sems = [DMA, DMA((4, parts)), DMA((4, parts)), DMA((parts,)), DMA((4, parts)), DMA((4, parts))]
+    else:
+        kernel = functools.partial(any_gather_kernel, n)
+        sems = [DMA, DMA((chips,)), DMA((chips,)), DMA((chips,)), DMA((chips,))]
+    return pl.pallas_call(
+        kernel,
+        out_shape=jax.ShapeDtypeStruct((n,) + x.shape, x.dtype),
+        in_specs=[pl.BlockSpec(memory_space=pl.ANY)],
+        out_specs=pl.BlockSpec(memory_space=pl.ANY),
+        scratch_shapes=sems,
+        compiler_params=pltpu.CompilerParams(collective_id=collective_id, has_side_effects=True),
+        cost_estimate=pl.CostEstimate(flops=0, transcendentals=0, bytes_accessed=n * x.size * 16),
+        name=f"gather_rows_{collective_id}",
+    )(x)
+
+
+def add_rows(total, first, rows, chunk, *terms):
+    @pl.loop(0, rows // chunk)
+    def _(i):
+        s = pl.ds(first + i * chunk, chunk)
+        value = terms[0][s].astype(f32)
+        for term in terms[1:]:
+            value = value + term[s].astype(f32)
+        total[s] = value.astype(total.dtype)
+
+
+def quad_scatter_kernel(
+    parts, p_ref, o_ref, mine, theirs, transit, got, load_sem, pair_send, pair_recv, over_send, over_recv, send_sem, recv_sem
+):
+    me = lax.axis_index("expert")
+    same, other = quad_places(me)
+    step = p_ref.shape[1] // parts
+    half = parts // 2
+    low, high = list(range(half)), list(range(half, parts))
+    mix = [p for pair in zip(low, high) for p in pair]
+    order = (3, 1, 2, 0)
+
+    def piece(p):
+        return pl.ds(p * step, step)
+
+    loads = {}
+    for k in order:
+        for p in mix:
+            loads[k, p] = pltpu.make_async_copy(
+                p_ref.at[same[k], piece(p)], mine.at[k, piece(p)], load_sem.at[k, p]
+            )
+            loads[k, p].start()
+    greet(8, me)
+    started = []
+
+    def go(copy):
+        copy.start()
+        started.append(copy)
+
+    for k in order:
+        for p in mix:
+            go(
+                remote(
+                    p_ref.at[other[k], piece(p)],
+                    theirs.at[k, piece(p)],
+                    pair_send.at[k, p],
+                    pair_recv.at[k, p],
+                    other[0],
+                )
+            )
+
+    def fold(k, p):
+        loads[k, p].wait()
+        spot = theirs.at[k, piece(p)]
+        remote(spot, spot, pair_send.at[k, p], pair_recv.at[k, p], other[0]).wait_recv()
+        add_rows(mine.at[k], p * step, step, 32, mine.at[k], theirs.at[k])
+
+    def ship(k, p):
+        go(
+            remote(
+                mine.at[k, piece(p)],
+                got.at[k - 1, piece(p)],
+                send_sem.at[k - 1, p],
+                recv_sem.at[k - 1, p],
+                same[k],
+            )
+        )
+
+    for p in mix:
+        fold(3, p)
+        to = same[1] if p < half else same[2]
+        go(remote(mine.at[3, piece(p)], transit.at[piece(p)], over_send.at[p], over_recv.at[p], to))
+    for a, b in zip(low, high):
+        for k, p in ((1, a), (2, b)):
+            fold(k, p)
+            ship(k, p)
+    for a, b in zip(low, high):
+        for k, p in ((2, a), (1, b)):
+            fold(k, p)
+            spot = transit.at[piece(p)]
+            remote(spot, spot, over_send.at[p], over_recv.at[p], other[0]).wait_recv()
+            add_rows(mine.at[k], p * step, step, 32, mine.at[k], transit)
+            ship(k, p)
+    for p in mix:
+        fold(0, p)
+    for p in mix:
+        for k in (0, 1):
+            spot = got.at[k, piece(p)]
+            remote(spot, spot, send_sem.at[k, p], recv_sem.at[k, p], other[0]).wait_recv()
+        add_rows(o_ref, p * step, step, 32, mine.at[0], got.at[0], got.at[1])
+    for copy in started:
+        copy.wait_send()
+
+
+def any_scatter_kernel(n, p_ref, o_ref, mine, theirs, got, load_sem, pair_send, pair_recv, send_sem, recv_sem):
+    me = lax.axis_index("expert")
+    same, other, _, _ = any_places(n, me)
+    rows = p_ref.shape[1]
+    order = list(range(1, n // 2)) + [0]
+    loads = {}
+    for k in order:
+        loads[k] = pltpu.make_async_copy(p_ref.at[same[k]], mine.at[k], load_sem.at[k])
+        loads[k].start()
+    greet(n, me)
+    started = []
+    for k in order:
+        copy = remote(p_ref.at[other[k]], theirs.at[k], pair_send.at[k], pair_recv.at[k], other[0])
+        copy.start()
+        started.append(copy)
+    for k in order:
+        loads[k].wait()
+        remote(theirs.at[k], theirs.at[k], pair_send.at[k], pair_recv.at[k], other[0]).wait_recv()
+        add_rows(mine.at[k], 0, rows, 32, mine.at[k], theirs.at[k])
+        if k:
+            copy = remote(mine.at[k], got.at[k], send_sem.at[k], recv_sem.at[k], same[k])
+            copy.start()
+            started.append(copy)
+    for k in range(1, n // 2):
+        remote(got.at[k], got.at[k], send_sem.at[k], recv_sem.at[k], other[0]).wait_recv()
+    add_rows(o_ref, 0, rows, 32, mine.at[0], *[got.at[k] for k in range(1, n // 2)])
+    for copy in started:
+        copy.wait_send()
+
+
+def scatter_sum(x, n, collective_id, parts=4):
+    chips = n // 2
+    shape = x.shape[1:]
+    blocks = pltpu.VMEM((chips,) + shape, bf16)
+    if n == 8:
+        kernel = functools.partial(quad_scatter_kernel, parts)
+        scratch = [blocks, blocks, pltpu.VMEM(shape, bf16), pltpu.VMEM((2,) + shape, bf16)]
+        scratch += [DMA((4, parts))] * 3 + [DMA((parts,))] * 2 + [DMA((2, parts))] * 2
+    else:
+        kernel = functools.partial(any_scatter_kernel, n)
+        scratch = [blocks] * 3 + [DMA((chips,))] * 5
+    return pl.pallas_call(
+        kernel,
+        out_shape=jax.ShapeDtypeStruct(shape, f32),
+        in_specs=[pl.BlockSpec(memory_space=pl.ANY)],
+        out_specs=pl.BlockSpec(memory_space=pltpu.VMEM),
+        scratch_shapes=scratch,
+        compiler_params=pltpu.CompilerParams(
+            collective_id=collective_id, has_side_effects=True, vmem_limit_bytes=(3 * chips + 12) << 20
+        ),
+        cost_estimate=pl.CostEstimate(flops=0, transcendentals=0, bytes_accessed=x.size * 16),
+        name=f"scatter_sum_{collective_id}",
+    )(x)
+
+
+def dot(left, right, left_dim=1, right_dim=0):
+    return lax.dot_general(
+        left, right, (((left_dim,), (right_dim,)), ((), ())), preferred_element_type=f32
+    )
+
+
+def head_values(lin, gain, cosine, signed_sine):
+    inverse = lax.rsqrt(jnp.mean(lin * lin, axis=-1, keepdims=True) + norm_eps)
+    normed = lin * inverse * gain
+    half = lin.shape[1] // 2
+    turned = normed * cosine + pltpu.roll(normed, half, 1) * signed_sine
+    return inverse, turned.astype(bf16)
+
+
+def head_probs(q_rot, k_rot, length, score_scale):
+    scores = dot(q_rot, k_rot, 1, 1) * score_scale
+    key = lax.broadcasted_iota(jnp.int32, scores.shape, 1)
+    masked = jnp.where(key < length, scores, big_negative)
+    raised = jnp.exp(masked - jnp.max(masked, axis=-1, keepdims=True))
+    return raised / jnp.sum(raised, axis=-1, keepdims=True)
+
+
+def attend_kernel(heads, head_dim, lengths_ref, x_ref, w_ref, qg_ref, kg_ref, cos_ref, sin_ref, mixed_ref):
+    length = lengths_ref[pl.program_id(0)]
+    wide = heads * head_dim
+    qkv = dot(x_ref[0], w_ref[...])
+    for h in range(heads):
+        at = h * head_dim
+        _, q_rot = head_values(qkv[:, at : at + head_dim], qg_ref[...], cos_ref[...], sin_ref[...])
+        _, k_rot = head_values(
+            qkv[:, wide + at : wide + at + head_dim], kg_ref[...], cos_ref[...], sin_ref[...]
+        )
+        v = qkv[:, 2 * wide + at : 2 * wide + at + head_dim].astype(bf16)
+        probs = head_probs(q_rot, k_rot, length, 1.0 / math.sqrt(head_dim))
+        mixed_ref[0, :, at : at + head_dim] = dot(probs.astype(bf16), v).astype(bf16)
+
+
+def attend(lengths, x, w_qkv, query_g, key_g, cosine, signed_sine):
+    seqs, rows, width = x.shape
+    head_dim = query_g.shape[0]
+    wide = w_qkv.shape[1] // 3
+    whole = lambda s, lens: (0, 0)
+    table = pl.BlockSpec((rows, head_dim), whole)
+    gain = pl.BlockSpec((1, head_dim), whole)
+    return pl.pallas_call(
+        functools.partial(attend_kernel, wide // head_dim, head_dim),
+        out_shape=jax.ShapeDtypeStruct((seqs, rows, wide), bf16),
+        grid_spec=pltpu.PrefetchScalarGridSpec(
+            num_scalar_prefetch=1,
+            grid=(seqs,),
+            in_specs=[
+                pl.BlockSpec((1, rows, width), lambda s, lens: (s, 0, 0)),
+                pl.BlockSpec((width, 3 * wide), whole),
+                gain,
+                gain,
+                table,
+                table,
+            ],
+            out_specs=pl.BlockSpec((1, rows, wide), lambda s, lens: (s, 0, 0)),
+        ),
+        compiler_params=pltpu.CompilerParams(vmem_limit_bytes=32 << 20),
+        cost_estimate=pl.CostEstimate(
+            flops=2 * seqs * rows * (width * 3 * wide + 2 * rows * wide),
+            transcendentals=seqs * rows * rows * wide // head_dim,
+            bytes_accessed=2 * (x.size + w_qkv.size),
+        ),
+        name="attend",
+    )(lengths, x, w_qkv, query_g[None, :], key_g[None, :], cosine, signed_sine)
+
+
+def attend_back_kernel(
+    heads,
+    head_dim,
+    lengths_ref,
+    x_ref,
+    g_ref,
+    mixed_ref,
+    w_ref,
+    wo_ref,
+    qg_ref,
+    kg_ref,
+    cos_ref,
+    sin_ref,
+    part_ref,
+    dw_ref,
+    dwo_ref,
+    dgain_ref,
+    dw_acc,
+    dwo_acc,
+    gain_acc,
+    gqkv_ref,
+):
+    step = pl.program_id(0)
+    length = lengths_ref[step]
+    wide = heads * head_dim
+    scale = 1.0 / math.sqrt(head_dim)
+    cosine, signed_sine = cos_ref[...], sin_ref[...]
+
+    @pl.when(step == 0)
+    def _():
+        dw_acc[...] = jnp.zeros_like(dw_acc)
+        dwo_acc[...] = jnp.zeros_like(dwo_acc)
+        gain_acc[...] = jnp.zeros_like(gain_acc)
+
+    qkv = dot(x_ref[0], w_ref[...])
+    g_mixed = dot(g_ref[0], wo_ref[...], 1, 1).astype(bf16)
+    dwo_acc[...] += dot(mixed_ref[0], g_ref[0], 0, 0)
+    for h in range(heads):
+        at = h * head_dim
+        q_lin = qkv[:, at : at + head_dim]
+        k_lin = qkv[:, wide + at : wide + at + head_dim]
+        v = qkv[:, 2 * wide + at : 2 * wide + at + head_dim].astype(bf16)
+        q_inv, q_rot = head_values(q_lin, qg_ref[...], cosine, signed_sine)
+        k_inv, k_rot = head_values(k_lin, kg_ref[...], cosine, signed_sine)
+        probs = head_probs(q_rot, k_rot, length, scale)
+        gm = g_mixed[:, at : at + head_dim]
+        g_probs = dot(gm, v, 1, 1)
+        g_scores = (probs * (g_probs - jnp.sum(probs * g_probs, axis=-1, keepdims=True))).astype(bf16)
+        g_v = dot(probs.astype(bf16), gm, 0, 0)
+        for i, (g_rot, lin, inv, gain) in enumerate(
+            (
+                (dot(g_scores, k_rot) * scale, q_lin, q_inv, qg_ref[...]),
+                (dot(g_scores, q_rot, 0, 0) * scale, k_lin, k_inv, kg_ref[...]),
+            )
+        ):
+            w = g_rot * cosine - pltpu.roll(g_rot, head_dim // 2, 1) * signed_sine
+            u = w * gain
+            g_lin = inv * (u - lin * inv * inv * jnp.mean(u * lin, axis=-1, keepdims=True))
+            gain_acc[i : i + 1, :] += jnp.sum(w * lin * inv, axis=0, keepdims=True)
+            gqkv_ref[:, i * wide + at : i * wide + at + head_dim] = g_lin.astype(bf16)
+        gqkv_ref[:, 2 * wide + at : 2 * wide + at + head_dim] = g_v.astype(bf16)
+    gqkv = gqkv_ref[...]
+    part_ref[0] = dot(gqkv, w_ref[...], 1, 1).astype(bf16)
+    dw_acc[...] += dot(x_ref[0], gqkv, 0, 0)
+
+    @pl.when(step == pl.num_programs(0) - 1)
+    def _():
+        dw_ref[...] = dw_acc[...].astype(bf16)
+        dwo_ref[...] = dwo_acc[...].astype(bf16)
+        dgain_ref[...] = gain_acc[...]
+
+
+def attend_back(lengths, x, g, mixed, w_qkv, w_out, query_g, key_g, cosine, signed_sine):
+    seqs, rows, width = x.shape
+    head_dim = query_g.shape[0]
+    wide = w_qkv.shape[1] // 3
+    whole = lambda s, lens: (0, 0)
+    block = lambda s, lens: (s, 0, 0)
+    table = pl.BlockSpec((rows, head_dim), whole)
+    gain = pl.BlockSpec((1, head_dim), whole)
+    return pl.pallas_call(
+        functools.partial(attend_back_kernel, wide // head_dim, head_dim),
+        out_shape=(
+            jax.ShapeDtypeStruct((seqs, rows, width), bf16),
+            jax.ShapeDtypeStruct((width, 3 * wide), bf16),
+            jax.ShapeDtypeStruct((wide, width), bf16),
+            jax.ShapeDtypeStruct((8, head_dim), f32),
+        ),
+        grid_spec=pltpu.PrefetchScalarGridSpec(
+            num_scalar_prefetch=1,
+            grid=(seqs,),
+            in_specs=[
+                pl.BlockSpec((1, rows, width), block),
+                pl.BlockSpec((1, rows, width), block),
+                pl.BlockSpec((1, rows, wide), block),
+                pl.BlockSpec((width, 3 * wide), whole),
+                pl.BlockSpec((wide, width), whole),
+                gain,
+                gain,
+                table,
+                table,
+            ],
+            out_specs=(
+                pl.BlockSpec((1, rows, width), block),
+                pl.BlockSpec((width, 3 * wide), whole),
+                pl.BlockSpec((wide, width), whole),
+                pl.BlockSpec((8, head_dim), whole),
+            ),
+            scratch_shapes=[
+                pltpu.VMEM((width, 3 * wide), f32),
+                pltpu.VMEM((wide, width), f32),
+                pltpu.VMEM((8, head_dim), f32),
+                pltpu.VMEM((rows, 3 * wide), bf16),
+            ],
+        ),
+        compiler_params=pltpu.CompilerParams(vmem_limit_bytes=48 << 20),
+        cost_estimate=pl.CostEstimate(
+            flops=2 * seqs * rows * (width * 11 * wide + 5 * rows * wide),
+            transcendentals=seqs * rows * rows * wide // head_dim,
+            bytes_accessed=2 * (3 * x.size + w_qkv.size * 2),
+        ),
+        name="attend_back",
+    )(lengths, x, g, mixed, w_qkv, w_out, query_g[None, :], key_g[None, :], cosine, signed_sine)
+
+
+def pad_rows(flat, tile):
+    rows = -(-flat.shape[0] // (128 * tile)) * tile
+    return jnp.pad(flat, (0, rows * 128 - flat.shape[0])).reshape(rows, 128)
 
 
 def einf(spec, left, right):
@@ -108,7 +620,9 @@
     small = jnp.concatenate(
         [w_router.reshape(-1), attn_gain, mlp_gain, query_gain, key_gain]
     )
-    small_all = lax.all_gather(small, "expert", axis=0, tiled=False)
+    ints = jnp.concatenate([routes.reshape(-1), jnp.broadcast_to(lengths, (top_k,))])
+    small_all, ints_all = gather_small(groups, 0, pad_rows(small, 16), pad_rows(ints, 8))
+    small_all, ints_all = small_all.reshape(groups, -1), ints_all.reshape(groups, -1)
     n_router = shard_rows * experts
     cuts = [0, n_router]
     for gain in (attn_gain, mlp_gain, query_gain, key_gain):
@@ -119,11 +633,7 @@
     )
     head_dim = query_g.shape[0]
     local_width = w_query.shape[1] // groups
-    local_heads = local_width // head_dim
-    score_scale = 1.0 / math.sqrt(head_dim)
-
-    ints = jnp.concatenate([routes.reshape(-1), jnp.broadcast_to(lengths, (top_k,))])
-    ints_all = lax.all_gather(ints, "expert", axis=0, tiled=False)
+
     routes_all = ints_all[:, : tok_rows * top_k].reshape(groups, tok_rows, top_k)
     lengths_all = ints_all[:, tok_rows * top_k]
     positions = jnp.arange(tok_rows, dtype=jnp.int32)
@@ -142,34 +652,17 @@
     inputs = seq_tokens.astype(f32)
     normed, inv_first = norm_fwd(inputs, attn_g)
     attn_in = normed.astype(bf16)
-    attn_all = lax.all_gather(attn_in, "expert", axis=0, tiled=True)
+    attn_all = gather_rows(attn_in, groups, 1)
     grad_output = seq_cot.astype(f32) * live_rows[:, None]
     cot_all = lax.all_gather(grad_output.astype(bf16), "expert", axis=0, tiled=False)
 
-    qkv = jnp.dot(attn_all, w_qkv, preferred_element_type=f32)
-    heads_shape = (groups, tok_rows, local_heads, head_dim)
-    q_lin = qkv[:, :local_width].reshape(heads_shape)
-    k_lin = qkv[:, local_width : 2 * local_width].reshape(heads_shape)
-    v_heads = qkv[:, 2 * local_width :].astype(bf16).reshape(heads_shape)
-    cosine, sine_table = rotary_tables(tok_rows, head_dim)
-    q_normed, q_inverse = norm_fwd(q_lin, query_g)
-    k_normed, k_inverse = norm_fwd(k_lin, key_g)
-    q_rot = rotary(q_normed, cosine, sine_table).astype(bf16)
-    k_rot = rotary(k_normed, cosine, sine_table).astype(bf16)
-    scores = einf("sthd,suhd->shtu", q_rot, k_rot) * score_scale
-    masked = jnp.where(live_all[:, None, None, :] > 0.5, scores, big_negative)
-    row_max = jnp.max(masked, axis=-1, keepdims=True)
-    raised = jnp.exp(masked - row_max)
-    attn_probs = raised / jnp.sum(raised, axis=-1, keepdims=True)
-    probs_low = attn_probs.astype(bf16)
-    mixed = (
-        einf("shtu,suhd->sthd", probs_low, v_heads).astype(bf16).reshape(groups, tok_rows, local_width)
-    )
+    cosine, signed_sine = rotary_tables(tok_rows, head_dim)
+    mixed = attend(lengths_all, attn_all, w_qkv, query_g, key_g, cosine, signed_sine)
     mixed_here = lax.all_to_all(mixed, "expert", split_axis=0, concat_axis=0, tiled=True)
     hidden = inputs + einf("xtm,xmd->td", mixed_here, wo_full.reshape(groups, local_width, width))
     mlp_normed, inv_second = norm_fwd(hidden, mlp_g)
     mlp_in = mlp_normed.astype(bf16)
-    mlp_all = lax.all_gather(mlp_in, "expert", axis=0, tiled=False)
+    mlp_all = gather_rows(mlp_in, groups, 2)
 
     logits = einf("std,de->ste", mlp_all, router_full)
     router = jax.nn.softmax(logits, axis=-1)
@@ -214,6 +707,7 @@
         (slot_gate[..., None] * cot_slots.astype(f32)).astype(bf16).reshape(local_experts, n_slots, width)
     )
     grad_down_w = einf("jrf,jrd->jfd", act_low, grad_recv)
+    act_low, grad_recv, grad_down_w = lax.optimization_barrier((act_low, grad_recv, grad_down_w))
     total_down = lax.psum_scatter(
         grad_down_w.astype(bf16), "dp", scatter_dimension=1, tiled=True
     ).astype(f32)
@@ -231,17 +725,19 @@
     grad_gate_in = (
         grad_act * up_in * sigmoid_gate * (1.0 + gate_in * (1.0 - sigmoid_gate))
     ).astype(bf16)
+    grad_gate_w = einf("jrd,jrf->jdf", expert_in, grad_gate_in)
+    grad_up_w = einf("jrd,jrf->jdf", expert_in, grad_up_in)
+    grad_gate_in, grad_up_in, grad_gate_w, grad_up_w = lax.optimization_barrier(
+        (grad_gate_in, grad_up_in, grad_gate_w.astype(bf16), grad_up_w.astype(bf16))
+    )
     grad_rows = (
         (einf("jrf,jdf->jrd", grad_gate_in, w_gate) + einf("jrf,jdf->jrd", grad_up_in, w_up))
         .astype(bf16)
         .reshape(local_experts, groups, capacity, width)
     )
     grad_part = einf("jsct,jscd->std", one_hot, grad_rows).astype(bf16)
-    grad_mlp_in = lax.psum_scatter(grad_part, "expert", scatter_dimension=0, tiled=True).astype(f32)
-    grad_mlp_in = grad_mlp_in.reshape(tok_rows, width)
-
-    grad_gate_w = einf("jrd,jrf->jdf", expert_in, grad_gate_in)
-    grad_up_w = einf("jrd,jrf->jdf", expert_in, grad_up_in)
+    grad_mlp_in = scatter_sum(grad_part, groups, 3)
+
     total_gate, total_up = (
         lax.psum_scatter(value.astype(bf16), "dp", scatter_dimension=1, tiled=True).astype(f32)
         for value in (grad_gate_w, grad_up_w)
@@ -268,37 +764,13 @@
     grad_hidden_norm, grad_mlp_g = norm_back(hidden, inv_second, mlp_g, grad_mlp_in, 0)
     grad_hidden = grad_output + grad_hidden_norm
     grad_hidden_low = grad_hidden.astype(bf16)
-    hidden_all = lax.all_gather(grad_hidden_low, "expert", axis=0, tiled=True)
-
-    grad_out_w = einf("rm,rd->md", mixed.reshape(groups * tok_rows, local_width), hidden_all)
-    grad_mixed = einf("rd,md->rm", hidden_all, w_out).astype(bf16).reshape(heads_shape)
-    grad_probs = einf("sthd,suhd->shtu", grad_mixed, v_heads)
-    grad_scores = (
-        attn_probs * (grad_probs - jnp.sum(attn_probs * grad_probs, axis=-1, keepdims=True))
-    ).astype(bf16)
-    grad_q_rot = einf("shtu,suhd->sthd", grad_scores, k_rot) * score_scale
-    grad_k_rot = einf("shtu,sthd->suhd", grad_scores, q_rot) * score_scale
-    grad_values = einf("shtu,sthd->suhd", probs_low, grad_mixed).astype(bf16)
-    grad_q_lin, grad_query_g = norm_back(
-        q_lin, q_inverse, query_g, rotary_back(grad_q_rot, cosine, sine_table), (0, 1, 2)
-    )
-    grad_k_lin, grad_key_g = norm_back(
-        k_lin, k_inverse, key_g, rotary_back(grad_k_rot, cosine, sine_table), (0, 1, 2)
-    )
-    flat = (groups * tok_rows, local_width)
-    grad_qkv = jnp.concatenate(
-        [
-            grad_q_lin.astype(bf16).reshape(flat),
-            grad_k_lin.astype(bf16).reshape(flat),
-            grad_values.reshape(flat),
-        ],
-        axis=1,
-    )
-    grad_attn_part = einf("rm,dm->rd", grad_qkv, w_qkv).astype(bf16)
-    grad_attn_in = lax.psum_scatter(
-        grad_attn_part, "expert", scatter_dimension=0, tiled=True
-    ).astype(f32)
-    grad_qkv_w = einf("rd,rm->dm", attn_all, grad_qkv).astype(bf16)
+    hidden_all = gather_rows(grad_hidden_low, groups, 4)
+    grad_attn_part, grad_qkv_w, grad_out_w, grad_gains = attend_back(
+        lengths_all, attn_all, hidden_all, mixed, w_qkv, w_out, query_g, key_g, cosine, signed_sine
+    )
+    grad_query_g, grad_key_g = grad_gains[0], grad_gains[1]
+    grad_attn_part, total_down = lax.optimization_barrier((grad_attn_part, total_down))
+    grad_attn_in = scatter_sum(grad_attn_part, groups, 5)
     w_back = lax.all_to_all(
         grad_qkv_w.reshape(groups, shard_rows, 3 * local_width),
         "expert",
@@ -313,19 +785,20 @@
             .reshape(shard_rows, groups * local_width)
             for i in range(3)
         ]
-        + [grad_out_w.astype(bf16)],
+        + [grad_out_w],
         axis=0,
     )
+    attn_w, total_up = lax.optimization_barrier((attn_w, total_up))
     attn_sum = lax.psum(attn_w, "dp").astype(f32)
     sum_q, sum_k, sum_v, sum_o = (
         attn_sum[i * shard_rows : (i + 1) * shard_rows] for i in range(4)
     )
 
+    grad_attn_in, total_gate = lax.optimization_barrier((grad_attn_in, total_gate))
     grad_input_norm, grad_attn_g = norm_back(inputs, inv_first, attn_g, grad_attn_in, 0)
     grad_input = undeal((grad_hidden + grad_input_norm).astype(bf16)).astype(f32)
 
-    expert_sum = lax.psum_scatter(sum_part, "expert", scatter_dimension=0, tiled=True)
-    expert_sum = expert_sum.reshape(tok_rows, width).astype(f32)
+    expert_sum = scatter_sum(sum_part, groups, 6)
     output = undeal((live_rows[:, None] * (hidden + expert_sum)).astype(bf16))
 
     pieces = [grad_router_w.astype(bf16).reshape(groups, n_router)] + [

time: 1550 us -> 1060 us (0.68)
  waiting for transfers between devices: 1010 us -> 259 us
  Pallas kernels: 0 us -> 367 us
  matrix products: 277 us -> 219 us
  local copies, waits for them, and re-layouts: 99.1 us -> 69.5 us
  other arithmetic: 68.9 us -> 52.2 us
    pallas_call x0 -> x9, Pallas kernels: none -> 367 us  [the longest x3 145 us: gather_rows(): pl.pallas_call(kernel, out_shape=jax.ShapeDtypeStruct((n,) + x.shape, x.d...]
    reduce_scatter x2, waiting for transfers between devices: 291 us -> 0.02 us  [body(): lax.psum_scatter(value.astype(bf16), 'dp', scatter_dimension=1, tiled=True)]
    unnamed x18 -> x8, waiting for transfers between devices: 140 us -> 11.7 us
    all_gather x3 -> x0, waiting for transfers between devices: 126 us -> none  [the longest x1 54.5 us: body(): hidden_all = lax.all_gather(grad_hidden_low, 'expert', axis=0, tiled=True)]
    reduce_scatter x3 -> x0, waiting for transfers between devices: 105 us -> none  [the longest x1 71 us: body(): lax.psum_scatter(sum_part, 'expert', scatter_dimension=0, tiled=True)]
    reduce_scatter x1, waiting for transfers between devices: 74.7 us -> 0.01 us  [body(): lax.psum_scatter(grad_down_w.astype(bf16), 'dp', scatter_dimension=1, til...]
    dot_general x26 -> x17, matrix products: 257 us -> 213 us  [einf(): return jnp.einsum(spec, left, right, preferred_element_type=f32)]
    all_to_all x2, waiting for transfers between devices: 46 us -> 22.9 us  [undeal(): lax.all_to_all(values.reshape(replicas, block_rows, width), 'dp', split_a...]
  transfers between devices with their start and end apart: 23 -> 15, of which waited for: 17 -> 7; matrix products, arithmetic and copies ran while one was open for 19% -> 27% of each run, Pallas kernels for 0% -> 35%
where the time goes in v2:
time: 1060 us; the launch traced here: 1050 us
  Pallas kernels  367 us (35%)
  waiting for transfers between devices  259 us (24%)
  matrix products  219 us (21%)
  local copies, waits for them, and re-layouts  69.5 us (7%)
  other arithmetic  52.2 us (5%)
  starting transfers between devices  33.2 us (3%)
  blocking collectives  28.3 us (3%)
  between operations  19.3 us (2%)
    dot_general x17, matrix products, einf(): return jnp.einsum(spec, left, right, preferred_element_type=f32)  213 us
    pallas_call x3, Pallas kernels, gather_rows(): pl.pallas_call(kernel, out_shape=jax.ShapeDtypeStruct((n,) + x.shape, x.d...  145 us
    psum x1, waiting for transfers between devices, body(): attn_sum = lax.psum(attn_w, 'dp').astype(f32)  133 us
    pallas_call x3, Pallas kernels, scatter_sum(): pl.pallas_call(kernel, out_shape=jax.ShapeDtypeStruct(shape, f32), in_spe...  122 us
    pallas_call x1, Pallas kernels, attend_back(): pl.pallas_call(functools.partial(attend_back_kernel, wide // head_dim, he...  44.7 us
    all_to_all x2, waiting for transfers between devices, deal(): lax.all_to_all(blocks, 'dp', split_axis=0, concat_axis=0, tiled=True)  42.6 us
    pallas_call x1, Pallas kernels, gather_small(): pl.pallas_call(functools.partial(small_kernel, n), out_shape=[jax.ShapeDt...  39.3 us
    all_to_all x1, waiting for transfers between devices, body(): lax.all_to_all(grad_qkv_w.reshape(groups, shard_rows, 3 * local_width), '...  35.5 us
  transfers between devices with their start and end apart: 15, of which 7 were waited for; matrix products, arithmetic and copies ran while one was open for 27% of the time, Pallas kernels for 35%

profile of v2, /device:TPU:0, one launch (start us, length us, event | category | flops | bytes accessed | tf_op | source)
XLA Modules:
  0.0 1047.0 jit_solution(16375928010656883059)
XLA Ops:
  9.5 1.6 gather_fusion.1
  11.1 6.3 all-to-all-start.3
  17.4 2.8 gather_fusion
  20.2 22.9 %all-to-all-done.3 = bf16[4,64,2048]{2,1,0:T(8,128)(2,1)S(1)} async-done(((bf16[4,64,2048]{2,1,0:T(8,128)(2,1)}), bf16[4,64,2048]{2,1,0:T(8,128)(2,1)S(1)}, u32[]{:S(2)}, u32[]{:S(2)}) %all-to-all-start.3) | async-done | bytes 1048608 | tf_op jit(solution)/shard_map/all_to_all | solution.py:607
  44.1 3.5 all-to-all-start
  49.6 1.7 bitcast_bitcast_fusion
  51.4 1.8 pad_maximum_fusion.1
  53.2 19.7 %all-to-all-done = bf16[4,64,2048]{2,1,0:T(8,128)(2,1)S(1)} async-done(((bf16[4,64,2048]{2,1,0:T(8,128)(2,1)}), bf16[4,64,2048]{2,1,0:T(8,128)(2,1)S(1)}, u32[]{:S(2)}, u32[]{:S(2)}) %all-to-all-start) | async-done | bytes 1048608 | tf_op jit(solution)/shard_map/all_to_all | solution.py:607
  73.8 3.7 all-to-all-start.1
  78.2 39.3 %gather_small.1 = (bf16[8,48,128]{2,1,0:T(8,128)(2,1)}, s32[8,24,128]{2,1,0:T(8,128)}) custom-call(bf16[48,128]{1,0:T(8,128)(2,1)} %pad_bitcast_fusion.refs_0_, s32[24,128]{1,0:T(8,128)} %select_bitcast_fusion.refs_1_), custom_call_target="tpu_custom_call" | custom-call | tf_op jit(solution)/shard_map/gather_small/pallas_call | solution.py:110
  123.1 1.5 fusion.33
  124.7 2.5 fusion.27.x_ref
  127.2 65.8 %gather_rows_1.1.x_ref = bf16[8,256,2048]{2,1,0:T(8,128)(2,1)} custom-call(bf16[256,2048]{1,0:T(8,128)(2,1)} %fusion.27.x_ref), custom_call_target="tpu_custom_call" | custom-call | bytes 67108864 | tf_op jit(solution)/shard_map/gather_rows_1/pallas_call | solution.py:204
  193.1 4.6 copy-done.4
  197.7 15.8 %attend.1.mixed_ref = bf16[8,256,256]{2,1,0:T(8,128)(2,1)S(1)} custom-call(s32[8]{0:T(128)S(1)} %slice_reduce_fusion.lengths_ref, bf16[8,256,2048]{2,1,0:T(8,128)(2,1)S(1)} %copy-done.4, bf16[2048,768]{1,0:T(8,128)(2,1)S(1)} %bitcast.230, f32[1,128]{1,0:T(1,128)S(1)} %reshape.388.qg_ref, f32[1,128]{1,0:T(1,128)S(1)} %reshape.389.kg_ref, ...), custom_call_target="tpu_custom_call" | custom-call | flops 6979321856 | bytes 11534336 | tf_op jit(solution)/shard_map/attend/pallas_call | solution.py:408
  214.4 3.6 all-to-all-start.2
  220.7 12.7 %all-to-all-done.2 = bf16[8,256,256]{2,1,0:T(8,128)(2,1)S(1)} async-done(((bf16[8,256,256]{2,1,0:T(8,128)(2,1)}), bf16[8,256,256]{2,1,0:T(8,128)(2,1)S(1)}, u32[]{:S(2)}, u32[]{:S(2)}) %all-to-all-start.2) | async-done | bytes 1048608 | tf_op jit(solution)/shard_map/all_to_all | solution.py:661
  233.3 6.1 multiply_reduce_fusion.2
  241.9 39.5 %gather_rows_2.1 = bf16[8,256,2048]{2,1,0:T(8,128)(2,1)} custom-call(bf16[256,2048]{1,0:T(8,128)(2,1)} %multiply_convert_fusion.8.x_ref), custom_call_target="tpu_custom_call" | custom-call | bytes 67108864 | tf_op jit(solution)/shard_map/gather_rows_2/pallas_call | solution.py:204
  281.5 8.6 convert_bitcast_fusion
  290.1 9.3 copy.116
  299.4 5.7 fusion.65
  308.4 17.2 %fusion.70 = f32[2,1152,1024]{2,1,0:T(8,128)} fusion(bf16[2,1152,2048]{2,1,0:T(8,128)(2,1)} %bitcast.233, bf16[2,2048,1024]{2,1,0:T(8,128)(2,1)} %param.33), kind=kOutput, calls=%fused_computation.153 | convolution fusion | flops 9663676416 | bytes 27262976 | tf_op jit(solution)/shard_map/jrd,jdf->jrf/dot_general | solution.py:565
  325.6 17.8 %multiply_convert_fusion.4 = (bf16[2,1152,1024]{2,1,0:T(8,128)(2,1)}, f32[2,1152,1024]{2,1,0:T(8,128)}) fusion(f32[2,1152,1024]{2,1,0:T(8,128)} %fusion.70, bf16[2,1152,2048]{2,1,0:T(8,128)(2,1)S(1)} %bitcast.238, bf16[2,2048,1024]{2,1,0:T(8,128)(2,1)} %param.34), kind=kOutput, calls=%fused_computation.19 | convolution fusion | flops 9677832192 | bytes 41418752 | tf_op jit(solution)/shard_map/jrd,jdf->jrf/dot_general | solution.py:565
  343.4 12.3 %fusion.1 = (bf16[2,8,144,2048]{3,2,0,1:T(8,128)(2,1)}, bf16[8,2048,2,144]{1,3,2,0:T(8,128)(2,1)}) fusion(f32[2,8,144]{2,0,1:T(2,128)S(1)} %select_reduce_fusion.1, s32[2,8,256]{2,0,1:T(2,128)S(1)} %copy.114, bf16[8,256,2048]{2,1,0:T(8,128)(2,1)} %all-gather.5.cloned.1.call-done), kind=kOutput, calls=%fused_computation.7 | convolution fusion | flops 2435383296 | bytes 27288576 | tf_op jit(solution)/shard_map/jsct,std->jscd/dot_general | solution.py:565
  355.7 9.3 copy.117
  365.0 17.7 %fusion.71 = bf16[2,1024,2048]{2,1,0:T(8,128)(2,1)} fusion(bf16[2,1152,1024]{2,1,0:T(8,128)(2,1)} %get-tuple-element.36, bf16[2,1152,2048]{2,1,0:T(8,128)(2,1)} %bitcast.239), kind=kOutput, calls=%fused_computation.154 | convolution fusion | flops 9663676416 | bytes 22544384 | tf_op jit(solution)/shard_map/jrf,jrd->jfd/dot_general | solution.py:565
  382.8 22.1 %multiply_convert_fusion.2 = (bf16[2,1152,1024]{2,1,0:T(8,128)(2,1)}, bf16[2,1152,1024]{2,1,0:T(8,128)(2,1)}) fusion(f32[2,1152,1024]{2,1,0:T(8,128)} %fusion.70, f32[2,1152,1024]{2,1,0:T(8,128)} %get-tuple-element.152, bf16[2,1152,2048]{2,1,0:T(8,128)(2,1)} %bitcast.240, bf16[2,1024,2048]{2,1,0:T(8,128)(2,1)} %param.35), kind=kOutput, calls=%fused_computation.17 | convolution fusion | flops 9694347264 | bytes 46137344 | tf_op jit(solution)/shard_map/jrd,jfd->jrf/dot_general | solution.py:565
  404.9 17.1 %convolution_convert_fusion.1 = bf16[2,2048,1024]{2,1,0:T(8,128)(2,1)} fusion(bf16[2,1152,2048]{2,1,0:T(8,128)(2,1)} %bitcast.234, bf16[2,1152,1024]{2,1,0:T(8,128)(2,1)} %get-tuple-element.39), kind=kOutput, calls=%fused_computation.29 | convolution fusion | flops 9667870720 | bytes 22544384 | tf_op jit(solution)/shard_map/jrd,jrf->jdf/dot_general | solution.py:565
  422.0 17.5 %convolution_convert_fusion.2 = bf16[2,2048,1024]{2,1,0:T(8,128)(2,1)} fusion(bf16[2,1152,2048]{2,1,0:T(8,128)(2,1)} %bitcast.235, bf16[2,1152,1024]{2,1,0:T(8,128)(2,1)} %get-tuple-element.38), kind=kOutput, calls=%fused_computation.30 | convolution fusion | flops 9667870720 | bytes 22544384 | tf_op jit(solution)/shard_map/jrd,jrf->jdf/dot_general | solution.py:565
  441.6 8.9 psum.21
  453.1 16.5 %convolution_convert_fusion = bf16[2,1152,2048]{2,1,0:T(8,128)(2,1)} fusion(bf16[2,1152,1024]{2,1,0:T(8,128)(2,1)} %get-tuple-element.36, bf16[2,1024,2048]{2,1,0:T(8,128)(2,1)} %param.35), kind=kOutput, calls=%fused_computation.13 | convolution fusion | flops 9668395008 | bytes 22544384 | tf_op jit(solution)/shard_map/jrf,jfd->jrd/dot_general | solution.py:565
  469.5 9.0 fusion.2
  479.6 3.3 all-to-all-start.5
  483.5 11.8 %bitcast_convert_fusion.1.p_ref = bf16[8,256,2048]{2,1,0:T(8,128)(2,1)} fusion(f32[2,8,144]{2,0,1:T(2,128)S(1)} %select_reduce_fusion.1, s32[2,8,256]{2,0,1:T(2,128)S(1)} %copy.114, bf16[2,8,144,2048]{3,2,1,0:T(8,128)(2,1)} %bitcast.242), kind=kOutput, calls=%fused_computation.12 | convolution fusion | flops 2434859008 | bytes 17851392 | tf_op jit(solution)/shard_map/jsct,jscd->std/dot_general | solution.py:565
  495.4 16.2 %fusion.72 = f32[2,1152,2048]{2,1,0:T(8,128)} fusion(bf16[2,1152,1024]{2,1,0:T(8,128)(2,1)S(1)} %bitcast.275, bf16[2,2048,1024]{2,1,0:T(8,128)(2,1)} %param.33), kind=kOutput, calls=%fused_computation.155 | convolution fusion | flops 9663676416 | bytes 31981568 | tf_op jit(solution)/shard_map/jrf,jdf->jrd/dot_general | solution.py:565
  511.6 18.8 %add_convert_fusion = bf16[2,1152,2048]{2,1,0:T(8,128)(2,1)} fusion(f32[2,1152,2048]{2,1,0:T(8,128)} %fusion.72, bf16[2,1152,1024]{2,1,0:T(8,128)(2,1)} %get-tuple-element.39, bf16[2,2048,1024]{2,1,0:T(8,128)(2,1)} %param.34), kind=kOutput, calls=%fused_computation.9 | convolution fusion | flops 9673113600 | bytes 41418752 | tf_op jit(solution)/shard_map/jrf,jdf->jrd/dot_general | solution.py:565
  530.4 9.0 bitcast_convert_fusion.p_ref
  539.4 41.5 %scatter_sum_6.1 = f32[256,2048]{1,0:T(8,128)S(1)} custom-call(bf16[8,256,2048]{2,1,0:T(8,128)(2,1)S(1)} %copy-done.3), custom_call_target="tpu_custom_call" | custom-call | bytes 67108864 | tf_op jit(solution)/shard_map/scatter_sum_6/pallas_call | solution.py:350
  580.9 40.2 %scatter_sum_3.1 = f32[256,2048]{1,0:T(8,128)S(1)} custom-call(bf16[8,256,2048]{2,1,0:T(8,128)(2,1)S(1)} %bitcast_convert_fusion.p_ref), custom_call_target="tpu_custom_call" | custom-call | bytes 67108864 | tf_op jit(solution)/shard_map/scatter_sum_3/pallas_call | solution.py:350
  624.2 3.3 multiply_reduce_fusion
  627.5 4.2 fusion.59
  631.8 40.1 %gather_rows_4.1.g_ref = bf16[8,256,2048]{2,1,0:T(8,128)(2,1)} custom-call(bf16[256,2048]{1,0:T(8,128)(2,1)} %get-tuple-element.121.x_ref), custom_call_target="tpu_custom_call" | custom-call | bytes 67108864 | tf_op jit(solution)/shard_map/gather_rows_4/pallas_call | solution.py:204
  671.9 44.7 %attend_back.1 = (bf16[8,256,2048]{2,1,0:T(8,128)(2,1)}, bf16[2048,768]{1,0:T(8,128)(2,1)}, bf16[256,2048]{1,0:T(8,128)(2,1)S(1)}, f32[8,128]{1,0:T(8,128)S(1)}) custom-call(s32[8]{0:T(128)S(1)} %copy-done.11, bf16[8,256,2048]{2,1,0:T(8,128)(2,1)} %gather_rows_1.1.x_ref, bf16[8,256,2048]{2,1,0:T(8,128)(2,1)} %gather_rows_4.1.g_ref, ...), custom_call_target="tpu_custom_call" | custom-call | flops 24964497408 | bytes 31457280 | tf_op jit(solution)/shard_map/attend_back/pallas_call | solution.py:514
  716.6 4.6 all-to-all-start.7
  723.6 35.5 %all-to-all-done.7 = bf16[8,256,768]{2,1,0:T(8,128)(2,1)} async-done(((bf16[8,256,768]{2,1,0:T(8,128)(2,1)}), bf16[8,256,768]{2,1,0:T(8,128)(2,1)}, u32[]{:S(2)}, u32[]{:S(2)}) %all-to-all-start.7) | async-done | bytes 3145760 | tf_op jit(solution)/shard_map/all_to_all | solution.py:774
  759.1 2.2 slice_bitcast_fusion.2
  764.6 4.1 convert_element_type.315
  768.8 3.4 copy-done.2
  772.2 40.0 %scatter_sum_5.1 = f32[256,2048]{1,0:T(8,128)S(1)} custom-call(bf16[8,256,2048]{2,1,0:T(8,128)(2,1)S(1)} %copy-done.2), custom_call_target="tpu_custom_call" | custom-call | bytes 67108864 | tf_op jit(solution)/shard_map/scatter_sum_5/pallas_call | solution.py:350
  812.2 4.2 convert_element_type.316
  817.8 3.6 pad_maximum_fusion
  821.4 4.2 convert_element_type.320
  825.6 4.3 all-to-all-start.4
  829.9 3.2 fusion.32
  833.1 22.9 %all-to-all-done.4 = bf16[4,64,2048]{2,1,0:T(8,128)(2,1)} async-done(((bf16[4,64,2048]{2,1,0:T(8,128)(2,1)}), bf16[4,64,2048]{2,1,0:T(8,128)(2,1)}, u32[]{:S(2)}, u32[]{:S(2)}) %all-to-all-start.4) | async-done | bytes 1048608 | tf_op jit(solution)/shard_map/all_to_all | solution.py:612
  856.0 3.5 all-to-all-start.6
  860.8 2.8 gather_fusion.2
  863.6 10.4 all-reduce.9.cloned.1.call-done
  874.0 1.6 dynamic-slice_reduce_fusion
  875.6 19.5 %psum.23 = bf16[4640]{0:T(1024)(128)(2,1)S(1)} all-reduce(bf16[4640]{0:T(1024)(128)(2,1)S(1)} %dynamic-slice_reduce_fusion), channel_id=1, replica_groups=mesh['dp'=4,'expert'=8] {'dp'}, use_global_device_ids=true, to_apply=%region_26.27 | all-reduce | flops 4640 | bytes 18560 | tf_op jit(solution)/shard_map/psum | solution.py:811
  897.6 1.6 bitcast_convert_fusion.2
  899.3 133.3 %all-reduce.7.cloned.1.call-done = bf16[1024,2048]{1,0:T(8,128)(2,1)} async-done(((bf16[1024,2048]{1,0:T(8,128)(2,1)}), bf16[1024,2048]{1,0:T(8,128)(2,1)}) %all-reduce.7.cloned.1.call-update) | async-done | bytes 4194320 | tf_op jit(solution)/shard_map/psum | solution.py:792
  1032.6 5.9 fusion.62
  (216 shorter events, 39.4 us)
Async XLA Ops:
  7.2 2.3 copy-start
  7.2 41.1 %copy-start.38 = (bf16[256,16]{0,1:T(8,128)(2,1)S(1)}, bf16[256,16]{0,1:T(8,128)(2,1)}, u32[]{:S(2)}) copy-start(bf16[256,16]{0,1:T(8,128)(2,1)} %param.28) | copy-start | bytes 24580
  7.2 41.3 %copy-start.39 = (s32[256,8]{0,1:T(8,128)S(1)}, s32[256,8]{0,1:T(8,128)}, u32[]{:S(2)}) copy-start(s32[256,8]{0,1:T(8,128)} %param.22) | copy-start | bytes 24580
  7.2 41.6 %copy-start.25 = (bf16[256,2048]{1,0:T(8,128)(2,1)S(1)}, bf16[256,2048]{1,0:T(8,128)(2,1)}, u32[]{:S(2)}) copy-start(bf16[256,2048]{1,0:T(8,128)(2,1)} %param.24) | copy-start | bytes 3145732
  7.2 41.7 %copy-start.47 = (bf16[16]{0:T(256)(128)(2,1)S(1)}, bf16[16]{0:T(256)(128)(2,1)}, u32[]{:S(2)}) copy-start(bf16[16]{0:T(256)(128)(2,1)} %param.32) | copy-start | bytes 100
  7.2 41.7 %copy-start.46 = (bf16[16]{0:T(256)(128)(2,1)S(1)}, bf16[16]{0:T(256)(128)(2,1)}, u32[]{:S(2)}) copy-start(bf16[16]{0:T(256)(128)(2,1)} %param.31) | copy-start | bytes 100
  7.2 41.7 %copy-start.45 = (bf16[256]{0:T(256)(128)(2,1)S(1)}, bf16[256]{0:T(256)(128)(2,1)}, u32[]{:S(2)}) copy-start(bf16[256]{0:T(256)(128)(2,1)} %param.30) | copy-start | bytes 1540
  7.3 41.7 %copy-start.44 = (bf16[256]{0:T(256)(128)(2,1)S(1)}, bf16[256]{0:T(256)(128)(2,1)}, u32[]{:S(2)}) copy-start(bf16[256]{0:T(256)(128)(2,1)} %param.29) | copy-start | bytes 1540
  7.3 226.0 %all-gather.3.cloned.1.call-start = ((), (), s32[]{:S(2)}) async-start(), calls=%async_computation.11 | async-start | bytes 9437184 | tf_op jit(solution)/shard_map/all_gather | solution.py:650
  11.1 32.0 %all-to-all-start.3 = ((bf16[4,64,2048]{2,1,0:T(8,128)(2,1)}), bf16[4,64,2048]{2,1,0:T(8,128)(2,1)S(1)}, u32[]{:S(2)}, u32[]{:S(2)}) async-start(bf16[4,64,2048]{2,1,0:T(8,128)(2,1)} %gather_fusion.1), calls=%async_computation.3 | async-start | bytes 2097152 | tf_op jit(solution)/shard_map/all_to_all | solution.py:607
  44.1 28.7 %all-to-all-start = ((bf16[4,64,2048]{2,1,0:T(8,128)(2,1)}), bf16[4,64,2048]{2,1,0:T(8,128)(2,1)S(1)}, u32[]{:S(2)}, u32[]{:S(2)}) async-start(bf16[4,64,2048]{2,1,0:T(8,128)(2,1)} %gather_fusion), calls=%async_computation | async-start | bytes 2097152 | tf_op jit(solution)/shard_map/all_to_all | solution.py:607
  73.8 119.2 %all-to-all-start.1 = ((bf16[8,256,768]{2,1,0:T(8,128)(2,1)}), bf16[8,256,768]{2,1,0:T(8,128)(2,1)S(1)}, u32[]{:S(2)}, u32[]{:S(2)}) async-start(bf16[8,256,768]{2,1,0:T(8,128)(2,1)} %pad_maximum_fusion.1), calls=%async_computation.1 | async-start | bytes 6291456 | tf_op jit(solution)/shard_map/all_to_all | solution.py:647
  77.5 265.9 %all-gather.5.cloned.1.call-start = ((), (), s32[]{:S(2)}) async-start(), calls=%async_computation.12 | async-start | bytes 9437184 | tf_op jit(solution)/shard_map/all_gather | solution.py:657
  118.4 4.6 copy-start.27
  119.4 2.9 copy-start.40
  119.5 101.1 %copy-start.10 = (s32[8]{0:T(128)}, s32[8]{0:T(128)S(1)}, u32[]{:S(2)}) copy-start(s32[8]{0:T(128)S(1)} %slice_reduce_fusion.lengths_ref) | copy-start | bytes 100
  122.3 70.8 %copy-start.12 = (f32[1,128]{1,0:T(1,128)}, f32[1,128]{1,0:T(1,128)S(1)}, u32[]{:S(2)}) copy-start(f32[1,128]{1,0:T(1,128)S(1)} %reshape.389.kg_ref) | copy-start | bytes 1540
  122.4 70.7 %copy-start.14 = (f32[1,128]{1,0:T(1,128)}, f32[1,128]{1,0:T(1,128)S(1)}, u32[]{:S(2)}) copy-start(f32[1,128]{1,0:T(1,128)S(1)} %reshape.388.qg_ref) | copy-start | bytes 1540
  122.4 70.6 %copy-start.29 = (f32[1,2,8,128]{3,1,2,0:T(2,128)}, f32[1,2,8,128]{3,1,2,0:T(2,128)S(1)}, u32[]{:S(2)}) copy-start(f32[1,2,8,128]{3,1,2,0:T(2,128)S(1)} %copy.147) | copy-start | bytes 24580
  124.7 88.7 %copy-start.34 = (f32[256]{0:T(256)}, f32[256]{0:T(256)S(1)}, u32[]{:S(2)}) copy-start(f32[256]{0:T(256)S(1)} %rsqrt.20) | copy-start | bytes 3076
  193.0 20.4 %copy-start.6 = (bf16[8,256,768]{2,1,0:T(8,128)(2,1)}, bf16[8,256,768]{2,1,0:T(8,128)(2,1)S(1)}, u32[]{:S(2)}) copy-start(bf16[8,256,768]{2,1,0:T(8,128)(2,1)S(1)} %all-to-all-done.1) | copy-start | bytes 9437188
  193.1 4.6 copy-start.4
  213.4 1.0 copy-start.8
  214.4 18.9 %all-to-all-start.2 = ((bf16[8,256,256]{2,1,0:T(8,128)(2,1)}), bf16[8,256,256]{2,1,0:T(8,128)(2,1)S(1)}, u32[]{:S(2)}, u32[]{:S(2)}) async-start(bf16[8,256,256]{2,1,0:T(8,128)(2,1)} %copy-done.8), calls=%async_computation.2 | async-start | bytes 2097152 | tf_op jit(solution)/shard_map/all_to_all | solution.py:661
  218.0 546.7 %reduce-scatter.4.cloned.1.call-start = ((), (), s32[]{:S(2)}) async-start(), calls=%async_computation.13 | async-start | bytes 10485760 | tf_op jit(solution)/shard_map/reduce_scatter | solution.py:711
  218.9 20.5 %copy-start.31 = (f32[1,2,8,128]{3,1,2,0:T(2,128)}, f32[1,2,8,128]{3,1,2,0:T(2,128)S(1)}, u32[]{:S(2)}) copy-start(f32[1,2,8,128]{3,1,2,0:T(2,128)S(1)} %copy.148) | copy-start | bytes 24580
  219.3 80.1 %copy-start.23 = (bf16[2048,16]{1,0:T(8,128)(2,1)}, bf16[2048,16]{1,0:T(8,128)(2,1)S(1)}, u32[]{:S(2)}) copy-start(bf16[2048,16]{1,0:T(8,128)(2,1)S(1)} %reshape.371) | copy-start | bytes 196612
  220.3 85.5 %copy-start.24 = (f32[8,256,16]{1,2,0:T(8,128)}, f32[8,256,16]{1,2,0:T(8,128)S(1)}, u32[]{:S(2)}) copy-start(f32[8,256,16]{1,2,0:T(8,128)S(1)} %convert_reduce_fusion) | copy-start | bytes 393220
  239.4 1.3 copy-start.19
  239.4 42.1 %copy-start.36 = (f32[256]{0:T(256)}, f32[256]{0:T(256)S(1)}, u32[]{:S(2)}) copy-start(f32[256]{0:T(256)S(1)} %add_rsqrt_fusion.1) | copy-start | bytes 3076
  305.1 20.5 %slice-start = ((s8[9437184]{0:T(1024)(128)(4,1)}), s8[4194304]{0:T(1024)(128)(4,1)S(1)}, s32[]{:S(2)}) async-start(s8[9437184]{0:T(1024)(128)(4,1)} %bitcast.236), calls=%async_computation.18 | async-start | bytes 8388608
  308.4 17.3 %slice-start.1 = ((s8[9437184]{0:T(1024)(128)(4,1)}), s8[4194304]{0:T(1024)(128)(4,1)S(1)}, s32[]{:S(2)}) async-start(s8[9437184]{0:T(1024)(128)(4,1)} %bitcast.236), calls=%async_computation.19 | async-start | bytes 8388608
  308.4 17.3 %slice-start.2 = ((s8[9437184]{0:T(1024)(128)(4,1)}), s8[1048576]{0:T(1024)(128)(4,1)S(1)}, s32[]{:S(2)}) async-start(s8[9437184]{0:T(1024)(128)(4,1)} %bitcast.236), calls=%async_computation.20 | async-start | bytes 2097152
  382.7 429.5 %reduce-scatter.6.cloned.1.call-start = ((), (), s32[]{:S(2)}) async-start(), calls=%async_computation.14 | async-start | bytes 10485760 | tf_op jit(solution)/shard_map/reduce_scatter | solution.py:742
  439.5 1.4 copy-start.42
  439.5 1.4 copy-start.43
  479.6 142.9 %all-to-all-start.5 = ((f32[8,2,256]{2,1,0:T(2,128)}), f32[8,2,256]{2,1,0:T(2,128)S(1)}, u32[]{:S(2)}, u32[]{:S(2)}) async-start(f32[8,2,256]{2,1,0:T(2,128)} %bitcast.44), calls=%async_computation.5 | async-start | bytes 32768 | tf_op jit(solution)/shard_map/all_to_all | solution.py:746
  482.9 338.4 %reduce-scatter.8.cloned.1.call-start = ((), (), s32[]{:S(2)}) async-start(), calls=%async_computation.15 | async-start | bytes 10485760 | tf_op jit(solution)/shard_map/reduce_scatter | solution.py:742
  483.0 12.4 %slice-start.3 = ((s8[4718592]{0:T(1024)(128)(4,1)}), s8[524288]{0:T(1024)(128)(4,1)S(1)}, s32[]{:S(2)}) async-start(s8[4718592]{0:T(1024)(128)(4,1)} %bitcast.274), calls=%async_computation.21 | async-start | bytes 1048576
  483.5 11.9 %slice-start.4 = ((s8[4718592]{0:T(1024)(128)(4,1)}), s8[4194304]{0:T(1024)(128)(4,1)S(1)}, s32[]{:S(2)}) async-start(s8[4718592]{0:T(1024)(128)(4,1)} %bitcast.274), calls=%async_computation.22 | async-start | bytes 8388608
  530.4 9.0 copy-start.3
  580.9 43.3 %copy-start.32 = (f32[1,2,8,128]{3,1,2,0:T(2,128)S(1)}, f32[1,2,8,128]{3,1,2,0:T(2,128)}, u32[]{:S(2)}) copy-start(f32[1,2,8,128]{3,1,2,0:T(2,128)} %copy-done.31) | copy-start | bytes 24580
  580.9 43.3 %copy-start.37 = (f32[256]{0:T(256)S(1)}, f32[256]{0:T(256)}, u32[]{:S(2)}) copy-start(f32[256]{0:T(256)} %copy-done.36) | copy-start | bytes 3076
  580.9 46.6 %copy-start.41 = (f32[256]{0:T(256)S(1)}, f32[256]{0:T(256)}, u32[]{:S(2)}) copy-start(f32[256]{0:T(256)} %copy-done.40) | copy-start | bytes 3076
  621.1 1.3 copy-start.5
  622.5 5.1 copy-start.20
  631.8 40.1 %copy-start.7 = (bf16[256,2048]{1,0:T(8,128)(2,1)S(1)}, bf16[256,2048]{1,0:T(8,128)(2,1)}, u32[]{:S(2)}) copy-start(bf16[256,2048]{1,0:T(8,128)(2,1)} %wo_ref.1) | copy-start | bytes 3145732
  631.8 40.1 %copy-start.9 = (bf16[8,256,256]{2,1,0:T(8,128)(2,1)S(1)}, bf16[8,256,256]{2,1,0:T(8,128)(2,1)}, u32[]{:S(2)}) copy-start(bf16[8,256,256]{2,1,0:T(8,128)(2,1)} %copy-done.8) | copy-start | bytes 3145732
  631.8 40.1 %copy-start.13 = (f32[1,128]{1,0:T(1,128)S(1)}, f32[1,128]{1,0:T(1,128)}, u32[]{:S(2)}) copy-start(f32[1,128]{1,0:T(1,128)} %copy-done.12) | copy-start | bytes 1540
  631.8 40.1 %copy-start.15 = (f32[1,128]{1,0:T(1,128)S(1)}, f32[1,128]{1,0:T(1,128)}, u32[]{:S(2)}) copy-start(f32[1,128]{1,0:T(1,128)} %copy-done.14) | copy-start | bytes 1540
  716.6 4.7 copy-start.22
  716.6 42.5 %all-to-all-start.7 = ((bf16[8,256,768]{2,1,0:T(8,128)(2,1)}), bf16[8,256,768]{2,1,0:T(8,128)(2,1)}, u32[]{:S(2)}, u32[]{:S(2)}) async-start(bf16[8,256,768]{2,1,0:T(8,128)(2,1)} %bitcast.250), calls=%async_computation.9 | async-start | bytes 6291456 | tf_op jit(solution)/shard_map/all_to_all | solution.py:774
  721.3 152.7 %all-reduce.9.cloned.1.call-start = ((), (), s32[]{:S(2)}) async-start(), calls=%async_computation.17 | async-start | bytes 151552
  768.8 3.4 copy-start.2
  772.2 44.2 %copy-start.30 = (f32[1,2,8,128]{3,1,2,0:T(2,128)S(1)}, f32[1,2,8,128]{3,1,2,0:T(2,128)}, u32[]{:S(2)}) copy-start(f32[1,2,8,128]{3,1,2,0:T(2,128)} %copy-done.29) | copy-start | bytes 24580
  772.2 44.2 %copy-start.35 = (f32[256]{0:T(256)S(1)}, f32[256]{0:T(256)}, u32[]{:S(2)}) copy-start(f32[256]{0:T(256)} %copy-done.34) | copy-start | bytes 3076
  812.2 4.2 copy-start.17
  817.7 214.9 %all-reduce.7.cloned.1.call-start = ((), (), s32[]{:S(2)}) async-start(), calls=%async_computation.16 | async-start | bytes 8388608 | tf_op jit(solution)/shard_map/psum | solution.py:792
  821.4 8.5 copy-start.18
  825.5 34.0 %copy-start.50 = (u32[32]{0:T(128)S(1)}, u32[32]{0:T(128)}, u32[]{:S(2)}) copy-start(u32[32]{0:T(128)} %constant.84) | copy-start | bytes 388
  825.6 34.5 %copy-start.49 = (s32[4]{0:T(128)S(1)}, s32[4]{0:T(128)}, u32[]{:S(2)}) copy-start(s32[4]{0:T(128)} %copy-done.48) | copy-start | bytes 52
  825.6 30.4 %all-to-all-start.4 = ((bf16[4,64,2048]{2,1,0:T(8,128)(2,1)}), bf16[4,64,2048]{2,1,0:T(8,128)(2,1)}, u32[]{:S(2)}, u32[]{:S(2)}) async-start(bf16[4,64,2048]{2,1,0:T(8,128)(2,1)} %bitcast.244), calls=%async_computation.4 | async-start | bytes 2097152 | tf_op jit(solution)/shard_map/all_to_all | solution.py:612
  856.0 41.0 %all-to-all-start.6 = ((bf16[4,64,2048]{2,1,0:T(8,128)(2,1)}), bf16[4,64,2048]{2,1,0:T(8,128)(2,1)S(1)}, u32[]{:S(2)}, u32[]{:S(2)}) async-start(bf16[4,64,2048]{2,1,0:T(8,128)(2,1)} %bitcast.245), calls=%async_computation.8 | async-start | bytes 2097152 | tf_op jit(solution)/shard_map/all_to_all | solution.py:612
  897.6 140.9 %copy-start.1 = (bf16[256,2048]{1,0:T(8,128)(2,1)S(1)}, bf16[256,2048]{1,0:T(8,128)(2,1)}, u32[]{:S(2)}) copy-start(bf16[256,2048]{1,0:T(8,128)(2,1)} %param.19) | copy-start | bytes 3145732
  (7 other events, 5.1 us)
Sparse Core Ops, SparseCore 0:
  10.0 57.0 all-gather.2
  122.3 78.3 all-gather.4
  382.8 142.0 reduce-scatter.3
  527.1 145.1 reduce-scatter.5
  674.5 145.1 reduce-scatter.7
  823.2 50.6 all-reduce.8
  876.5 156.0 all-reduce.6

commit v3 on v2

--- a/solution.py
+++ b/solution.py
@@ -15,6 +15,7 @@
 f32 = jnp.float32
 MESH = pl.DeviceIdType.MESH
 DMA = pltpu.SemaphoreType.DMA
+small_cost = pl.CostEstimate(flops=0, transcendentals=0, bytes_accessed=1024)
 
 
 def norm_fwd(values, scales):
@@ -51,13 +52,16 @@
     )
 
 
-def greet(n, me):
+def greet(n, me, replicas=1):
     barrier = pltpu.get_barrier_semaphore()
     for k in range(1, n):
         pl.semaphore_signal(
             barrier, inc=1, device_id=peer(lax.rem(me + k, n)), device_id_type=MESH
         )
-    pl.semaphore_wait(barrier, n - 1)
+    for k in range(1, replicas):
+        other = lax.rem(lax.axis_index("dp") + k, replicas)
+        pl.semaphore_signal(barrier, inc=1, device_id={"dp": other}, device_id_type=MESH)
+    pl.semaphore_wait(barrier, n + replicas - 2)
 
 
 def quad_places(me):
@@ -87,45 +91,195 @@
     )
 
 
-def small_kernel(n, *refs):
-    ins, outs, (send_sem, recv_sem) = refs[: len(refs) // 2 - 1], refs[len(refs) // 2 - 1 : -2], refs[-2:]
+def deal_copies(replicas, src, dst, own_sem, send_sem, recv_sem):
+    here = lax.axis_index("dp")
+    rows = src.shape[1]
+    mine = pl.ds(here * rows, rows)
+    own = pltpu.make_async_copy(src.at[here], dst.at[mine], own_sem)
+    away = []
+    for k in range(1, replicas):
+        to = lax.rem(here + k, replicas)
+        away.append(
+            pltpu.make_async_remote_copy(
+                src_ref=src.at[to],
+                dst_ref=dst.at[mine],
+                send_sem=send_sem.at[k],
+                recv_sem=recv_sem.at[k],
+                device_id={"dp": to},
+                device_id_type=MESH,
+            )
+        )
+    return own, away
+
+
+def front_kernel(
+    n,
+    replicas,
+    small,
+    ints,
+    blocks,
+    wq,
+    wk,
+    wv,
+    small_all,
+    ints_all,
+    seq,
+    w_all,
+    small_send,
+    small_recv,
+    own_sem,
+    deal_send,
+    deal_recv,
+    w_own,
+    w_send,
+    w_recv,
+):
     me = lax.axis_index("expert")
-    for src, out in zip(ins, outs):
-        out[me] = src[...]
-    greet(n, me)
+    wide = wq.shape[1] // n
+    small_all[me] = small[...]
+    ints_all[me] = ints[...]
+    own, away = deal_copies(replicas, blocks, seq, own_sem, deal_send, deal_recv)
+    own.start()
+
+    def columns(weight, index):
+        return weight.at[:, pl.ds(pl.multiple_of(index * wide, wide), wide)]
+
+    kept = []
+    for i, weight in enumerate((wq, wk, wv)):
+        copy = pltpu.make_async_copy(
+            columns(weight, me), w_all.at[me, :, pl.ds(i * wide, wide)], w_own.at[i]
+        )
+        copy.start()
+        kept.append(copy)
+    greet(n, me, replicas)
+    copies = []
+
+    def go(copy):
+        copy.start()
+        copies.append(copy)
+
+    for k in range(1, n):
+        to = lax.rem(me + k, n)
+        go(remote(small, small_all.at[me], small_send.at[0, k], small_recv.at[0, k], to))
+        go(remote(ints, ints_all.at[me], small_send.at[1, k], small_recv.at[1, k], to))
+    for copy in away:
+        go(copy)
+    for k in range(1, n):
+        to = lax.rem(me + k, n)
+        for i, weight in enumerate((wq, wk, wv)):
+            go(
+                remote(
+                    columns(weight, to),
+                    w_all.at[me, :, pl.ds(i * wide, wide)],
+                    w_send.at[i, k],
+                    w_recv.at[i, k],
+                    to,
+                )
+            )
+    for copy in copies:
+        copy.wait()
+    own.wait()
+    for copy in kept:
+        copy.wait()
+
+
+def front(n, replicas, collective_id, small, ints, blocks, wq, wk, wv):
+    vmem = pl.BlockSpec(memory_space=pltpu.VMEM)
+    away = pl.BlockSpec(memory_space=pl.ANY)
+    rows, width = wq.shape
+    return pl.pallas_call(
+        functools.partial(front_kernel, n, replicas),
+        out_shape=[
+            jax.ShapeDtypeStruct((n,) + small.shape, small.dtype),
+            jax.ShapeDtypeStruct((n,) + ints.shape, ints.dtype),
+            jax.ShapeDtypeStruct((replicas * blocks.shape[1], width), bf16),
+            jax.ShapeDtypeStruct((n, rows, 3 * (width // n)), bf16),
+        ],
+        in_specs=[vmem, vmem, away, away, away, away],
+        out_specs=[vmem, vmem, away, away],
+        scratch_shapes=[
+            DMA((2, n)),
+            DMA((2, n)),
+            DMA,
+            DMA((replicas,)),
+            DMA((replicas,)),
+            DMA((3,)),
+            DMA((3, n)),
+            DMA((3, n)),
+        ],
+        compiler_params=pltpu.CompilerParams(collective_id=collective_id, has_side_effects=True),
+        cost_estimate=small_cost,
+        name="front",
+    )(small, ints, blocks, wq, wk, wv)
+
+
+def small_sum_kernel(n, replicas, x_ref, o_ref, got, total, send_sem, recv_sem, over_send, over_recv):
+    me = lax.axis_index("expert")
+    here = lax.axis_index("dp")
+    greet(n, me, replicas)
     copies = []
     for k in range(1, n):
-        for i, (src, out) in enumerate(zip(ins, outs)):
-            copy = remote(
-                src, out.at[me], send_sem.at[i, k], recv_sem.at[i, k], lax.rem(me + k, n)
-            )
-            copy.start()
-            copies.append(copy)
+        to = lax.rem(me + k, n)
+        copy = remote(x_ref.at[to], got.at[me], send_sem.at[k], recv_sem.at[k], to)
+        copy.start()
+        copies.append(copy)
+    got[me] = x_ref[me]
     for copy in copies:
         copy.wait()
-
-
-def gather_small(n, collective_id, *values):
+    value = got[0]
+    for k in range(1, n):
+        value = value + got[k]
+    total[here] = value
+    copies = []
+    for k in range(1, replicas):
+        copy = pltpu.make_async_remote_copy(
+            src_ref=total.at[here],
+            dst_ref=total.at[here],
+            send_sem=over_send.at[k],
+            recv_sem=over_recv.at[k],
+            device_id={"dp": lax.rem(here + k, replicas)},
+            device_id_type=MESH,
+        )
+        copy.start()
+        copies.append(copy)
+    for copy in copies:
+        copy.wait()
+    value = total[0]
+    for k in range(1, replicas):
+        value = value + total[k]
+    o_ref[...] = value
+
+
+def small_sum(x, replicas, collective_id):
+    n = x.shape[0]
+    shape = x.shape[1:]
     vmem = pl.BlockSpec(memory_space=pltpu.VMEM)
     return pl.pallas_call(
-        functools.partial(small_kernel, n),
-        out_shape=[jax.ShapeDtypeStruct((n,) + v.shape, v.dtype) for v in values],
-        in_specs=[vmem] * len(values),
-        out_specs=[vmem] * len(values),
-        scratch_shapes=[DMA((len(values), n)), DMA((len(values), n))],
+        functools.partial(small_sum_kernel, n, replicas),
+        out_shape=jax.ShapeDtypeStruct(shape, f32),
+        in_specs=[vmem],
+        out_specs=vmem,
+        scratch_shapes=[
+            pltpu.VMEM(x.shape, f32),
+            pltpu.VMEM((replicas,) + shape, f32),
+            DMA((n,)),
+            DMA((n,)),
+            DMA((replicas,)),
+            DMA((replicas,)),
+        ],
         compiler_params=pltpu.CompilerParams(collective_id=collective_id, has_side_effects=True),
-        name="gather_small",
-    )(*values)
-
-
-def quad_gather_kernel(parts, x_ref, o_ref, own_sem, send_sem, recv_sem, pass_sem, pair_send, pair_recv):
+        name="small_sum",
+    )(x)
+
+
+def quad_gather_kernel(parts, meet, x_ref, o_ref, own_sem, send_sem, recv_sem, pass_sem, pair_send, pair_recv):
     me = lax.axis_index("expert")
     same, other = quad_places(me)
     step = x_ref.shape[0] // parts
     half = parts // 2
     own = pltpu.make_async_copy(x_ref, o_ref.at[me], own_sem)
     own.start()
-    greet(8, me)
+    meet(me)
     started = []
 
     def go(copy):
@@ -165,12 +319,12 @@
     own.wait()
 
 
-def any_gather_kernel(n, x_ref, o_ref, own_sem, send_sem, recv_sem, pair_send, pair_recv):
+def any_gather_kernel(n, meet, x_ref, o_ref, own_sem, send_sem, recv_sem, pair_send, pair_recv):
     me = lax.axis_index("expert")
     same, other, same_from, other_from = any_places(n, me)
     own = pltpu.make_async_copy(x_ref, o_ref.at[me], own_sem)
     own.start()
-    greet(n, me)
+    meet(me)
     started = []
     for k in range(n // 2):
         if k:
@@ -193,24 +347,62 @@
     own.wait()
 
 
-def gather_rows(x, n, collective_id, parts=4):
+def gather_plan(n, parts):
     chips = n // 2
     if n == 8:
-        kernel = functools.partial(quad_gather_kernel, parts)
         sems = [DMA, DMA((4, parts)), DMA((4, parts)), DMA((parts,)), DMA((4, parts)), DMA((4, parts))]
-    else:
-        kernel = functools.partial(any_gather_kernel, n)
-        sems = [DMA, DMA((chips,)), DMA((chips,)), DMA((chips,)), DMA((chips,))]
+        return functools.partial(quad_gather_kernel, parts), sems
+    sems = [DMA, DMA((chips,)), DMA((chips,)), DMA((chips,)), DMA((chips,))]
+    return functools.partial(any_gather_kernel, n), sems
+
+
+def gather_only(n, kernel, *refs):
+    kernel(functools.partial(greet, n), *refs)
+
+
+def gather_and_deal(n, replicas, kernel, x_ref, blocks, o_ref, seq, own_sem, deal_send, deal_recv, *sems):
+    own, away = deal_copies(replicas, blocks, seq, own_sem, deal_send, deal_recv)
+
+    def meet(me):
+        own.start()
+        greet(n, me, replicas)
+        for copy in away:
+            copy.start()
+
+    kernel(meet, x_ref, o_ref, *sems)
+    for copy in away:
+        copy.wait()
+    own.wait()
+
+
+def gather_rows(x, n, collective_id, parts=4, blocks=None):
+    kernel, sems = gather_plan(n, parts)
+    params = pltpu.CompilerParams(collective_id=collective_id, has_side_effects=True)
+    away = pl.BlockSpec(memory_space=pl.ANY)
+    shape = jax.ShapeDtypeStruct((n,) + x.shape, x.dtype)
+    name = f"gather_rows_{collective_id}"
+    if blocks is None:
+        return pl.pallas_call(
+            functools.partial(gather_only, n, kernel),
+            out_shape=shape,
+            in_specs=[away],
+            out_specs=away,
+            scratch_shapes=sems,
+            compiler_params=params,
+            cost_estimate=small_cost,
+            name=name,
+        )(x)
+    replicas = blocks.shape[0]
     return pl.pallas_call(
-        kernel,
-        out_shape=jax.ShapeDtypeStruct((n,) + x.shape, x.dtype),
-        in_specs=[pl.BlockSpec(memory_space=pl.ANY)],
-        out_specs=pl.BlockSpec(memory_space=pl.ANY),
-        scratch_shapes=sems,
-        compiler_params=pltpu.CompilerParams(collective_id=collective_id, has_side_effects=True),
-        cost_estimate=pl.CostEstimate(flops=0, transcendentals=0, bytes_accessed=n * x.size * 16),
-        name=f"gather_rows_{collective_id}",
-    )(x)
+        functools.partial(gather_and_deal, n, replicas, kernel),
+        out_shape=[shape, jax.ShapeDtypeStruct((replicas * blocks.shape[1], blocks.shape[2]), bf16)],
+        in_specs=[away, away],
+        out_specs=[away, away],
+        scratch_shapes=[DMA, DMA((replicas,)), DMA((replicas,))] + sems,
+        compiler_params=params,
+        cost_estimate=small_cost,
+        name=name,
+    )(x, blocks)
 
 
 def add_rows(total, first, rows, chunk, *terms):
@@ -223,8 +415,50 @@
         total[s] = value.astype(total.dtype)
 
 
+class Riders:
+    def __init__(self, n, replicas, gates, stats, gates_out, stats_out, got, sems):
+        self.n, self.replicas = n, replicas
+        self.refs = (gates, stats, gates_out, stats_out, got)
+        self.sems = sems
+
+    def start(self, me):
+        gates, stats, gates_out, _, got = self.refs
+        here = lax.axis_index("dp")
+        gates_out[me] = gates[me]
+        got[here] = stats[...]
+        greet(self.n, me, self.replicas)
+        self.copies = []
+        for k in range(1, self.n):
+            to = lax.rem(me + k, self.n)
+            self.copies.append(
+                remote(gates.at[to], gates_out.at[me], self.sems[0].at[k], self.sems[1].at[k], to)
+            )
+        for k in range(1, self.replicas):
+            self.copies.append(
+                pltpu.make_async_remote_copy(
+                    src_ref=stats,
+                    dst_ref=got.at[here],
+                    send_sem=self.sems[2].at[k],
+                    recv_sem=self.sems[3].at[k],
+                    device_id={"dp": lax.rem(here + k, self.replicas)},
+                    device_id_type=MESH,
+                )
+            )
+        for copy in self.copies:
+            copy.start()
+
+    def finish(self):
+        _, _, _, stats_out, got = self.refs
+        for copy in self.copies:
+            copy.wait()
+        value = got[0]
+        for k in range(1, self.replicas):
+            value = value + got[k]
+        stats_out[...] = value
+
+
 def quad_scatter_kernel(
-    parts, p_ref, o_ref, mine, theirs, transit, got, load_sem, pair_send, pair_recv, over_send, over_recv, send_sem, recv_sem
+    parts, meet, p_ref, o_ref, mine, theirs, transit, got, load_sem, pair_send, pair_recv, over_send, over_recv, send_sem, recv_sem
 ):
     me = lax.axis_index("expert")
     same, other = quad_places(me)
@@ -244,7 +478,7 @@
                 p_ref.at[same[k], piece(p)], mine.at[k, piece(p)], load_sem.at[k, p]
             )
             loads[k, p].start()
-    greet(8, me)
+    meet(me)
     started = []
 
     def go(copy):
@@ -306,7 +540,7 @@
         copy.wait_send()
 
 
-def any_scatter_kernel(n, p_ref, o_ref, mine, theirs, got, load_sem, pair_send, pair_recv, send_sem, recv_sem):
+def any_scatter_kernel(n, meet, p_ref, o_ref, mine, theirs, got, load_sem, pair_send, pair_recv, send_sem, recv_sem):
     me = lax.axis_index("expert")
     same, other, _, _ = any_places(n, me)
     rows = p_ref.shape[1]
@@ -315,7 +549,7 @@
     for k in order:
         loads[k] = pltpu.make_async_copy(p_ref.at[same[k]], mine.at[k], load_sem.at[k])
         loads[k].start()
-    greet(n, me)
+    meet(me)
     started = []
     for k in order:
         copy = remote(p_ref.at[other[k]], theirs.at[k], pair_send.at[k], pair_recv.at[k], other[0])
@@ -336,7 +570,17 @@
         copy.wait_send()
 
 
-def scatter_sum(x, n, collective_id, parts=4):
+def scatter_only(n, kernel, *refs):
+    kernel(functools.partial(greet, n), *refs)
+
+
+def scatter_and_ride(n, replicas, kernel, p_ref, gates, stats, o_ref, gates_out, stats_out, got, *rest):
+    riders = Riders(n, replicas, gates, stats, gates_out, stats_out, got, rest[:4])
+    kernel(riders.start, p_ref, o_ref, *rest[4:])
+    riders.finish()
+
+
+def scatter_sum(x, n, collective_id, parts=4, replicas=1, riders=None):
     chips = n // 2
     shape = x.shape[1:]
     blocks = pltpu.VMEM((chips,) + shape, bf16)
@@ -347,18 +591,45 @@
     else:
         kernel = functools.partial(any_scatter_kernel, n)
         scratch = [blocks] * 3 + [DMA((chips,))] * 5
-    return pl.pallas_call(
-        kernel,
-        out_shape=jax.ShapeDtypeStruct(shape, f32),
-        in_specs=[pl.BlockSpec(memory_space=pl.ANY)],
-        out_specs=pl.BlockSpec(memory_space=pltpu.VMEM),
-        scratch_shapes=scratch,
+    vmem = pl.BlockSpec(memory_space=pltpu.VMEM)
+    away = pl.BlockSpec(memory_space=pl.ANY)
+    common = dict(
         compiler_params=pltpu.CompilerParams(
             collective_id=collective_id, has_side_effects=True, vmem_limit_bytes=(3 * chips + 12) << 20
         ),
-        cost_estimate=pl.CostEstimate(flops=0, transcendentals=0, bytes_accessed=x.size * 16),
+        cost_estimate=small_cost,
         name=f"scatter_sum_{collective_id}",
-    )(x)
+    )
+    out = jax.ShapeDtypeStruct(shape, f32)
+    if riders is None:
+        return pl.pallas_call(
+            functools.partial(scatter_only, n, kernel),
+            out_shape=out,
+            in_specs=[away],
+            out_specs=vmem,
+            scratch_shapes=scratch,
+            **common,
+        )(x)
+    gates, stats = riders
+    return pl.pallas_call(
+        functools.partial(scatter_and_ride, n, replicas, kernel),
+        out_shape=[
+            out,
+            jax.ShapeDtypeStruct(gates.shape, f32),
+            jax.ShapeDtypeStruct(stats.shape, f32),
+        ],
+        in_specs=[away, vmem, vmem],
+        out_specs=[vmem, vmem, vmem],
+        scratch_shapes=[
+            pltpu.VMEM((replicas,) + stats.shape, f32),
+            DMA((n,)),
+            DMA((n,)),
+            DMA((replicas,)),
+            DMA((replicas,)),
+        ]
+        + scratch,
+        **common,
+    )(x, gates, stats)
 
 
 def dot(left, right, left_dim=1, right_dim=0):
@@ -422,11 +693,7 @@
             out_specs=pl.BlockSpec((1, rows, wide), lambda s, lens: (s, 0, 0)),
         ),
         compiler_params=pltpu.CompilerParams(vmem_limit_bytes=32 << 20),
-        cost_estimate=pl.CostEstimate(
-            flops=2 * seqs * rows * (width * 3 * wide + 2 * rows * wide),
-            transcendentals=seqs * rows * rows * wide // head_dim,
-            bytes_accessed=2 * (x.size + w_qkv.size),
-        ),
+        cost_estimate=small_cost,
         name="attend",
     )(lengths, x, w_qkv, query_g[None, :], key_g[None, :], cosine, signed_sine)
 
@@ -547,13 +814,155 @@
             ],
         ),
         compiler_params=pltpu.CompilerParams(vmem_limit_bytes=48 << 20),
-        cost_estimate=pl.CostEstimate(
-            flops=2 * seqs * rows * (width * 11 * wide + 5 * rows * wide),
-            transcendentals=seqs * rows * rows * wide // head_dim,
-            bytes_accessed=2 * (3 * x.size + w_qkv.size * 2),
-        ),
+        cost_estimate=small_cost,
         name="attend_back",
     )(lengths, x, g, mixed, w_qkv, w_out, query_g[None, :], key_g[None, :], cosine, signed_sine)
+
+
+def slot_matrix(slot_row, capacity):
+    return lax.broadcasted_iota(jnp.int32, (capacity, slot_row.shape[1]), 0) == slot_row
+
+
+def stack(pieces):
+    return pieces[0] if len(pieces) == 1 else jnp.concatenate(pieces, axis=0)
+
+
+def expert_in_kernel(capacity, x_ref, cot_ref, slot_ref, gate_ref, wg_ref, wu_ref, in_ref, gr_ref, act_ref, g_ref, u_ref):
+    for j in range(wg_ref.shape[0]):
+        rows, grads = [], []
+        for s in range(x_ref.shape[0]):
+            chosen = slot_matrix(slot_ref[j, s], capacity)
+            one_hot = jnp.where(chosen, 1.0, 0.0).astype(bf16)
+            weight = jnp.sum(jnp.where(chosen, gate_ref[j, s], 0.0), axis=1, keepdims=True)
+            rows.append(dot(one_hot, x_ref[s]))
+            grads.append(weight * dot(one_hot, cot_ref[s]))
+        taken = stack(rows).astype(bf16)
+        in_ref[j] = taken
+        gr_ref[j] = stack(grads).astype(bf16)
+        gate_in = dot(taken, wg_ref[j])
+        up_in = dot(taken, wu_ref[j])
+        g_ref[j] = gate_in
+        u_ref[j] = up_in
+        act_ref[j] = (gate_in * jax.nn.sigmoid(gate_in) * up_in).astype(bf16)
+
+
+def step_rows(groups):
+    return 2 if groups % 2 == 0 else 1
+
+
+def expert_forward(mlp_all, cot_all, slot_of, gates, w_gate, w_up, capacity):
+    groups, tok_rows, width = mlp_all.shape
+    local, _, ff = w_gate.shape
+    seqs = step_rows(groups)
+    slots = seqs * capacity
+    tok = pl.BlockSpec((seqs, tok_rows, width), lambda i: (i, 0, 0))
+    route = pl.BlockSpec((local, seqs, 1, tok_rows), lambda i: (0, i, 0, 0))
+    weight = pl.BlockSpec((local, width, ff), lambda i: (0, 0, 0), pipeline_mode=pl.Buffered(1))
+    wide = pl.BlockSpec((local, slots, width), lambda i: (0, i, 0))
+    slim = pl.BlockSpec((local, slots, ff), lambda i: (0, i, 0))
+    total = groups * capacity
+    return pl.pallas_call(
+        functools.partial(expert_in_kernel, capacity),
+        out_shape=[
+            jax.ShapeDtypeStruct((local, total, width), bf16),
+            jax.ShapeDtypeStruct((local, total, width), bf16),
+            jax.ShapeDtypeStruct((local, total, ff), bf16),
+            jax.ShapeDtypeStruct((local, total, ff), f32),
+            jax.ShapeDtypeStruct((local, total, ff), f32),
+        ],
+        grid=(groups // seqs,),
+        in_specs=[tok, tok, route, route, weight, weight],
+        out_specs=[wide, wide, slim, slim, slim],
+        compiler_params=pltpu.CompilerParams(vmem_limit_bytes=60 << 20),
+        cost_estimate=small_cost,
+        name="expert_forward",
+    )(mlp_all, cot_all, slot_of[:, :, None, :], gates[:, :, None, :], w_gate, w_up)
+
+
+def expert_out_kernel(capacity, act_ref, cot_ref, slot_ref, gate_ref, wd_ref, sum_ref, gg_ref):
+    parts = [None] * cot_ref.shape[0]
+    for j in range(wd_ref.shape[0]):
+        out = dot(act_ref[j], wd_ref[j])
+        for s in range(cot_ref.shape[0]):
+            one_hot = jnp.where(slot_matrix(slot_ref[j, s], capacity), 1.0, 0.0).astype(bf16)
+            here = dot(one_hot, out[s * capacity : (s + 1) * capacity].astype(bf16), 0, 0)
+            gg_ref[j, s] = jnp.sum(here * cot_ref[s].astype(f32), axis=1, keepdims=True)
+            term = gate_ref[j, s] * here
+            parts[s] = term if j == 0 else parts[s] + term
+    for s in range(cot_ref.shape[0]):
+        sum_ref[s] = parts[s].astype(bf16)
+
+
+def expert_combine(act, cot_all, slot_of, gates, w_down, capacity):
+    groups, tok_rows, width = cot_all.shape
+    local, ff, _ = w_down.shape
+    seqs = step_rows(groups)
+    tok = pl.BlockSpec((seqs, tok_rows, width), lambda i: (i, 0, 0))
+    route = pl.BlockSpec((local, seqs, 1, tok_rows), lambda i: (0, i, 0, 0))
+    column = pl.BlockSpec((local, seqs, tok_rows, 1), lambda i: (0, i, 0, 0))
+    weight = pl.BlockSpec((local, ff, width), lambda i: (0, 0, 0), pipeline_mode=pl.Buffered(1))
+    slim = pl.BlockSpec((local, seqs * capacity, ff), lambda i: (0, i, 0))
+    return pl.pallas_call(
+        functools.partial(expert_out_kernel, capacity),
+        out_shape=[
+            jax.ShapeDtypeStruct((groups, tok_rows, width), bf16),
+            jax.ShapeDtypeStruct((local, groups, tok_rows, 1), f32),
+        ],
+        grid=(groups // seqs,),
+        in_specs=[slim, tok, route, column, weight],
+        out_specs=[tok, column],
+        compiler_params=pltpu.CompilerParams(vmem_limit_bytes=60 << 20),
+        cost_estimate=small_cost,
+        name="expert_combine",
+    )(act, cot_all, slot_of[:, :, None, :], gates[:, :, :, None], w_down)
+
+
+def expert_back_kernel(capacity, gr_ref, g_ref, u_ref, slot_ref, wg_ref, wu_ref, wd_ref, gg_ref, gu_ref, part_ref):
+    seqs = part_ref.shape[0]
+    parts = [None] * seqs
+    for j in range(wd_ref.shape[0]):
+        grad_act = dot(gr_ref[j], wd_ref[j], 1, 1)
+        gate_in = g_ref[j]
+        sigma = jax.nn.sigmoid(gate_in)
+        grad_up = (grad_act * (gate_in * sigma)).astype(bf16)
+        grad_gate = (grad_act * u_ref[j] * sigma * (1.0 + gate_in * (1.0 - sigma))).astype(bf16)
+        gg_ref[j] = grad_gate
+        gu_ref[j] = grad_up
+        rows = dot(grad_gate, wg_ref[j], 1, 1) + dot(grad_up, wu_ref[j], 1, 1)
+        for s in range(seqs):
+            one_hot = jnp.where(slot_matrix(slot_ref[j, s], capacity), 1.0, 0.0).astype(bf16)
+            term = dot(one_hot, rows[s * capacity : (s + 1) * capacity].astype(bf16), 0, 0)
+            parts[s] = term if j == 0 else parts[s] + term
+    for s in range(seqs):
+        part_ref[s] = parts[s].astype(bf16)
+
+
+def expert_back(grad_recv, gate_in, up_in, slot_of, w_gate, w_up, w_down, groups, tok_rows, capacity):
+    local, width, ff = w_gate.shape
+    seqs = step_rows(groups)
+    slots = seqs * capacity
+    total = groups * capacity
+    tok = pl.BlockSpec((seqs, tok_rows, width), lambda i: (i, 0, 0))
+    route = pl.BlockSpec((local, seqs, 1, tok_rows), lambda i: (0, i, 0, 0))
+    once = pl.Buffered(1)
+    weight = pl.BlockSpec((local, width, ff), lambda i: (0, 0, 0), pipeline_mode=once)
+    down = pl.BlockSpec((local, ff, width), lambda i: (0, 0, 0), pipeline_mode=once)
+    wide = pl.BlockSpec((local, slots, width), lambda i: (0, i, 0))
+    slim = pl.BlockSpec((local, slots, ff), lambda i: (0, i, 0))
+    return pl.pallas_call(
+        functools.partial(expert_back_kernel, capacity),
+        out_shape=[
+            jax.ShapeDtypeStruct((local, total, ff), bf16),
+            jax.ShapeDtypeStruct((local, total, ff), bf16),
+            jax.ShapeDtypeStruct((groups, tok_rows, width), bf16),
+        ],
+        grid=(groups // seqs,),
+        in_specs=[wide, slim, slim, route, weight, weight, down],
+        out_specs=[slim, slim, tok],
+        compiler_params=pltpu.CompilerParams(vmem_limit_bytes=63 << 20),
+        cost_estimate=small_cost,
+        name="expert_back",
+    )(grad_recv, gate_in, up_in, slot_of[:, :, None, :], w_gate, w_up, w_down)
 
 
 def pad_rows(flat, tile):
@@ -602,11 +1011,8 @@
     matched = (order_row[:, None] == dp_ids[None, :]).astype(jnp.int32)
     inverse_order = jnp.sum(matched * dp_ids[:, None], axis=0)
 
-    def deal(values):
-        blocks = values.reshape(replicas, block_rows, width)[inverse_order]
-        return lax.all_to_all(blocks, "dp", split_axis=0, concat_axis=0, tiled=True).reshape(
-            tok_rows, width
-        )
+    def blocks_to_deal(values):
+        return values.reshape(replicas, block_rows, width)[inverse_order]
 
     def undeal(values):
         back = lax.all_to_all(
@@ -614,15 +1020,23 @@
         )
         return back[order_row].reshape(tok_rows, width)
 
-    seq_tokens = deal(tokens)
-    seq_cot = deal(cotangent)
-
     small = jnp.concatenate(
         [w_router.reshape(-1), attn_gain, mlp_gain, query_gain, key_gain]
     )
     ints = jnp.concatenate([routes.reshape(-1), jnp.broadcast_to(lengths, (top_k,))])
-    small_all, ints_all = gather_small(groups, 0, pad_rows(small, 16), pad_rows(ints, 8))
+    small_all, ints_all, seq_tokens, w_qkv = front(
+        groups,
+        replicas,
+        0,
+        pad_rows(small, 16),
+        pad_rows(ints, 8),
+        blocks_to_deal(tokens),
+        w_query,
+        w_key,
+        w_value,
+    )
     small_all, ints_all = small_all.reshape(groups, -1), ints_all.reshape(groups, -1)
+    w_qkv = w_qkv.reshape(width, -1)
     n_router = shard_rows * experts
     cuts = [0, n_router]
     for gain in (attn_gain, mlp_gain, query_gain, key_gain):
@@ -640,19 +1054,12 @@
     live_all = (positions[None, :] < lengths_all[:, None]).astype(f32)
     live_rows = (positions < lengths[0]).astype(f32)
 
-    def columns(weight):
-        return weight.reshape(shard_rows, groups, local_width).transpose(1, 0, 2)
-
-    w_send = jnp.concatenate([columns(w_query), columns(w_key), columns(w_value)], axis=2)
-    w_qkv = lax.all_to_all(w_send, "expert", split_axis=0, concat_axis=0, tiled=True).reshape(
-        width, 3 * local_width
-    )
     wo_full = lax.all_gather(w_out, "expert", axis=0, tiled=True)
 
     inputs = seq_tokens.astype(f32)
     normed, inv_first = norm_fwd(inputs, attn_g)
     attn_in = normed.astype(bf16)
-    attn_all = gather_rows(attn_in, groups, 1)
+    attn_all, seq_cot = gather_rows(attn_in, groups, 1, blocks=blocks_to_deal(cotangent))
     grad_output = seq_cot.astype(f32) * live_rows[:, None]
     cot_all = lax.all_gather(grad_output.astype(bf16), "expert", axis=0, tiled=False)
 
@@ -675,10 +1082,7 @@
     counts = jnp.sum(picked * live_all[:, :, None], axis=(0, 1))
     prob_sums = jnp.sum(router * live_all[:, :, None], axis=(0, 1))
     live_count = jnp.sum(live_all)[None]
-    sums = lax.psum(jnp.concatenate([counts, prob_sums, live_count]), "dp")
-    counts, prob_sums, live_count = sums[:experts], sums[experts : 2 * experts], sums[2 * experts :]
-    fraction = counts / (live_count * top_k)
-    balance_loss = balance_coef * (experts * jnp.sum(fraction * prob_sums / total_slots))
+    stats = pad_rows(jnp.concatenate([counts, prob_sums, live_count]), 8)
 
     first = me * local_experts
     own_picked = lax.dynamic_slice_in_dim(picked, first, local_experts, 2)
@@ -688,64 +1092,37 @@
     own_picked = own_picked.transpose(2, 0, 1)
     own_gates = own_gates.transpose(2, 0, 1)
     slot_of = jnp.where(own_picked > 0.5, rank.astype(jnp.int32), -1)
-    slot_ids = jnp.arange(capacity, dtype=jnp.int32)
-    is_slot = slot_of[:, :, None, :] == slot_ids[None, None, :, None]
-    one_hot = is_slot.astype(bf16)
-    slot_gate = jnp.sum(jnp.where(is_slot, own_gates[:, :, None, :], 0.0), axis=-1)
-    n_slots = groups * capacity
-
-    expert_in = einf("jsct,std->jscd", one_hot, mlp_all).astype(bf16).reshape(
-        local_experts, n_slots, width
-    )
-    gate_in = einf("jrd,jdf->jrf", expert_in, w_gate)
-    up_in = einf("jrd,jdf->jrf", expert_in, w_up)
-    sigmoid_gate = jax.nn.sigmoid(gate_in)
-    activated = gate_in * sigmoid_gate
-    act_low = (activated * up_in).astype(bf16)
-    cot_slots = einf("jsct,std->jscd", one_hot, cot_all).astype(bf16)
-    grad_recv = (
-        (slot_gate[..., None] * cot_slots.astype(f32)).astype(bf16).reshape(local_experts, n_slots, width)
+    expert_in, grad_recv, act_low, gate_in, up_in = expert_forward(
+        mlp_all, cot_all, slot_of, own_gates, w_gate, w_up, capacity
     )
     grad_down_w = einf("jrf,jrd->jfd", act_low, grad_recv)
-    act_low, grad_recv, grad_down_w = lax.optimization_barrier((act_low, grad_recv, grad_down_w))
-    total_down = lax.psum_scatter(
-        grad_down_w.astype(bf16), "dp", scatter_dimension=1, tiled=True
-    ).astype(f32)
-
-    expert_out = einf("jrf,jfd->jrd", act_low, w_down).astype(bf16).reshape(
-        local_experts, groups, capacity, width
-    )
-    grad_gate_slot = jnp.sum(cot_slots.astype(f32) * expert_out.astype(f32), axis=-1)
-    own_grad_gates = jnp.sum(jnp.where(is_slot, grad_gate_slot[..., None], 0.0), axis=2)
-    weighted = (slot_gate[..., None] * expert_out.astype(f32)).astype(bf16)
-    sum_part = einf("jsct,jscd->std", one_hot, weighted).astype(bf16)
-
-    grad_act = einf("jrd,jfd->jrf", grad_recv, w_down)
-    grad_up_in = (grad_act * activated).astype(bf16)
-    grad_gate_in = (
-        grad_act * up_in * sigmoid_gate * (1.0 + gate_in * (1.0 - sigmoid_gate))
-    ).astype(bf16)
+    act_low, grad_recv, grad_down_w = lax.optimization_barrier(
+        (act_low, grad_recv, grad_down_w.astype(bf16))
+    )
+    total_down = lax.psum_scatter(grad_down_w, "dp", scatter_dimension=1, tiled=True).astype(f32)
+    grad_gate_in, grad_up_in, grad_part = expert_back(
+        grad_recv, gate_in, up_in, slot_of, w_gate, w_up, w_down, groups, tok_rows, capacity
+    )
     grad_gate_w = einf("jrd,jrf->jdf", expert_in, grad_gate_in)
     grad_up_w = einf("jrd,jrf->jdf", expert_in, grad_up_in)
-    grad_gate_in, grad_up_in, grad_gate_w, grad_up_w = lax.optimization_barrier(
-        (grad_gate_in, grad_up_in, grad_gate_w.astype(bf16), grad_up_w.astype(bf16))
-    )
-    grad_rows = (
-        (einf("jrf,jdf->jrd", grad_gate_in, w_gate) + einf("jrf,jdf->jrd", grad_up_in, w_up))
-        .astype(bf16)
-        .reshape(local_experts, groups, capacity, width)
-    )
-    grad_part = einf("jsct,jscd->std", one_hot, grad_rows).astype(bf16)
-    grad_mlp_in = scatter_sum(grad_part, groups, 3)
-
+    grad_part, act_low, grad_gate_w, grad_up_w = lax.optimization_barrier(
+        (grad_part, act_low, grad_gate_w.astype(bf16), grad_up_w.astype(bf16))
+    )
     total_gate, total_up = (
-        lax.psum_scatter(value.astype(bf16), "dp", scatter_dimension=1, tiled=True).astype(f32)
+        lax.psum_scatter(value, "dp", scatter_dimension=1, tiled=True).astype(f32)
         for value in (grad_gate_w, grad_up_w)
     )
-
-    gate_back = lax.all_to_all(
-        own_grad_gates.transpose(1, 0, 2), "expert", split_axis=0, concat_axis=0, tiled=True
-    )
+    sum_part, own_grad_gates = expert_combine(act_low, cot_all, slot_of, own_gates, w_down, capacity)
+    gate_rows = own_grad_gates.transpose(1, 0, 2, 3).reshape(groups, -1, 128)
+    grad_mlp_in, gate_back, sums = scatter_sum(
+        grad_part, groups, 3, replicas=replicas, riders=(gate_rows, stats)
+    )
+    sums = sums.reshape(-1)
+    counts, prob_sums = sums[:experts], sums[experts : 2 * experts]
+    live_count = sums[2 * experts : 2 * experts + 1]
+    fraction = counts / (live_count * top_k)
+    balance_loss = balance_coef * (experts * jnp.sum(fraction * prob_sums / total_slots))
+
     grad_gates = gate_back.reshape(experts, tok_rows).T
     my_router = lax.dynamic_index_in_dim(router, me, 0, keepdims=False)
     my_picked = lax.dynamic_index_in_dim(picked, me, 0, keepdims=False)
@@ -764,12 +1141,12 @@
     grad_hidden_norm, grad_mlp_g = norm_back(hidden, inv_second, mlp_g, grad_mlp_in, 0)
     grad_hidden = grad_output + grad_hidden_norm
     grad_hidden_low = grad_hidden.astype(bf16)
+    grad_hidden_low, total_down = lax.optimization_barrier((grad_hidden_low, total_down))
     hidden_all = gather_rows(grad_hidden_low, groups, 4)
     grad_attn_part, grad_qkv_w, grad_out_w, grad_gains = attend_back(
         lengths_all, attn_all, hidden_all, mixed, w_qkv, w_out, query_g, key_g, cosine, signed_sine
     )
     grad_query_g, grad_key_g = grad_gains[0], grad_gains[1]
-    grad_attn_part, total_down = lax.optimization_barrier((grad_attn_part, total_down))
     grad_attn_in = scatter_sum(grad_attn_part, groups, 5)
     w_back = lax.all_to_all(
         grad_qkv_w.reshape(groups, shard_rows, 3 * local_width),
@@ -798,17 +1175,18 @@
     grad_input_norm, grad_attn_g = norm_back(inputs, inv_first, attn_g, grad_attn_in, 0)
     grad_input = undeal((grad_hidden + grad_input_norm).astype(bf16)).astype(f32)
 
+    sum_part, grad_input = lax.optimization_barrier((sum_part, grad_input))
     expert_sum = scatter_sum(sum_part, groups, 6)
     output = undeal((live_rows[:, None] * (hidden + expert_sum)).astype(bf16))
 
-    pieces = [grad_router_w.astype(bf16).reshape(groups, n_router)] + [
-        value.astype(bf16).reshape(groups, -1)
-        for value in (grad_attn_g, grad_mlp_g, grad_query_g, grad_key_g)
+    pieces = [grad_router_w.reshape(groups, n_router)] + [
+        value.reshape(groups, -1) for value in (grad_attn_g, grad_mlp_g, grad_query_g, grad_key_g)
     ]
-    part_small = lax.psum_scatter(
-        jnp.concatenate(pieces, axis=1), "expert", scatter_dimension=0, tiled=True
-    )
-    sum_small = lax.psum(part_small.reshape(-1), "dp").astype(f32)
+    pieces = jnp.concatenate(pieces, axis=1)
+    n_small = pieces.shape[1]
+    pad = -n_small % 1024
+    pieces = jnp.pad(pieces, ((0, 0), (0, pad))).reshape(groups, -1, 128)
+    sum_small = small_sum(pieces, replicas, 7).reshape(-1)
     sum_r = sum_small[:n_router].reshape(shard_rows, experts)
     sum_ga, sum_gm, sum_gq, sum_gk = (sum_small[cuts[i] : cuts[i + 1]] for i in range(1, 5))
     return (

time: 1060 us -> 968 us (0.913)
  Pallas kernels: 367 us -> 566 us
  matrix products: 219 us -> 69.3 us
  waiting for transfers between devices: 259 us -> 196 us
  blocking collectives: 28.3 us -> 0 us
  local copies, waits for them, and re-layouts: 69.5 us -> 50.9 us
  other arithmetic: 52.2 us -> 37.8 us
  starting transfers between devices: 33.2 us -> 19.7 us
    pallas_call x7 -> x11, Pallas kernels: 306 us -> 505 us  [the longest x2 109 us: scatter_sum(): pl.pallas_call(functools.partial(scatter_only, n, kernel), out_shape=out,...]
    dot_general x17 -> x8, matrix products: 213 us -> 69.3 us  [einf(): return jnp.einsum(spec, left, right, preferred_element_type=f32)]
    psum x1, waiting for transfers between devices: 133 us -> 33 us  [body(): attn_sum = lax.psum(attn_w, 'dp').astype(f32)]
    reduce_scatter x3, waiting for transfers between devices: 0.02 us -> 98.9 us  [the longest x2 98.9 us: body(): lax.psum_scatter(value, 'dp', scatter_dimension=1, tiled=True).astype(f32)]
    all_to_all x4 -> x0, waiting for transfers between devices: 42.6 us -> none  [the longest x2 42.6 us: deal(): lax.all_to_all(blocks, 'dp', split_axis=0, concat_axis=0, tiled=True)]
    all_to_all x1, waiting for transfers between devices: 35.5 us -> 0.01 us  [body(): lax.all_to_all(grad_qkv_w.reshape(groups, shard_rows, 3 * local_width), '...]
    psum x2 -> x0, blocking collectives: 28.3 us -> none  [the longest x1 19.5 us: body(): sum_small = lax.psum(part_small.reshape(-1), 'dp').astype(f32)]
    convert_element_type x7 -> x0, local copies, waits for them, and re-layouts: 19 us -> none  [the longest x1 9.29 us: body(): einf('jsct,std->jscd', one_hot, mlp_all).astype(bf16)]
  transfers between devices with their start and end apart: 15 -> 10, of which waited for: 7 -> 4; matrix products, arithmetic and copies ran while one was open for 27% -> 12% of each run, Pallas kernels for 35% -> 55%
where the time goes in v3:
time: 968 us; the launch traced here: 959 us
  Pallas kernels  566 us (58%)
  waiting for transfers between devices  196 us (20%)
  matrix products  69.3 us (7%)
  local copies, waits for them, and re-layouts  50.9 us (5%)
  other arithmetic  37.8 us (4%)
  starting transfers between devices  19.7 us (2%)
  between operations  19.2 us (2%)
    pallas_call x2, Pallas kernels, scatter_sum(): pl.pallas_call(functools.partial(scatter_only, n, kernel), out_shape=out,...  109 us
    reduce_scatter x2, waiting for transfers between devices, body(): lax.psum_scatter(value, 'dp', scatter_dimension=1, tiled=True).astype(f32)  98.9 us
    pallas_call x2, Pallas kernels, gather_rows(): pl.pallas_call(functools.partial(gather_only, n, kernel), out_shape=shape...  79.2 us
    dot_general x8, matrix products, einf(): return jnp.einsum(spec, left, right, preferred_element_type=f32)  69.3 us
    pallas_call x1, Pallas kernels, gather_rows(): pl.pallas_call(functools.partial(gather_and_deal, n, replicas, kernel), o...  55.4 us
    pallas_call x1, Pallas kernels, front(): pl.pallas_call(functools.partial(front_kernel, n, replicas), out_shape=[j...  54.5 us
    pallas_call x1, Pallas kernels, small_sum(): pl.pallas_call(functools.partial(small_sum_kernel, n, replicas), out_shap...  54 us
    pallas_call x1, Pallas kernels, expert_back(): pl.pallas_call(functools.partial(expert_back_kernel, capacity), out_shape...  49.9 us
  transfers between devices with their start and end apart: 10, of which 4 were waited for; matrix products, arithmetic and copies ran while one was open for 12% of the time, Pallas kernels for 55%

profile of v3, /device:TPU:0, one launch (start us, length us, event | category | flops | bytes accessed | tf_op | source)
XLA Modules:
  0.0 959.2 jit_solution(18123676013602637135)
XLA Ops:
  7.3 0.7 all-gather.4.cloned.1.call-update
  8.7 0.8 copy.87
  9.6 0.8 copy.86
  11.4 1.6 gather_fusion
  14.3 54.5 %front.1 = (bf16[8,48,128]{2,1,0:T(8,128)(2,1)}, s32[8,24,128]{2,1,0:T(8,128)}, bf16[256,2048]{1,0:T(8,128)(2,1)}, bf16[8,256,768]{2,1,0:T(8,128)(2,1)}) custom-call(bf16[48,128]{1,0:T(8,128)(2,1)} %pad_bitcast_fusion.1.small, s32[24,128]{1,0:T(8,128)} %select_bitcast_fusion.ints, bf16[4,64,2048]{2,1,0:T(8,128)(2,1)} %gather_fusion, bf16[256,2048]{1,0:T(8,128)(2,1)} %wq.1, ...), custom_call_target="tpu_custom_call" | custom-call | bytes 1024 | tf_op jit(solution)/shard_map/front/pallas_call | solution.py:190
  68.9 1.0 copy.144
  69.9 1.6 gather_fusion.1
  71.8 1.3 fusion.2.x_ref
  73.1 55.4 %gather_rows_1.1 = (bf16[8,256,2048]{2,1,0:T(8,128)(2,1)}, bf16[256,2048]{1,0:T(8,128)(2,1)}) custom-call(bf16[256,2048]{1,0:T(8,128)(2,1)} %fusion.2.x_ref, bf16[4,64,2048]{2,1,0:T(8,128)(2,1)} %gather_fusion.1), custom_call_target="tpu_custom_call" | custom-call | bytes 1024 | tf_op jit(solution)/shard_map/gather_rows_1/pallas_call | solution.py:396
  128.6 2.6 fusion.12
  133.0 3.4 copy-done.2
  136.4 16.0 %attend.1.mixed_ref = bf16[8,256,256]{2,1,0:T(8,128)(2,1)S(1)} custom-call(s32[8]{0:T(128)S(1)} %slice_reduce_fusion.lengths_ref, bf16[8,256,2048]{2,1,0:T(8,128)(2,1)S(1)} %copy-done.2, bf16[2048,768]{1,0:T(8,128)(2,1)S(1)} %bitcast.146, f32[1,128]{1,0:T(1,128)S(1)} %reshape.315.qg_ref, f32[1,128]{1,0:T(1,128)S(1)} %reshape.316.kg_ref, ...), custom_call_target="tpu_custom_call" | custom-call | bytes 1024 | tf_op jit(solution)/shard_map/attend/pallas_call | solution.py:679
  152.4 1.0 copy-done.4
  153.3 4.4 all-to-all-start
  159.3 25.0 %all-to-all-done = bf16[8,256,256]{2,1,0:T(8,128)(2,1)} async-done(((bf16[8,256,256]{2,1,0:T(8,128)(2,1)}), bf16[8,256,256]{2,1,0:T(8,128)(2,1)}, u32[]{:S(2)}, u32[]{:S(2)}) %all-to-all-start) | async-done | bytes 1048608 | tf_op jit(solution)/shard_map/all_to_all | solution.py:1068
  184.3 7.5 multiply_reduce_fusion.2
  191.8 2.9 multiply_convert_fusion.1.refs_0_
  194.7 39.6 %gather_rows_2.1.x_ref = bf16[8,256,2048]{2,1,0:T(8,128)(2,1)} custom-call(bf16[256,2048]{1,0:T(8,128)(2,1)} %multiply_convert_fusion.1.refs_0_), custom_call_target="tpu_custom_call" | custom-call | bytes 1024 | tf_op jit(solution)/shard_map/gather_rows_2/pallas_call | solution.py:385
  234.2 5.7 fusion.42
  240.0 0.8 multiply_reduce_fusion.4
  243.7 36.8 %expert_forward.1 = (bf16[2,1152,2048]{2,1,0:T(8,128)(2,1)}, bf16[2,1152,2048]{2,1,0:T(8,128)(2,1)}, bf16[2,1152,1024]{2,1,0:T(8,128)(2,1)}, f32[2,1152,1024]{2,1,0:T(8,128)}, f32[2,1152,1024]{2,1,0:T(8,128)}) custom-call(bf16[8,256,2048]{2,1,0:T(8,128)(2,1)} %gather_rows_2.1.x_ref, bf16[8,256,2048]{2,1,0:T(8,128)(2,1)} %bitcast.149, ...), custom_call_target="tpu_custom_call" | custom-call | bytes 1024 | tf_op jit(solution)/shard_map/expert_forward/pallas_call | solution.py:864
  280.5 17.7 %convolution_convert_fusion.2 = bf16[2,1024,2048]{2,1,0:T(8,128)(2,1)} fusion(bf16[2,1152,1024]{2,1,0:T(8,128)(2,1)} %get-tuple-element.69.act_ref, bf16[2,1152,2048]{2,1,0:T(8,128)(2,1)} %get-tuple-element.61.gr_ref), kind=kOutput, calls=%fused_computation.6 | convolution fusion | flops 9667870720 | bytes 22544384 | tf_op jit(solution)/shard_map/jrf,jrd->jfd/dot_general | solution.py:974
  298.3 49.9 %expert_back.1 = (bf16[2,1152,1024]{2,1,0:T(8,128)(2,1)}, bf16[2,1152,1024]{2,1,0:T(8,128)(2,1)}, bf16[8,256,2048]{2,1,0:T(8,128)(2,1)}) custom-call(bf16[2,1152,2048]{2,1,0:T(8,128)(2,1)} %get-tuple-element.61.gr_ref, f32[2,1152,1024]{2,1,0:T(8,128)} %get-tuple-element.62.g_ref, f32[2,1152,1024]{2,1,0:T(8,128)} %get-tuple-element.63.u_ref, ...), custom_call_target="tpu_custom_call" | custom-call | bytes 1024 | tf_op jit(solution)/shard_map/expert_back/pallas_call | solution.py:952
  348.2 17.4 %convolution_convert_fusion = bf16[2,2048,1024]{2,1,0:T(8,128)(2,1)} fusion(bf16[2,1152,2048]{2,1,0:T(8,128)(2,1)} %get-tuple-element.66, bf16[2,1152,1024]{2,1,0:T(8,128)(2,1)} %get-tuple-element.68), kind=kOutput, calls=%fused_computation.4 | convolution fusion | flops 9667870720 | bytes 22544384 | tf_op jit(solution)/shard_map/jrd,jrf->jdf/dot_general | solution.py:974
  365.6 17.2 %convolution_convert_fusion.1 = bf16[2,2048,1024]{2,1,0:T(8,128)(2,1)} fusion(bf16[2,1152,2048]{2,1,0:T(8,128)(2,1)} %get-tuple-element.66, bf16[2,1152,1024]{2,1,0:T(8,128)(2,1)} %get-tuple-element.67), kind=kOutput, calls=%fused_computation.5 | convolution fusion | flops 9667870720 | bytes 22544384 | tf_op jit(solution)/shard_map/jrd,jrf->jdf/dot_general | solution.py:974
  384.7 2.0 copy.96.gate_ref
  386.7 23.6 %expert_combine.1 = (bf16[8,256,2048]{2,1,0:T(8,128)(2,1)}, f32[2,8,256,1]{3,2,1,0:T(8,128)}) custom-call(bf16[2,1152,1024]{2,1,0:T(8,128)(2,1)} %get-tuple-element.69.act_ref, bf16[8,256,2048]{2,1,0:T(8,128)(2,1)} %bitcast.150, s32[2,8,1,256]{3,2,1,0:T(1,128)} %broadcast_in_dim.12.slot_ref, f32[2,8,256,1]{3,2,1,0:T(8,128)} %copy.96.gate_ref, ...), custom_call_target="tpu_custom_call" | custom-call | bytes 1024 | tf_op jit(solution)/shard_map/expert_combine/pallas_call | solution.py:905
  410.2 2.2 copy.97
  412.5 0.7 fusion.30.stats
  413.2 3.4 copy-done.8
  416.6 42.8 %scatter_sum_3.1 = (f32[256,2048]{1,0:T(8,128)S(1)}, f32[8,4,128]{2,1,0:T(4,128)S(1)}, f32[8,128]{1,0:T(8,128)S(1)}) custom-call(bf16[8,256,2048]{2,1,0:T(8,128)(2,1)S(1)} %copy-done.8, f32[8,4,128]{2,1,0:T(4,128)S(1)} %reshape.297.gates, f32[8,128]{1,0:T(8,128)S(1)} %fusion.30.stats), custom_call_target="tpu_custom_call" | custom-call | bytes 1024 | tf_op jit(solution)/shard_map/scatter_sum_3/pallas_call | solution.py:614
  460.7 1.0 constant_dynamic-slice_fusion.1
  461.8 0.7 multiply_reduce_fusion.5
  462.6 3.3 multiply_reduce_fusion
  465.9 4.1 fusion.38
  470.0 4.1 convert_element_type.187
  474.2 39.6 %gather_rows_4.1.g_ref = bf16[8,256,2048]{2,1,0:T(8,128)(2,1)} custom-call(bf16[256,2048]{1,0:T(8,128)(2,1)} %get-tuple-element.77.refs_0_), custom_call_target="tpu_custom_call" | custom-call | bytes 1024 | tf_op jit(solution)/shard_map/gather_rows_4/pallas_call | solution.py:385
  513.8 45.4 %attend_back.1 = (bf16[8,256,2048]{2,1,0:T(8,128)(2,1)}, bf16[2048,768]{1,0:T(8,128)(2,1)}, bf16[256,2048]{1,0:T(8,128)(2,1)S(1)}, f32[8,128]{1,0:T(8,128)S(1)}) custom-call(s32[8]{0:T(128)S(1)} %slice_reduce_fusion.lengths_ref, bf16[8,256,2048]{2,1,0:T(8,128)(2,1)} %get-tuple-element.56.x_ref, bf16[8,256,2048]{2,1,0:T(8,128)(2,1)} %gather_rows_4.1.g_ref, ...), custom_call_target="tpu_custom_call" | custom-call | bytes 1024 | tf_op jit(solution)/shard_map/attend_back/pallas_call | solution.py:781
  559.1 4.5 all-to-all-start.3
  563.6 3.5 copy-done.7
  567.1 67.9 %scatter_sum_5.1 = f32[256,2048]{1,0:T(8,128)S(1)} custom-call(bf16[8,256,2048]{2,1,0:T(8,128)(2,1)S(1)} %copy-done.7), custom_call_target="tpu_custom_call" | custom-call | bytes 1024 | tf_op jit(solution)/shard_map/scatter_sum_5/pallas_call | solution.py:605
  635.0 4.1 convert_element_type.188
  639.1 98.9 %reduce-scatter.8.cloned.1.call-done = bf16[2,512,1024]{2,1,0:T(8,128)(2,1)} async-done(((bf16[2,2048,1024]{2,1,0:T(8,128)(2,1)}), bf16[2,512,1024]{2,1,0:T(8,128)(2,1)}) %reduce-scatter.8.cloned.1.call-update) | async-done | bytes 2097168 | tf_op jit(solution)/shard_map/reduce_scatter | solution.py:1112
  738.0 4.2 convert_element_type.193
  742.8 0.9 copy-done.14
  743.8 1.7 fusion.7
  745.4 4.4 all-to-all-start.1
  749.9 2.2 slice_bitcast_fusion.2
  752.5 2.5 pad_maximum_fusion
  755.7 37.9 %all-to-all-done.1 = bf16[4,64,2048]{2,1,0:T(8,128)(2,1)S(1)} async-done(((bf16[4,64,2048]{2,1,0:T(8,128)(2,1)}), bf16[4,64,2048]{2,1,0:T(8,128)(2,1)S(1)}, u32[]{:S(2)}, u32[]{:S(2)}) %all-to-all-start.1) | async-done | bytes 1048608 | tf_op jit(solution)/shard_map/all_to_all | solution.py:1018
  794.2 1.6 bitcast_convert_fusion
  795.9 3.4 copy-done.6
  799.2 40.7 %scatter_sum_6.1 = f32[256,2048]{1,0:T(8,128)S(1)} custom-call(bf16[8,256,2048]{2,1,0:T(8,128)(2,1)S(1)} %copy-done.6), custom_call_target="tpu_custom_call" | custom-call | bytes 1024 | tf_op jit(solution)/shard_map/scatter_sum_6/pallas_call | solution.py:605
  839.9 3.0 multiply_convert_fusion
  842.9 6.3 all-to-all-start.2
  851.4 0.7 copy.143
  852.1 54.0 %small_sum.1 = f32[40,128]{1,0:T(8,128)} custom-call(f32[8,40,128]{2,1,0:T(8,128)} %bitcast.160), custom_call_target="tpu_custom_call" | custom-call | tf_op jit(solution)/shard_map/small_sum/pallas_call | solution.py:257
  906.0 0.7 slice.98
  906.8 0.7 copy.103
  907.5 1.3 fusion.41
  908.8 1.3 slice_bitcast_fusion.3
  910.2 1.6 gather_fusion.3
  911.8 33.0 %all-reduce.7.cloned.1.call-done = bf16[1024,2048]{1,0:T(8,128)(2,1)} async-done(((bf16[1024,2048]{1,0:T(8,128)(2,1)}), bf16[1024,2048]{1,0:T(8,128)(2,1)}) %all-reduce.7.cloned.1.call-update) | async-done | bytes 4194320 | tf_op jit(solution)/shard_map/psum | solution.py:1169
  944.7 6.0 fusion.40
  (187 shorter events, 15.0 us)
Async XLA Ops:
  7.2 3.4 copy-start
  7.2 4.2 copy-start.16
  7.2 5.8 copy-start.49
  7.2 5.8 copy-start.50
  7.2 5.8 copy-start.51
  7.2 5.8 copy-start.52
  7.2 177.1 %all-gather.4.cloned.1.call-start = ((), (), s32[]{:S(2)}) async-start(), calls=%async_computation.7 | async-start | bytes 9437184 | tf_op jit(solution)/shard_map/all_gather | solution.py:1057
  8.0 235.7 %all-gather.6.cloned.1.call-start = ((), (), s32[]{:S(2)}) async-start(), calls=%async_computation.12 | async-start | bytes 9437184 | tf_op jit(solution)/shard_map/all_gather | solution.py:1064
  14.3 55.6 %copy-start.17 = (bf16[256,2048]{1,0:T(8,128)(2,1)S(1)}, bf16[256,2048]{1,0:T(8,128)(2,1)}, u32[]{:S(2)}) copy-start(bf16[256,2048]{1,0:T(8,128)(2,1)} %param.19) | copy-start | bytes 3145732
  68.9 2.7 copy-start.10
  69.9 3.2 copy-start.26
  71.8 56.7 %copy-start.30 = (f32[256]{0:T(256)}, f32[256]{0:T(256)S(1)}, u32[]{:S(2)}) copy-start(f32[256]{0:T(256)S(1)} %add_rsqrt_fusion.1) | copy-start | bytes 3076
  128.5 2.9 copy-start.28
  128.6 2.6 copy-start.42
  128.6 4.4 copy-start.3
  131.5 0.6 copy-start.21
  133.0 3.4 copy-start.2
  152.3 1.0 copy-start.4
  153.3 4.5 copy-start.22
  153.3 31.0 %all-to-all-start = ((bf16[8,256,256]{2,1,0:T(8,128)(2,1)}), bf16[8,256,256]{2,1,0:T(8,128)(2,1)}, u32[]{:S(2)}, u32[]{:S(2)}) async-start(bf16[8,256,256]{2,1,0:T(8,128)(2,1)} %copy-done.4), calls=%async_computation | async-start | bytes 2097152 | tf_op jit(solution)/shard_map/all_to_all | solution.py:1068
  157.7 26.6 %copy-start.11 = (bf16[256,2048]{1,0:T(8,128)(2,1)S(1)}, bf16[256,2048]{1,0:T(8,128)(2,1)}, u32[]{:S(2)}) copy-start(bf16[256,2048]{1,0:T(8,128)(2,1)} %get-tuple-element.53) | copy-start | bytes 3145732
  157.7 312.3 %reduce-scatter.4.cloned.1.call-start = ((), (), s32[]{:S(2)}) async-start(), calls=%async_computation.8 | async-start | bytes 10485760 | tf_op jit(solution)/shard_map/reduce_scatter | solution.py:1102
  191.8 42.4 %copy-start.32 = (f32[256]{0:T(256)}, f32[256]{0:T(256)S(1)}, u32[]{:S(2)}) copy-start(f32[256]{0:T(256)S(1)} %add_rsqrt_fusion) | copy-start | bytes 3076
  240.8 0.7 copy-start.18
  241.6 0.7 copy-start.25
  298.2 336.8 %reduce-scatter.6.cloned.1.call-start = ((), (), s32[]{:S(2)}) async-start(), calls=%async_computation.9 | async-start | bytes 10485760 | tf_op jit(solution)/shard_map/reduce_scatter | solution.py:1112
  382.8 355.2 %reduce-scatter.8.cloned.1.call-start = ((), (), s32[]{:S(2)}) async-start(), calls=%async_computation.10 | async-start | bytes 10485760 | tf_op jit(solution)/shard_map/reduce_scatter | solution.py:1112
  384.0 78.5 %copy-start.36 = (f32[256]{0:T(256)}, f32[256]{0:T(256)S(1)}, u32[]{:S(2)}) copy-start(f32[256]{0:T(256)S(1)} %fusion.33) | copy-start | bytes 3076
  410.2 2.3 copy-start.47
  410.2 2.3 copy-start.48
  413.2 3.4 copy-start.8
  416.6 45.9 %copy-start.33 = (f32[256]{0:T(256)S(1)}, f32[256]{0:T(256)}, u32[]{:S(2)}) copy-start(f32[256]{0:T(256)} %copy-done.32) | copy-start | bytes 3076
  459.4 6.4 copy-start.19
  460.7 5.1 copy-start.38
  461.7 4.1 copy-start.23
  461.7 4.1 copy-start.34
  462.4 3.4 copy-start.45
  462.5 3.3 copy-start.40
  462.5 3.3 copy-start.15
  462.5 3.3 copy-start.43
  474.1 39.6 %copy-start.5 = (bf16[8,256,256]{2,1,0:T(8,128)(2,1)S(1)}, bf16[8,256,256]{2,1,0:T(8,128)(2,1)}, u32[]{:S(2)}) copy-start(bf16[8,256,256]{2,1,0:T(8,128)(2,1)} %copy-done.4) | copy-start | bytes 3145732
  474.1 39.6 %copy-start.9 = (bf16[256,2048]{1,0:T(8,128)(2,1)S(1)}, bf16[256,2048]{1,0:T(8,128)(2,1)}, u32[]{:S(2)}) copy-start(bf16[256,2048]{1,0:T(8,128)(2,1)} %wo_ref.1) | copy-start | bytes 3145732
  559.1 186.3 %all-to-all-start.3 = ((bf16[8,256,768]{2,1,0:T(8,128)(2,1)}), bf16[8,256,768]{2,1,0:T(8,128)(2,1)}, u32[]{:S(2)}, u32[]{:S(2)}) async-start(bf16[8,256,768]{2,1,0:T(8,128)(2,1)} %bitcast.155), calls=%async_computation.5 | async-start | bytes 6291456 | tf_op jit(solution)/shard_map/all_to_all | solution.py:1151
  563.6 3.5 copy-start.7
  639.1 103.0 %copy-start.27 = (f32[1,2,8,128]{3,1,2,0:T(2,128)S(1)}, f32[1,2,8,128]{3,1,2,0:T(2,128)}, u32[]{:S(2)}) copy-start(f32[1,2,8,128]{3,1,2,0:T(2,128)} %copy-done.26) | copy-start | bytes 24580
  639.1 103.0 %copy-start.31 = (f32[256]{0:T(256)S(1)}, f32[256]{0:T(256)}, u32[]{:S(2)}) copy-start(f32[256]{0:T(256)} %copy-done.30) | copy-start | bytes 3076
  738.0 4.2 copy-start.12
  742.2 1.6 copy-start.14
  745.4 48.2 %all-to-all-start.1 = ((bf16[4,64,2048]{2,1,0:T(8,128)(2,1)}), bf16[4,64,2048]{2,1,0:T(8,128)(2,1)S(1)}, u32[]{:S(2)}, u32[]{:S(2)}) async-start(bf16[4,64,2048]{2,1,0:T(8,128)(2,1)} %bitcast.151), calls=%async_computation.3 | async-start | bytes 2097152 | tf_op jit(solution)/shard_map/all_to_all | solution.py:1018
  749.9 194.9 %all-reduce.7.cloned.1.call-start = ((), (), s32[]{:S(2)}) async-start(), calls=%async_computation.11 | async-start | bytes 8388608 | tf_op jit(solution)/shard_map/psum | solution.py:1169
  755.0 0.7 copy-start.54
  795.9 3.4 copy-start.6
  799.2 40.7 %copy-start.44 = (f32[256]{0:T(256)S(1)}, f32[256]{0:T(256)}, u32[]{:S(2)}) copy-start(f32[256]{0:T(256)} %copy-done.42) | copy-start | bytes 3076
  842.9 6.3 copy-start.13
  842.9 6.3 copy-start.20
  842.9 6.3 copy-start.24
  842.9 6.3 copy-start.35
  842.9 6.3 copy-start.37
  842.9 6.3 copy-start.39
  842.9 6.3 copy-start.41
  842.9 6.3 copy-start.46
  842.9 67.3 %all-to-all-start.2 = ((bf16[4,64,2048]{2,1,0:T(8,128)(2,1)}), bf16[4,64,2048]{2,1,0:T(8,128)(2,1)S(1)}, u32[]{:S(2)}, u32[]{:S(2)}) async-start(bf16[4,64,2048]{2,1,0:T(8,128)(2,1)} %bitcast.29), calls=%async_computation.4 | async-start | bytes 2097152 | tf_op jit(solution)/shard_map/all_to_all | solution.py:1018
  849.2 1.1 copy-start.29
  944.7 6.0 copy-start.1
  (1 other events, 0.6 us)
Sparse Core Ops, SparseCore 0:
  10.0 97.2 all-gather.3
  131.3 65.4 all-gather.5
  298.3 144.7 reduce-scatter.3
  445.4 145.1 reduce-scatter.5
  592.8 145.1 reduce-scatter.7
  755.1 189.5 all-reduce.6

commit v4 on v3

--- a/solution.py
+++ b/solution.py
@@ -15,6 +15,7 @@
 f32 = jnp.float32
 MESH = pl.DeviceIdType.MESH
 DMA = pltpu.SemaphoreType.DMA
+kernel_vmem = 62 << 20
 small_cost = pl.CostEstimate(flops=0, transcendentals=0, bytes_accessed=1024)
 
 
@@ -207,69 +208,402 @@
             DMA((3, n)),
             DMA((3, n)),
         ],
-        compiler_params=pltpu.CompilerParams(collective_id=collective_id, has_side_effects=True),
+        compiler_params=pltpu.CompilerParams(
+            collective_id=collective_id, has_side_effects=True, vmem_limit_bytes=kernel_vmem
+        ),
         cost_estimate=small_cost,
         name="front",
     )(small, ints, blocks, wq, wk, wv)
 
 
-def small_sum_kernel(n, replicas, x_ref, o_ref, got, total, send_sem, recv_sem, over_send, over_recv):
+VMEM_SPEC = pl.BlockSpec(memory_space=pltpu.VMEM)
+AWAY_SPEC = pl.BlockSpec(memory_space=pl.ANY)
+
+
+def along_dp(src, dst, send, recv, to):
+    return pltpu.make_async_remote_copy(
+        src_ref=src, dst_ref=dst, send_sem=send, recv_sem=recv, device_id={"dp": to}, device_id_type=MESH
+    )
+
+
+class Exchange:
+    over_dp = False
+
+    def __init__(self, x, n, replicas, columns=None):
+        self.n = n
+        self.columns = columns or x.shape[2]
+        self.ins = [(x, VMEM_SPEC)]
+        self.outs = [(jax.ShapeDtypeStruct(x.shape, x.dtype), VMEM_SPEC)]
+        self.scratch = [DMA((n,)), DMA((n,))]
+
+    def start(self, me, src, out, send, recv):
+        cols = pl.ds(0, self.columns)
+        self.copies = []
+        for k in range(1, self.n):
+            to = lax.rem(me + k, self.n)
+            self.copies.append(
+                remote(src.at[to, :, cols], out.at[me, :, cols], send.at[k], recv.at[k], to)
+            )
+            self.copies[-1].start()
+        out[me, :, : self.columns] = src[me, :, : self.columns]
+        if self.columns < src.shape[2]:
+            out[:, :, self.columns :] = src[:, :, self.columns :]
+
+    def finish(self, me, *refs):
+        for copy in self.copies:
+            copy.wait()
+
+
+class DpSum:
+    over_dp = True
+
+    def __init__(self, x, n, replicas):
+        self.replicas = replicas
+        self.ins = [(x, VMEM_SPEC)]
+        self.outs = [(jax.ShapeDtypeStruct(x.shape, x.dtype), VMEM_SPEC)]
+        self.scratch = [pltpu.VMEM((replicas,) + x.shape, x.dtype), DMA((replicas,)), DMA((replicas,))]
+
+    def start(self, me, src, out, got, send, recv):
+        here = lax.axis_index("dp")
+        got[here] = src[...]
+        self.copies = []
+        for k in range(1, self.replicas):
+            to = lax.rem(here + k, self.replicas)
+            self.copies.append(along_dp(src, got.at[here], send.at[k], recv.at[k], to))
+            self.copies[-1].start()
+
+    def finish(self, me, src, out, got, send, recv):
+        for copy in self.copies:
+            copy.wait()
+        value = got[0]
+        for k in range(1, self.replicas):
+            value = value + got[k]
+        out[...] = value
+
+
+class SmallSum:
+    over_dp = True
+
+    def __init__(self, x, n, replicas):
+        self.n, self.replicas = n, replicas
+        shape = x.shape[1:]
+        self.ins = [(x, VMEM_SPEC)]
+        self.outs = [(jax.ShapeDtypeStruct(shape, f32), VMEM_SPEC)]
+        self.scratch = [pltpu.VMEM(x.shape, f32), pltpu.VMEM((replicas,) + shape, f32)]
+        self.scratch += [DMA((n,)), DMA((n,)), DMA((replicas,)), DMA((replicas,))]
+
+    def start(self, me, src, out, got, total, send, recv, over_send, over_recv):
+        got[me] = src[me]
+        self.copies = []
+        for k in range(1, self.n):
+            to = lax.rem(me + k, self.n)
+            self.copies.append(remote(src.at[to], got.at[me], send.at[k], recv.at[k], to))
+            self.copies[-1].start()
+
+    def finish(self, me, src, out, got, total, send, recv, over_send, over_recv):
+        here = lax.axis_index("dp")
+        for copy in self.copies:
+            copy.wait()
+        value = got[0]
+        for k in range(1, self.n):
+            value = value + got[k]
+        total[here] = value
+        copies = []
+        for k in range(1, self.replicas):
+            to = lax.rem(here + k, self.replicas)
+            copies.append(along_dp(total.at[here], total.at[here], over_send.at[k], over_recv.at[k], to))
+            copies[-1].start()
+        for copy in copies:
+            copy.wait()
+        value = total[0]
+        for k in range(1, self.replicas):
+            value = value + total[k]
+        out[...] = value
+
+
+class Deal:
+    over_dp = True
+
+    def __init__(self, blocks, n, replicas):
+        self.replicas = replicas
+        _, rows, width = blocks.shape
+        self.ins = [(blocks, AWAY_SPEC)]
+        self.outs = [(jax.ShapeDtypeStruct((replicas * rows, width), blocks.dtype), AWAY_SPEC)]
+        self.scratch = [DMA, DMA((replicas,)), DMA((replicas,))]
+
+    def start(self, me, src, out, own, send, recv):
+        kept, away = deal_copies(self.replicas, src, out, own, send, recv)
+        kept.start()
+        for copy in away:
+            copy.start()
+        self.copies = away + [kept]
+
+    def finish(self, me, *refs):
+        for copy in self.copies:
+            copy.wait()
+
+
+class DpGather:
+    over_dp = True
+
+    def __init__(self, x, n, replicas, parts=4):
+        self.replicas, self.parts = replicas, parts
+        self.size = x.shape[0] // parts
+        self.ins = [(x, AWAY_SPEC)]
+        self.outs = [(jax.ShapeDtypeStruct((replicas,) + x.shape, x.dtype), AWAY_SPEC)]
+        self.scratch = [DMA, DMA((2, replicas, parts)), DMA((2, replicas, parts))]
+
+    def piece(self, p):
+        return pl.ds(p * self.size, self.size)
+
+    def hop(self, src, out, send, recv, way, k, p):
+        here = lax.axis_index("dp")
+        step = 1 - 2 * way
+        block = out.at[here - step * k, self.piece(p)]
+        origin = block if k else src.at[self.piece(p)]
+        return along_dp(origin, block, send.at[way, k, p], recv.at[way, k, p], here + step)
+
+    def sends(self, way, k):
+        here = lax.axis_index("dp")
+        last = self.replicas - 1
+        if way == 0:
+            return (here >= k) & (here < last), here >= k + 1
+        return (here + k <= last) & (here > 0), here + k + 1 <= last
+
+    def start(self, me, src, out, own, send, recv):
+        self.copy = pltpu.make_async_copy(src, out.at[lax.axis_index("dp")], own)
+        self.copy.start()
+        for way in range(2):
+
+            @pl.when(self.sends(way, 0)[0])
+            def _():
+                for p in range(self.parts):
+                    self.hop(src, out, send, recv, way, 0, p).start()
+
+    def steps(self, src, out, own, send, recv):
+        here = lax.axis_index("dp")
+        for k in range(self.replicas - 1):
+            for p in range(self.parts):
+                for way in range(2):
+
+                    @pl.when(self.sends(way, k)[1])
+                    def _():
+                        block = out.at[here - (1 - 2 * way) * (k + 1), self.piece(p)]
+                        along_dp(
+                            block, block, send.at[way, k, p], recv.at[way, k, p], here
+                        ).wait_recv()
+
+                    if k + 1 < self.replicas - 1:
+
+                        @pl.when(self.sends(way, k + 1)[0])
+                        def _():
+                            self.hop(src, out, send, recv, way, k + 1, p).start()
+
+                yield
+
+        for k in range(self.replicas - 1):
+            for way in range(2):
+
+                @pl.when(self.sends(way, k)[0])
+                def _():
+                    for p in range(self.parts):
+                        self.hop(src, out, send, recv, way, k, p).wait_send()
+
+        self.copy.wait()
+
+
+class LineSum:
+    over_dp = True
+
+    def __init__(self, x, n, replicas, parts=4):
+        self.replicas, self.parts = replicas, parts
+        self.blocks, rows, columns = x.shape
+        self.rows = rows // replicas
+        self.size = self.rows // parts
+        held = pltpu.VMEM((replicas, self.blocks, self.rows, columns), bf16)
+        self.ins = [(x, AWAY_SPEC)]
+        self.outs = [(jax.ShapeDtypeStruct((self.blocks, self.rows, columns), f32), VMEM_SPEC)]
+        sems = DMA((2, replicas, parts))
+        self.scratch = [held, held, held, DMA((replicas, parts)), sems, sems]
+
+    def load(self, x, own, sem, c, p):
+        rows = pl.ds(pl.multiple_of(c * self.rows + p * self.size, self.size), self.size)
+        return pltpu.make_async_copy(
+            x.at[:, rows], own.at[c, :, pl.ds(p * self.size, self.size)], sem.at[c, p]
+        )
+
+    def hop(self, own, got, send, recv, way, c, p):
+        here = lax.axis_index("dp")
+        rows = pl.ds(p * self.size, self.size)
+        return along_dp(
+            own.at[c, :, rows],
+            got.at[c, :, rows],
+            send.at[way, c, p],
+            recv.at[way, c, p],
+            here + 1 - 2 * way,
+        )
+
+    def add(self, total, got, c, p, widen=None):
+        chunk = min(self.size, 32)
+        for b in range(self.blocks):
+
+            @pl.loop(0, self.size // chunk)
+            def _(i):
+                rows = pl.ds(p * self.size + i * chunk, chunk)
+                if widen is None:
+                    value = total[c, b, rows].astype(f32) + got[c, b, rows].astype(f32)
+                    total[c, b, rows] = value.astype(bf16)
+                elif got is None:
+                    widen[b, rows] = total[c, b, rows].astype(f32)
+                else:
+                    widen[b, rows] = widen[b, rows] + got[c, b, rows].astype(f32)
+
+    def start(self, me, x, out, own, up, down, loads, send, recv):
+        for t in range(self.replicas):
+            for p in range(self.parts):
+                self.load(x, own, loads, t, p).start()
+
+    def steps(self, x, out, own, up, down, loads, send, recv):
+        here = lax.axis_index("dp")
+        last = self.replicas - 1
+        for t in range(last):
+            for p in range(self.parts):
+                for way, c, got in ((0, last - t, up), (1, t, down)):
+                    bound = here < c if way == 0 else here > c
+                    inner = here > 0 if way == 0 else here < last
+
+                    @pl.when(bound)
+                    def _():
+                        self.load(x, own, loads, c, p).wait()
+
+                        @pl.when(inner)
+                        def _():
+                            self.hop(own, got, send, recv, way, c, p).wait_recv()
+                            self.add(own, got, c, p)
+
+                        self.hop(own, got, send, recv, way, c, p).start()
+
+                yield
+        for p in range(self.parts):
+            self.load(x, own, loads, here, p).wait()
+            self.add(own, None, here, p, out)
+            for way, got, inner in ((0, up, here > 0), (1, down, here < last)):
+
+                @pl.when(inner)
+                def _():
+                    self.hop(own, got, send, recv, way, here, p).wait_recv()
+                    self.add(own, got, here, p, out)
+
+        for t in range(last):
+            for p in range(self.parts):
+                for way, c, got in ((0, last - t, up), (1, t, down)):
+
+                    @pl.when(here < c if way == 0 else here > c)
+                    def _():
+                        self.hop(own, got, send, recv, way, c, p).wait_send()
+
+
+def close_kernel(exchange, gather, line, meet, share, x, full, out, rows, *refs):
+    swap_refs, refs = refs[:2], refs[2:]
+    gather_refs, line_refs = refs[: len(gather.scratch)], refs[len(gather.scratch) :]
     me = lax.axis_index("expert")
-    here = lax.axis_index("dp")
-    greet(n, me, replicas)
-    copies = []
-    for k in range(1, n):
-        to = lax.rem(me + k, n)
-        copy = remote(x_ref.at[to], got.at[me], send_sem.at[k], recv_sem.at[k], to)
-        copy.start()
-        copies.append(copy)
-    got[me] = x_ref[me]
-    for copy in copies:
-        copy.wait()
-    value = got[0]
-    for k in range(1, n):
-        value = value + got[k]
-    total[here] = value
-    copies = []
-    for k in range(1, replicas):
-        copy = pltpu.make_async_remote_copy(
-            src_ref=total.at[here],
-            dst_ref=total.at[here],
-            send_sem=over_send.at[k],
-            recv_sem=over_recv.at[k],
-            device_id={"dp": lax.rem(here + k, replicas)},
-            device_id_type=MESH,
-        )
-        copy.start()
-        copies.append(copy)
-    for copy in copies:
-        copy.wait()
-    value = total[0]
-    for k in range(1, replicas):
-        value = value + total[k]
-    o_ref[...] = value
-
-
-def small_sum(x, replicas, collective_id):
-    n = x.shape[0]
-    shape = x.shape[1:]
-    vmem = pl.BlockSpec(memory_space=pltpu.VMEM)
+    line.start(me, x, out, *line_refs)
+    meet(me)
+    exchange.start(me, share, rows, *swap_refs)
+    running = [line.steps(x, out, *line_refs)]
+    next(running[0])
+    exchange.finish(me)
+    gather.start(me, rows, full, *gather_refs)
+    running.append(gather.steps(rows, full, *gather_refs))
+    while running:
+        running = [r for r in running if next(r, True) is None]
+
+
+def close(attn_share, columns, grad_up_w, n, replicas, collective_id, riders):
+    exchange = Exchange(attn_share, n, replicas, columns)
+    gather = DpGather(attn_share, n, replicas)
+    line = LineSum(grad_up_w, n, replicas)
+    return riding_call(
+        n,
+        replicas,
+        functools.partial(close_kernel, exchange, gather, line),
+        exchange.ins + line.ins,
+        gather.outs + line.outs,
+        [pltpu.VMEM(attn_share.shape, bf16)] + exchange.scratch + gather.scratch + line.scratch,
+        riders,
+        collective_id,
+        "close",
+    )
+
+
+class SmallGather:
+    over_dp = False
+
+    def __init__(self, x, n, replicas):
+        self.n = n
+        self.ins = [(x, VMEM_SPEC)]
+        self.outs = [(jax.ShapeDtypeStruct((n,) + x.shape, x.dtype), VMEM_SPEC)]
+        self.scratch = [DMA((n,)), DMA((n,))]
+
+    def start(self, me, src, out, send, recv):
+        out[me] = src[...]
+        self.copies = []
+        for k in range(1, self.n):
+            to = lax.rem(me + k, self.n)
+            self.copies.append(remote(src, out.at[me], send.at[k], recv.at[k], to))
+            self.copies[-1].start()
+
+    def finish(self, me, *refs):
+        for copy in self.copies:
+            copy.wait()
+
+
+def riding_kernel(n, replicas, main, counts, riders, *refs):
+    n_in, n_out, n_scratch = counts
+    at = [0]
+
+    def take(count):
+        at[0] += count
+        return refs[at[0] - count : at[0]]
+
+    main_in = take(n_in)
+    rider_in = [take(len(r.ins)) for r in riders]
+    main_out = take(n_out)
+    rider_out = [take(len(r.outs)) for r in riders]
+    main_scratch = take(n_scratch)
+    rider_refs = [i + o + take(len(r.scratch)) for r, i, o in zip(riders, rider_in, rider_out)]
+
+    def meet(me):
+        greet(n, me, replicas if any(r.over_dp for r in riders) else 1)
+        for rider, own in zip(riders, rider_refs):
+            rider.start(me, *own)
+
+    main(meet, *main_in, *main_out, *main_scratch)
+    me = lax.axis_index("expert")
+    for rider, own in zip(riders, rider_refs):
+        rider.finish(me, *own)
+
+
+def riding_call(n, replicas, main, ins, outs, scratch, riders, collective_id, name):
+    pairs_in = ins + [pair for r in riders for pair in r.ins]
+    pairs_out = outs + [pair for r in riders for pair in r.outs]
+    counts = (len(ins), len(outs), len(scratch))
     return pl.pallas_call(
-        functools.partial(small_sum_kernel, n, replicas),
-        out_shape=jax.ShapeDtypeStruct(shape, f32),
-        in_specs=[vmem],
-        out_specs=vmem,
-        scratch_shapes=[
-            pltpu.VMEM(x.shape, f32),
-            pltpu.VMEM((replicas,) + shape, f32),
-            DMA((n,)),
-            DMA((n,)),
-            DMA((replicas,)),
-            DMA((replicas,)),
-        ],
-        compiler_params=pltpu.CompilerParams(collective_id=collective_id, has_side_effects=True),
-        name="small_sum",
-    )(x)
+        functools.partial(riding_kernel, n, replicas, main, counts, riders),
+        out_shape=[shape for shape, _ in pairs_out],
+        in_specs=[spec for _, spec in pairs_in],
+        out_specs=[spec for _, spec in pairs_out],
+        scratch_shapes=scratch + [shape for r in riders for shape in r.scratch],
+        compiler_params=pltpu.CompilerParams(
+            collective_id=collective_id, has_side_effects=True, vmem_limit_bytes=kernel_vmem
+        ),
+        cost_estimate=small_cost,
+        name=name,
+    )(*[value for value, _ in pairs_in])
+
+
+def ride_only(meet, *refs):
+    meet(lax.axis_index("expert"))
 
 
 def quad_gather_kernel(parts, meet, x_ref, o_ref, own_sem, send_sem, recv_sem, pass_sem, pair_send, pair_recv):
@@ -356,53 +690,20 @@
     return functools.partial(any_gather_kernel, n), sems
 
 
-def gather_only(n, kernel, *refs):
-    kernel(functools.partial(greet, n), *refs)
-
-
-def gather_and_deal(n, replicas, kernel, x_ref, blocks, o_ref, seq, own_sem, deal_send, deal_recv, *sems):
-    own, away = deal_copies(replicas, blocks, seq, own_sem, deal_send, deal_recv)
-
-    def meet(me):
-        own.start()
-        greet(n, me, replicas)
-        for copy in away:
-            copy.start()
-
-    kernel(meet, x_ref, o_ref, *sems)
-    for copy in away:
-        copy.wait()
-    own.wait()
-
-
-def gather_rows(x, n, collective_id, parts=4, blocks=None):
+def gather_rows(x, n, replicas, collective_id, riders=(), parts=4):
     kernel, sems = gather_plan(n, parts)
-    params = pltpu.CompilerParams(collective_id=collective_id, has_side_effects=True)
-    away = pl.BlockSpec(memory_space=pl.ANY)
-    shape = jax.ShapeDtypeStruct((n,) + x.shape, x.dtype)
-    name = f"gather_rows_{collective_id}"
-    if blocks is None:
-        return pl.pallas_call(
-            functools.partial(gather_only, n, kernel),
-            out_shape=shape,
-            in_specs=[away],
-            out_specs=away,
-            scratch_shapes=sems,
-            compiler_params=params,
-            cost_estimate=small_cost,
-            name=name,
-        )(x)
-    replicas = blocks.shape[0]
-    return pl.pallas_call(
-        functools.partial(gather_and_deal, n, replicas, kernel),
-        out_shape=[shape, jax.ShapeDtypeStruct((replicas * blocks.shape[1], blocks.shape[2]), bf16)],
-        in_specs=[away, away],
-        out_specs=[away, away],
-        scratch_shapes=[DMA, DMA((replicas,)), DMA((replicas,))] + sems,
-        compiler_params=params,
-        cost_estimate=small_cost,
-        name=name,
-    )(x, blocks)
+    out = jax.ShapeDtypeStruct((n,) + x.shape, x.dtype)
+    return riding_call(
+        n,
+        replicas,
+        kernel,
+        [(x, AWAY_SPEC)],
+        [(out, AWAY_SPEC)],
+        sems,
+        list(riders),
+        collective_id,
+        f"gather_rows_{collective_id}",
+    )
 
 
 def add_rows(total, first, rows, chunk, *terms):
@@ -413,48 +714,6 @@
         for term in terms[1:]:
             value = value + term[s].astype(f32)
         total[s] = value.astype(total.dtype)
-
-
-class Riders:
-    def __init__(self, n, replicas, gates, stats, gates_out, stats_out, got, sems):
-        self.n, self.replicas = n, replicas
-        self.refs = (gates, stats, gates_out, stats_out, got)
-        self.sems = sems
-
-    def start(self, me):
-        gates, stats, gates_out, _, got = self.refs
-        here = lax.axis_index("dp")
-        gates_out[me] = gates[me]
-        got[here] = stats[...]
-        greet(self.n, me, self.replicas)
-        self.copies = []
-        for k in range(1, self.n):
-            to = lax.rem(me + k, self.n)
-            self.copies.append(
-                remote(gates.at[to], gates_out.at[me], self.sems[0].at[k], self.sems[1].at[k], to)
-            )
-        for k in range(1, self.replicas):
-            self.copies.append(
-                pltpu.make_async_remote_copy(
-                    src_ref=stats,
-                    dst_ref=got.at[here],
-                    send_sem=self.sems[2].at[k],
-                    recv_sem=self.sems[3].at[k],
-                    device_id={"dp": lax.rem(here + k, self.replicas)},
-                    device_id_type=MESH,
-                )
-            )
-        for copy in self.copies:
-            copy.start()
-
-    def finish(self):
-        _, _, _, stats_out, got = self.refs
-        for copy in self.copies:
-            copy.wait()
-        value = got[0]
-        for k in range(1, self.replicas):
-            value = value + got[k]
-        stats_out[...] = value
 
 
 def quad_scatter_kernel(
@@ -570,17 +829,7 @@
         copy.wait_send()
 
 
-def scatter_only(n, kernel, *refs):
-    kernel(functools.partial(greet, n), *refs)
-
-
-def scatter_and_ride(n, replicas, kernel, p_ref, gates, stats, o_ref, gates_out, stats_out, got, *rest):
-    riders = Riders(n, replicas, gates, stats, gates_out, stats_out, got, rest[:4])
-    kernel(riders.start, p_ref, o_ref, *rest[4:])
-    riders.finish()
-
-
-def scatter_sum(x, n, collective_id, parts=4, replicas=1, riders=None):
+def scatter_sum(x, n, replicas, collective_id, riders=(), parts=4):
     chips = n // 2
     shape = x.shape[1:]
     blocks = pltpu.VMEM((chips,) + shape, bf16)
@@ -591,45 +840,17 @@
     else:
         kernel = functools.partial(any_scatter_kernel, n)
         scratch = [blocks] * 3 + [DMA((chips,))] * 5
-    vmem = pl.BlockSpec(memory_space=pltpu.VMEM)
-    away = pl.BlockSpec(memory_space=pl.ANY)
-    common = dict(
-        compiler_params=pltpu.CompilerParams(
-            collective_id=collective_id, has_side_effects=True, vmem_limit_bytes=(3 * chips + 12) << 20
-        ),
-        cost_estimate=small_cost,
-        name=f"scatter_sum_{collective_id}",
-    )
-    out = jax.ShapeDtypeStruct(shape, f32)
-    if riders is None:
-        return pl.pallas_call(
-            functools.partial(scatter_only, n, kernel),
-            out_shape=out,
-            in_specs=[away],
-            out_specs=vmem,
-            scratch_shapes=scratch,
-            **common,
-        )(x)
-    gates, stats = riders
-    return pl.pallas_call(
-        functools.partial(scatter_and_ride, n, replicas, kernel),
-        out_shape=[
-            out,
-            jax.ShapeDtypeStruct(gates.shape, f32),
-            jax.ShapeDtypeStruct(stats.shape, f32),
-        ],
-        in_specs=[away, vmem, vmem],
-        out_specs=[vmem, vmem, vmem],
-        scratch_shapes=[
-            pltpu.VMEM((replicas,) + stats.shape, f32),
-            DMA((n,)),
-            DMA((n,)),
-            DMA((replicas,)),
-            DMA((replicas,)),
-        ]
-        + scratch,
-        **common,
-    )(x, gates, stats)
+    return riding_call(
+        n,
+        replicas,
+        kernel,
+        [(x, AWAY_SPEC)],
+        [(jax.ShapeDtypeStruct(shape, f32), VMEM_SPEC)],
+        scratch,
+        list(riders),
+        collective_id,
+        f"scatter_sum_{collective_id}",
+    )
 
 
 def dot(left, right, left_dim=1, right_dim=0):
@@ -654,7 +875,9 @@
     return raised / jnp.sum(raised, axis=-1, keepdims=True)
 
 
-def attend_kernel(heads, head_dim, lengths_ref, x_ref, w_ref, qg_ref, kg_ref, cos_ref, sin_ref, mixed_ref):
+def attend_kernel(
+    heads, head_dim, lengths_ref, x_ref, w_ref, wo_ref, qg_ref, kg_ref, cos_ref, sin_ref, mixed_ref, part_ref
+):
     length = lengths_ref[pl.program_id(0)]
     wide = heads * head_dim
     qkv = dot(x_ref[0], w_ref[...])
@@ -667,9 +890,10 @@
         v = qkv[:, 2 * wide + at : 2 * wide + at + head_dim].astype(bf16)
         probs = head_probs(q_rot, k_rot, length, 1.0 / math.sqrt(head_dim))
         mixed_ref[0, :, at : at + head_dim] = dot(probs.astype(bf16), v).astype(bf16)
-
-
-def attend(lengths, x, w_qkv, query_g, key_g, cosine, signed_sine):
+    part_ref[0] = dot(mixed_ref[0], wo_ref[...]).astype(bf16)
+
+
+def attend(lengths, x, w_qkv, w_out, query_g, key_g, cosine, signed_sine):
     seqs, rows, width = x.shape
     head_dim = query_g.shape[0]
     wide = w_qkv.shape[1] // 3
@@ -678,24 +902,31 @@
     gain = pl.BlockSpec((1, head_dim), whole)
     return pl.pallas_call(
         functools.partial(attend_kernel, wide // head_dim, head_dim),
-        out_shape=jax.ShapeDtypeStruct((seqs, rows, wide), bf16),
+        out_shape=[
+            jax.ShapeDtypeStruct((seqs, rows, wide), bf16),
+            jax.ShapeDtypeStruct((seqs, rows, width), bf16),
+        ],
         grid_spec=pltpu.PrefetchScalarGridSpec(
             num_scalar_prefetch=1,
             grid=(seqs,),
             in_specs=[
                 pl.BlockSpec((1, rows, width), lambda s, lens: (s, 0, 0)),
                 pl.BlockSpec((width, 3 * wide), whole),
+                pl.BlockSpec((wide, width), whole),
                 gain,
                 gain,
                 table,
                 table,
             ],
-            out_specs=pl.BlockSpec((1, rows, wide), lambda s, lens: (s, 0, 0)),
+            out_specs=[
+                pl.BlockSpec((1, rows, wide), lambda s, lens: (s, 0, 0)),
+                pl.BlockSpec((1, rows, width), lambda s, lens: (s, 0, 0)),
+            ],
         ),
-        compiler_params=pltpu.CompilerParams(vmem_limit_bytes=32 << 20),
+        compiler_params=pltpu.CompilerParams(vmem_limit_bytes=kernel_vmem),
         cost_estimate=small_cost,
         name="attend",
-    )(lengths, x, w_qkv, query_g[None, :], key_g[None, :], cosine, signed_sine)
+    )(lengths, x, w_qkv, w_out, query_g[None, :], key_g[None, :], cosine, signed_sine)
 
 
 def attend_back_kernel(
@@ -713,7 +944,6 @@
     sin_ref,
     part_ref,
     dw_ref,
-    dwo_ref,
     dgain_ref,
     dw_acc,
     dwo_acc,
@@ -765,8 +995,10 @@
 
     @pl.when(step == pl.num_programs(0) - 1)
     def _():
-        dw_ref[...] = dw_acc[...].astype(bf16)
-        dwo_ref[...] = dwo_acc[...].astype(bf16)
+        dw_ref[:, : 3 * wide] = dw_acc[...].astype(bf16)
+        for i in range(dwo_acc.shape[1] // wide):
+            at = i * wide
+            dw_ref[at : at + wide, 3 * wide :] = dwo_acc[:, at : at + wide].astype(bf16)
         dgain_ref[...] = gain_acc[...]
 
 
@@ -782,8 +1014,7 @@
         functools.partial(attend_back_kernel, wide // head_dim, head_dim),
         out_shape=(
             jax.ShapeDtypeStruct((seqs, rows, width), bf16),
-            jax.ShapeDtypeStruct((width, 3 * wide), bf16),
-            jax.ShapeDtypeStruct((wide, width), bf16),
+            jax.ShapeDtypeStruct((width, 4 * wide), bf16),
             jax.ShapeDtypeStruct((8, head_dim), f32),
         ),
         grid_spec=pltpu.PrefetchScalarGridSpec(
@@ -802,8 +1033,7 @@
             ],
             out_specs=(
                 pl.BlockSpec((1, rows, width), block),
-                pl.BlockSpec((width, 3 * wide), whole),
-                pl.BlockSpec((wide, width), whole),
+                pl.BlockSpec((width, 4 * wide), whole),
                 pl.BlockSpec((8, head_dim), whole),
             ),
             scratch_shapes=[
@@ -813,7 +1043,7 @@
                 pltpu.VMEM((rows, 3 * wide), bf16),
             ],
         ),
-        compiler_params=pltpu.CompilerParams(vmem_limit_bytes=48 << 20),
+        compiler_params=pltpu.CompilerParams(vmem_limit_bytes=kernel_vmem),
         cost_estimate=small_cost,
         name="attend_back",
     )(lengths, x, g, mixed, w_qkv, w_out, query_g[None, :], key_g[None, :], cosine, signed_sine)
@@ -850,14 +1080,14 @@
     return 2 if groups % 2 == 0 else 1
 
 
-def expert_forward(mlp_all, cot_all, slot_of, gates, w_gate, w_up, capacity):
+def expert_forward(mlp_all, cot_all, slot_of, gates, w_gate, w_up, capacity, index):
     groups, tok_rows, width = mlp_all.shape
-    local, _, ff = w_gate.shape
+    local, ff = 1, w_gate.shape[2]
     seqs = step_rows(groups)
     slots = seqs * capacity
     tok = pl.BlockSpec((seqs, tok_rows, width), lambda i: (i, 0, 0))
-    route = pl.BlockSpec((local, seqs, 1, tok_rows), lambda i: (0, i, 0, 0))
-    weight = pl.BlockSpec((local, width, ff), lambda i: (0, 0, 0), pipeline_mode=pl.Buffered(1))
+    route = pl.BlockSpec((local, seqs, 1, tok_rows), lambda i: (index, i, 0, 0))
+    weight = pl.BlockSpec((local, width, ff), lambda i: (index, 0, 0), pipeline_mode=pl.Buffered(1))
     wide = pl.BlockSpec((local, slots, width), lambda i: (0, i, 0))
     slim = pl.BlockSpec((local, slots, ff), lambda i: (0, i, 0))
     total = groups * capacity
@@ -873,16 +1103,18 @@
         grid=(groups // seqs,),
         in_specs=[tok, tok, route, route, weight, weight],
         out_specs=[wide, wide, slim, slim, slim],
-        compiler_params=pltpu.CompilerParams(vmem_limit_bytes=60 << 20),
+        compiler_params=pltpu.CompilerParams(vmem_limit_bytes=kernel_vmem),
         cost_estimate=small_cost,
         name="expert_forward",
     )(mlp_all, cot_all, slot_of[:, :, None, :], gates[:, :, None, :], w_gate, w_up)
 
 
-def expert_out_kernel(capacity, act_ref, cot_ref, slot_ref, gate_ref, wd_ref, sum_ref, gg_ref):
+def expert_out_kernel(capacity, *refs):
+    act_refs = refs[:-6]
+    cot_ref, slot_ref, gate_ref, wd_ref, sum_ref, gg_ref = refs[-6:]
     parts = [None] * cot_ref.shape[0]
     for j in range(wd_ref.shape[0]):
-        out = dot(act_ref[j], wd_ref[j])
+        out = dot(act_refs[j][0], wd_ref[j])
         for s in range(cot_ref.shape[0]):
             one_hot = jnp.where(slot_matrix(slot_ref[j, s], capacity), 1.0, 0.0).astype(bf16)
             here = dot(one_hot, out[s * capacity : (s + 1) * capacity].astype(bf16), 0, 0)
@@ -893,7 +1125,7 @@
         sum_ref[s] = parts[s].astype(bf16)
 
 
-def expert_combine(act, cot_all, slot_of, gates, w_down, capacity):
+def expert_combine(acts, cot_all, slot_of, gates, w_down, capacity):
     groups, tok_rows, width = cot_all.shape
     local, ff, _ = w_down.shape
     seqs = step_rows(groups)
@@ -901,7 +1133,7 @@
     route = pl.BlockSpec((local, seqs, 1, tok_rows), lambda i: (0, i, 0, 0))
     column = pl.BlockSpec((local, seqs, tok_rows, 1), lambda i: (0, i, 0, 0))
     weight = pl.BlockSpec((local, ff, width), lambda i: (0, 0, 0), pipeline_mode=pl.Buffered(1))
-    slim = pl.BlockSpec((local, seqs * capacity, ff), lambda i: (0, i, 0))
+    slim = pl.BlockSpec((1, seqs * capacity, ff), lambda i: (0, i, 0))
     return pl.pallas_call(
         functools.partial(expert_out_kernel, capacity),
         out_shape=[
@@ -909,23 +1141,26 @@
             jax.ShapeDtypeStruct((local, groups, tok_rows, 1), f32),
         ],
         grid=(groups // seqs,),
-        in_specs=[slim, tok, route, column, weight],
+        in_specs=[slim] * local + [tok, route, column, weight],
         out_specs=[tok, column],
-        compiler_params=pltpu.CompilerParams(vmem_limit_bytes=60 << 20),
+        compiler_params=pltpu.CompilerParams(vmem_limit_bytes=kernel_vmem),
         cost_estimate=small_cost,
         name="expert_combine",
-    )(act, cot_all, slot_of[:, :, None, :], gates[:, :, :, None], w_down)
-
-
-def expert_back_kernel(capacity, gr_ref, g_ref, u_ref, slot_ref, wg_ref, wu_ref, wd_ref, gg_ref, gu_ref, part_ref):
+    )(*acts, cot_all, slot_of[:, :, None, :], gates[:, :, :, None], w_down)
+
+
+def expert_back_kernel(capacity, *refs):
+    local = (len(refs) - 7) // 3
+    gr_refs, g_refs, u_refs = (refs[i * local : (i + 1) * local] for i in range(3))
+    slot_ref, wg_ref, wu_ref, wd_ref, gg_ref, gu_ref, part_ref = refs[3 * local :]
     seqs = part_ref.shape[0]
     parts = [None] * seqs
     for j in range(wd_ref.shape[0]):
-        grad_act = dot(gr_ref[j], wd_ref[j], 1, 1)
-        gate_in = g_ref[j]
+        grad_act = dot(gr_refs[j][0], wd_ref[j], 1, 1)
+        gate_in = g_refs[j][0]
         sigma = jax.nn.sigmoid(gate_in)
         grad_up = (grad_act * (gate_in * sigma)).astype(bf16)
-        grad_gate = (grad_act * u_ref[j] * sigma * (1.0 + gate_in * (1.0 - sigma))).astype(bf16)
+        grad_gate = (grad_act * u_refs[j][0] * sigma * (1.0 + gate_in * (1.0 - sigma))).astype(bf16)
         gg_ref[j] = grad_gate
         gu_ref[j] = grad_up
         rows = dot(grad_gate, wg_ref[j], 1, 1) + dot(grad_up, wu_ref[j], 1, 1)
@@ -947,7 +1182,8 @@
     once = pl.Buffered(1)
     weight = pl.BlockSpec((local, width, ff), lambda i: (0, 0, 0), pipeline_mode=once)
     down = pl.BlockSpec((local, ff, width), lambda i: (0, 0, 0), pipeline_mode=once)
-    wide = pl.BlockSpec((local, slots, width), lambda i: (0, i, 0))
+    wide = pl.BlockSpec((1, slots, width), lambda i: (0, i, 0))
+    one = pl.BlockSpec((1, slots, ff), lambda i: (0, i, 0))
     slim = pl.BlockSpec((local, slots, ff), lambda i: (0, i, 0))
     return pl.pallas_call(
         functools.partial(expert_back_kernel, capacity),
@@ -957,12 +1193,34 @@
             jax.ShapeDtypeStruct((groups, tok_rows, width), bf16),
         ],
         grid=(groups // seqs,),
-        in_specs=[wide, slim, slim, route, weight, weight, down],
+        in_specs=[wide] * local + [one] * (2 * local) + [route, weight, weight, down],
         out_specs=[slim, slim, tok],
-        compiler_params=pltpu.CompilerParams(vmem_limit_bytes=63 << 20),
+        compiler_params=pltpu.CompilerParams(vmem_limit_bytes=kernel_vmem),
         cost_estimate=small_cost,
         name="expert_back",
-    )(grad_recv, gate_in, up_in, slot_of[:, :, None, :], w_gate, w_up, w_down)
+    )(*grad_recv, *gate_in, *up_in, slot_of[:, :, None, :], w_gate, w_up, w_down)
+
+
+def assemble_kernel(x_ref, *outs):
+    wide = x_ref.shape[3] // 4
+    for i, out in enumerate(outs):
+        for s in range(x_ref.shape[1]):
+            out[:, s * wide : (s + 1) * wide] = x_ref[0, s, :, i * wide : (i + 1) * wide].astype(f32)
+
+
+def assemble(x):
+    shares, blocks, rows, columns = x.shape
+    width = blocks * columns // 4
+    return pl.pallas_call(
+        assemble_kernel,
+        out_shape=[jax.ShapeDtypeStruct((shares * rows, width), f32)] * 4,
+        grid=(shares,),
+        in_specs=[pl.BlockSpec((1, blocks, rows, columns), lambda p: (p, 0, 0, 0))],
+        out_specs=[pl.BlockSpec((rows, width), lambda p: (p, 0))] * 4,
+        compiler_params=pltpu.CompilerParams(vmem_limit_bytes=kernel_vmem),
+        cost_estimate=small_cost,
+        name="assemble",
+    )(x)
 
 
 def pad_rows(flat, tile):
@@ -1014,12 +1272,6 @@
     def blocks_to_deal(values):
         return values.reshape(replicas, block_rows, width)[inverse_order]
 
-    def undeal(values):
-        back = lax.all_to_all(
-            values.reshape(replicas, block_rows, width), "dp", split_axis=0, concat_axis=0, tiled=True
-        )
-        return back[order_row].reshape(tok_rows, width)
-
     small = jnp.concatenate(
         [w_router.reshape(-1), attn_gain, mlp_gain, query_gain, key_gain]
     )
@@ -1054,25 +1306,32 @@
     live_all = (positions[None, :] < lengths_all[:, None]).astype(f32)
     live_rows = (positions < lengths[0]).astype(f32)
 
-    wo_full = lax.all_gather(w_out, "expert", axis=0, tiled=True)
-
     inputs = seq_tokens.astype(f32)
     normed, inv_first = norm_fwd(inputs, attn_g)
     attn_in = normed.astype(bf16)
-    attn_all, seq_cot = gather_rows(attn_in, groups, 1, blocks=blocks_to_deal(cotangent))
+    attn_all, seq_cot = gather_rows(
+        attn_in, groups, replicas, 1, riders=[Deal(blocks_to_deal(cotangent), groups, replicas)]
+    )
     grad_output = seq_cot.astype(f32) * live_rows[:, None]
     cot_all = lax.all_gather(grad_output.astype(bf16), "expert", axis=0, tiled=False)
 
     cosine, signed_sine = rotary_tables(tok_rows, head_dim)
-    mixed = attend(lengths_all, attn_all, w_qkv, query_g, key_g, cosine, signed_sine)
-    mixed_here = lax.all_to_all(mixed, "expert", split_axis=0, concat_axis=0, tiled=True)
-    hidden = inputs + einf("xtm,xmd->td", mixed_here, wo_full.reshape(groups, local_width, width))
+    mixed, hidden_part = attend(
+        lengths_all, attn_all, w_qkv, w_out, query_g, key_g, cosine, signed_sine
+    )
+    hidden = inputs + scatter_sum(hidden_part, groups, replicas, 8)[0]
     mlp_normed, inv_second = norm_fwd(hidden, mlp_g)
     mlp_in = mlp_normed.astype(bf16)
-    mlp_all = gather_rows(mlp_in, groups, 2)
-
-    logits = einf("std,de->ste", mlp_all, router_full)
-    router = jax.nn.softmax(logits, axis=-1)
+    logits = einf("td,de->te", mlp_in, router_full)
+    my_router = jax.nn.softmax(logits, axis=-1)
+    mlp_all, router = gather_rows(
+        mlp_in,
+        groups,
+        replicas,
+        2,
+        riders=[SmallGather(pad_rows(my_router.reshape(-1), 8), groups, replicas)],
+    )
+    router = router.reshape(groups, -1)[:, : tok_rows * experts].reshape(groups, tok_rows, experts)
     expert_ids = jnp.arange(experts, dtype=jnp.int32)
     picked = jnp.sum(
         (routes_all[:, :, :, None] == expert_ids).astype(f32), axis=2
@@ -1092,30 +1351,33 @@
     own_picked = own_picked.transpose(2, 0, 1)
     own_gates = own_gates.transpose(2, 0, 1)
     slot_of = jnp.where(own_picked > 0.5, rank.astype(jnp.int32), -1)
-    expert_in, grad_recv, act_low, gate_in, up_in = expert_forward(
-        mlp_all, cot_all, slot_of, own_gates, w_gate, w_up, capacity
-    )
-    grad_down_w = einf("jrf,jrd->jfd", act_low, grad_recv)
-    act_low, grad_recv, grad_down_w = lax.optimization_barrier(
-        (act_low, grad_recv, grad_down_w.astype(bf16))
-    )
-    total_down = lax.psum_scatter(grad_down_w, "dp", scatter_dimension=1, tiled=True).astype(f32)
+    expert_in, grad_recv, act_low, gate_in, up_in, total_down = [], [], [], [], [], []
+    for j in range(local_experts):
+        taken, recv, act, gate, up = expert_forward(
+            mlp_all, cot_all, slot_of, own_gates, w_gate, w_up, capacity, j
+        )
+        grad_down_w = einf("rf,rd->fd", act[0], recv[0]).astype(bf16)
+        act, recv, mlp_all, grad_down_w = lax.optimization_barrier((act, recv, mlp_all, grad_down_w))
+        total_down.append(lax.psum_scatter(grad_down_w, "dp", scatter_dimension=0, tiled=True))
+        for values, value in zip(
+            (expert_in, grad_recv, act_low, gate_in, up_in), (taken, recv, act, gate, up)
+        ):
+            values.append(value)
     grad_gate_in, grad_up_in, grad_part = expert_back(
         grad_recv, gate_in, up_in, slot_of, w_gate, w_up, w_down, groups, tok_rows, capacity
     )
-    grad_gate_w = einf("jrd,jrf->jdf", expert_in, grad_gate_in)
-    grad_up_w = einf("jrd,jrf->jdf", expert_in, grad_up_in)
-    grad_part, act_low, grad_gate_w, grad_up_w = lax.optimization_barrier(
-        (grad_part, act_low, grad_gate_w.astype(bf16), grad_up_w.astype(bf16))
-    )
-    total_gate, total_up = (
-        lax.psum_scatter(value, "dp", scatter_dimension=1, tiled=True).astype(f32)
-        for value in (grad_gate_w, grad_up_w)
-    )
+    expert_in = jnp.concatenate(expert_in, axis=0)
+    grad_gate_w = einf("jrd,jrf->jdf", expert_in, grad_gate_in).astype(bf16)
+    grad_part, act_low, grad_gate_w = lax.optimization_barrier((grad_part, act_low, grad_gate_w))
+    total_gate = lax.psum_scatter(grad_gate_w, "dp", scatter_dimension=1, tiled=True)
     sum_part, own_grad_gates = expert_combine(act_low, cot_all, slot_of, own_gates, w_down, capacity)
     gate_rows = own_grad_gates.transpose(1, 0, 2, 3).reshape(groups, -1, 128)
     grad_mlp_in, gate_back, sums = scatter_sum(
-        grad_part, groups, 3, replicas=replicas, riders=(gate_rows, stats)
+        grad_part,
+        groups,
+        replicas,
+        3,
+        riders=[Exchange(gate_rows, groups, replicas), DpSum(stats, groups, replicas)],
     )
     sums = sums.reshape(-1)
     counts, prob_sums = sums[:experts], sums[experts : 2 * experts]
@@ -1124,7 +1386,6 @@
     balance_loss = balance_coef * (experts * jnp.sum(fraction * prob_sums / total_slots))
 
     grad_gates = gate_back.reshape(experts, tok_rows).T
-    my_router = lax.dynamic_index_in_dim(router, me, 0, keepdims=False)
     my_picked = lax.dynamic_index_in_dim(picked, me, 0, keepdims=False)
     my_gates = lax.dynamic_index_in_dim(gates, me, 0, keepdims=False)
     my_sum = lax.dynamic_index_in_dim(chosen_sum, me, 0, keepdims=False)
@@ -1142,53 +1403,57 @@
     grad_hidden = grad_output + grad_hidden_norm
     grad_hidden_low = grad_hidden.astype(bf16)
     grad_hidden_low, total_down = lax.optimization_barrier((grad_hidden_low, total_down))
-    hidden_all = gather_rows(grad_hidden_low, groups, 4)
-    grad_attn_part, grad_qkv_w, grad_out_w, grad_gains = attend_back(
+    (hidden_all,) = gather_rows(grad_hidden_low, groups, replicas, 4)
+    grad_attn_part, grad_attn_w, grad_gains = attend_back(
         lengths_all, attn_all, hidden_all, mixed, w_qkv, w_out, query_g, key_g, cosine, signed_sine
     )
     grad_query_g, grad_key_g = grad_gains[0], grad_gains[1]
-    grad_attn_in = scatter_sum(grad_attn_part, groups, 5)
-    w_back = lax.all_to_all(
-        grad_qkv_w.reshape(groups, shard_rows, 3 * local_width),
-        "expert",
-        split_axis=0,
-        concat_axis=0,
-        tiled=True,
-    )
-    attn_w = jnp.concatenate(
-        [
-            w_back[:, :, i * local_width : (i + 1) * local_width]
-            .transpose(1, 0, 2)
-            .reshape(shard_rows, groups * local_width)
-            for i in range(3)
-        ]
-        + [grad_out_w],
-        axis=0,
-    )
-    attn_w, total_up = lax.optimization_barrier((attn_w, total_up))
-    attn_sum = lax.psum(attn_w, "dp").astype(f32)
-    sum_q, sum_k, sum_v, sum_o = (
-        attn_sum[i * shard_rows : (i + 1) * shard_rows] for i in range(4)
-    )
-
-    grad_attn_in, total_gate = lax.optimization_barrier((grad_attn_in, total_gate))
+    attn_share = lax.psum_scatter(
+        grad_attn_w.reshape(groups, shard_rows, 4 * local_width), "dp", scatter_dimension=1, tiled=True
+    )
+    sum_part, grad_attn_part = lax.optimization_barrier((sum_part, grad_attn_part))
+    (expert_sum,) = scatter_sum(sum_part, groups, replicas, 6)
+    out_seq = (live_rows[:, None] * (hidden + expert_sum)).astype(bf16)
+
+    def to_deal(values):
+        return values.reshape(replicas, block_rows, width)
+
+    grad_up_in, grad_attn_part, out_seq, total_gate = lax.optimization_barrier(
+        (grad_up_in, grad_attn_part, out_seq, total_gate)
+    )
+    grad_up_w = einf("jrd,jrf->jdf", expert_in, grad_up_in).astype(bf16)
+    grad_up_w, grad_attn_part = lax.optimization_barrier((grad_up_w, grad_attn_part))
+    grad_attn_in, out_home = scatter_sum(
+        grad_attn_part, groups, replicas, 5, riders=[Deal(to_deal(out_seq), groups, replicas)]
+    )
+    grad_attn_in, attn_share = lax.optimization_barrier((grad_attn_in, attn_share))
     grad_input_norm, grad_attn_g = norm_back(inputs, inv_first, attn_g, grad_attn_in, 0)
-    grad_input = undeal((grad_hidden + grad_input_norm).astype(bf16)).astype(f32)
-
-    sum_part, grad_input = lax.optimization_barrier((sum_part, grad_input))
-    expert_sum = scatter_sum(sum_part, groups, 6)
-    output = undeal((live_rows[:, None] * (hidden + expert_sum)).astype(bf16))
+    grad_seq = (grad_hidden + grad_input_norm).astype(bf16)
 
     pieces = [grad_router_w.reshape(groups, n_router)] + [
         value.reshape(groups, -1) for value in (grad_attn_g, grad_mlp_g, grad_query_g, grad_key_g)
     ]
     pieces = jnp.concatenate(pieces, axis=1)
-    n_small = pieces.shape[1]
-    pad = -n_small % 1024
+    pad = -pieces.shape[1] % 1024
     pieces = jnp.pad(pieces, ((0, 0), (0, pad))).reshape(groups, -1, 128)
-    sum_small = small_sum(pieces, replicas, 7).reshape(-1)
+
+    attn_sum, total_up, sum_small, grad_home = close(
+        attn_share,
+        3 * local_width,
+        grad_up_w,
+        groups,
+        replicas,
+        7,
+        [SmallSum(pieces, groups, replicas), Deal(to_deal(grad_seq), groups, replicas)],
+    )
+    grad_input = to_deal(grad_home)[order_row].reshape(tok_rows, width).astype(f32)
+    output = to_deal(out_home)[order_row].reshape(tok_rows, width)
+    sum_q, sum_k, sum_v, sum_o = assemble(attn_sum)
+    sum_small = sum_small.reshape(-1)
     sum_r = sum_small[:n_router].reshape(shard_rows, experts)
     sum_ga, sum_gm, sum_gq, sum_gk = (sum_small[cuts[i] : cuts[i + 1]] for i in range(1, 5))
+    total_down = jnp.stack(total_down).astype(f32)
+    total_gate = total_gate.astype(f32)
     return (
         output,
         balance_loss,

time: 968 us -> 926 us (0.957)
  Pallas kernels: 566 us -> 749 us
  waiting for transfers between devices: 196 us -> 15.4 us
  starting transfers between devices: 19.7 us -> 0.42 us
  matrix products: 69.3 us -> 56.3 us
    pallas_call x7 -> x9, Pallas kernels: 340 us -> 521 us  [the longest x8 515 us: riding_call(): pl.pallas_call(functools.partial(riding_kernel, n, replicas, main, counts...]
    reduce_scatter x3 -> x4, waiting for transfers between devices: 98.9 us -> 15.3 us  [the longest x1 15.3 us: body(): lax.psum_scatter(grad_attn_w.reshape(groups, shard_rows, 4 * local_width)...]
    all_to_all x4 -> x0, waiting for transfers between devices: 62.9 us -> none  [the longest x2 37.9 us: undeal(): lax.all_to_all(values.reshape(replicas, block_rows, width), 'dp', split_a...]
    psum x1 -> x0, waiting for transfers between devices: 33 us -> none  [body(): attn_sum = lax.psum(attn_w, 'dp').astype(f32)]
    all_to_all x4 -> x0, starting transfers between devices: 19.5 us -> none  [the longest x2 10.7 us: undeal(): lax.all_to_all(values.reshape(replicas, block_rows, width), 'dp', split_a...]
    dot_general x8, matrix products: 69.3 us -> 56.3 us  [einf(): return jnp.einsum(spec, left, right, preferred_element_type=f32)]
    pallas_call x1, Pallas kernels: 54.5 us -> 43.2 us  [front(): pl.pallas_call(functools.partial(front_kernel, n, replicas), out_shape=[j...]
    unnamed x120 -> x57, local copies, waits for them, and re-layouts: 25.1 us -> 17 us
  transfers between devices with their start and end apart: 10 -> 5, of which waited for: 4 -> 1; matrix products, arithmetic and copies ran while one was open for 12% -> 9% of each run, Pallas kernels for 55% -> 47%
where the time goes in v4:
time: 926 us; the launch traced here: 921 us
  Pallas kernels  749 us (81%)
  matrix products  56.3 us (6%)
  local copies, waits for them, and re-layouts  49 us (5%)
  other arithmetic  32.1 us (3%)
  between operations  18.5 us (2%)
  waiting for transfers between devices  15.4 us (2%)
    pallas_call x8, Pallas kernels, riding_call(): pl.pallas_call(functools.partial(riding_kernel, n, replicas, main, counts...  515 us
    dot_general x8, matrix products, einf(): return jnp.einsum(spec, left, right, preferred_element_type=f32)  56.3 us
    pallas_call x1, Pallas kernels, expert_back(): pl.pallas_call(functools.partial(expert_back_kernel, capacity), out_shape...  48.9 us
    pallas_call x1, Pallas kernels, attend_back(): pl.pallas_call(functools.partial(attend_back_kernel, wide // head_dim, he...  46.5 us
    pallas_call x1, Pallas kernels, front(): pl.pallas_call(functools.partial(front_kernel, n, replicas), out_shape=[j...  43.2 us
    pallas_call x2, Pallas kernels, expert_forward(): pl.pallas_call(functools.partial(expert_in_kernel, capacity), out_shape=[...  42.6 us
    pallas_call x1, Pallas kernels, attend(): pl.pallas_call(functools.partial(attend_kernel, wide // head_dim, head_di...  24.1 us
    pallas_call x1, Pallas kernels, expert_combine(): pl.pallas_call(functools.partial(expert_out_kernel, capacity), out_shape=...  23.4 us
  transfers between devices with their start and end apart: 5, of which 1 were waited for; matrix products, arithmetic and copies ran while one was open for 9% of the time, Pallas kernels for 47%

profile of v4, /device:TPU:0, one launch (start us, length us, event | category | flops | bytes accessed | tf_op | source)
XLA Modules:
  0.0 921.1 jit_solution(17338019670415008220)
XLA Ops:
  8.0 0.9 dynamic-slice_reduce_fusion
  9.0 0.8 copy.71
  10.0 2.8 concatenate.21
  13.3 0.8 copy.72
  14.3 1.6 gather_fusion.1
  15.8 1.6 gather_fusion
  18.0 43.2 %front.1 = (bf16[8,48,128]{2,1,0:T(8,128)(2,1)}, s32[8,24,128]{2,1,0:T(8,128)}, bf16[256,2048]{1,0:T(8,128)(2,1)}, bf16[8,256,768]{2,1,0:T(8,128)(2,1)}) custom-call(bf16[48,128]{1,0:T(8,128)(2,1)} %pad_bitcast_fusion.1.small, s32[24,128]{1,0:T(8,128)} %select_bitcast_fusion.ints, bf16[4,64,2048]{2,1,0:T(8,128)(2,1)} %gather_fusion, bf16[256,2048]{1,0:T(8,128)(2,1)} %wq.1, ...), custom_call_target="tpu_custom_call" | custom-call | bytes 1024 | tf_op jit(solution)/shard_map/front/pallas_call | solution.py:191
  61.2 0.9 copy.107
  62.2 1.5 fusion.20
  63.7 2.5 fusion.14.refs_0_
  66.2 42.5 %gather_rows_1.1 = (bf16[8,256,2048]{2,1,0:T(8,128)(2,1)}, bf16[256,2048]{1,0:T(8,128)(2,1)}) custom-call(bf16[256,2048]{1,0:T(8,128)(2,1)} %fusion.14.refs_0_, bf16[4,64,2048]{2,1,0:T(8,128)(2,1)} %gather_fusion.1), custom_call_target="tpu_custom_call" | custom-call | bytes 1024 | tf_op jit(solution)/shard_map/gather_rows_1/pallas_call | solution.py:591
  108.8 2.5 fusion.24
  113.9 0.6 slice_reduce_fusion.lengths_ref
  115.1 0.8 pad_maximum_fusion
  115.9 24.1 %attend.1 = (bf16[8,256,256]{2,1,0:T(8,128)(2,1)}, bf16[8,256,2048]{2,1,0:T(8,128)(2,1)}) custom-call(s32[8]{0:T(128)} %slice_reduce_fusion.lengths_ref, bf16[8,256,2048]{2,1,0:T(8,128)(2,1)} %get-tuple-element.83.x_ref, bf16[2048,768]{1,0:T(8,128)(2,1)} %bitcast.145, bf16[256,2048]{1,0:T(8,128)(2,1)} %wo_ref.3, f32[1,128]{1,0:T(1,128)} %reshape.315.qg_ref, ...), custom_call_target="tpu_custom_call" | custom-call | bytes 1024 | tf_op jit(solution)/shard_map/attend/pallas_call | solution.py:903
  140.0 59.7 %scatter_sum_8.1 = f32[256,2048]{1,0:T(8,128)} custom-call(bf16[8,256,2048]{2,1,0:T(8,128)(2,1)} %get-tuple-element.85.refs_0_), custom_call_target="tpu_custom_call" | custom-call | bytes 1024 | tf_op jit(solution)/shard_map/scatter_sum_8/pallas_call | solution.py:591
  199.7 1.9 multiply_reduce_fusion.2
  203.5 0.7 reshape.297.refs_1_
  204.2 43.1 %gather_rows_2.1 = (bf16[8,256,2048]{2,1,0:T(8,128)(2,1)}, f32[8,32,128]{2,1,0:T(8,128)}) custom-call(bf16[256,2048]{1,0:T(8,128)(2,1)} %copy-done.6, f32[32,128]{1,0:T(8,128)} %reshape.297.refs_1_), custom_call_target="tpu_custom_call" | custom-call | bytes 1024 | tf_op jit(solution)/shard_map/gather_rows_2/pallas_call | solution.py:591
  247.3 1.2 reshape_reshape.3
  249.3 0.7 broadcast_in_dim.15.slot_ref.refs_6_.refs_3_
  250.6 21.5 %expert_forward.2 = (bf16[1,1152,2048]{2,1,0:T(8,128)(2,1)}, bf16[1,1152,2048]{2,1,0:T(8,128)(2,1)}, bf16[1,1152,1024]{2,1,0:T(8,128)(2,1)}, f32[1,1152,1024]{2,1,0:T(8,128)}, f32[1,1152,1024]{2,1,0:T(8,128)}) custom-call(bf16[8,256,2048]{2,1,0:T(8,128)(2,1)} %get-tuple-element.92.x_ref, bf16[8,256,2048]{2,1,0:T(8,128)(2,1)} %bitcast.142, ...), custom_call_target="tpu_custom_call" | custom-call | bytes 1024 | tf_op jit(solution)/shard_map/expert_forward/pallas_call | solution.py:1094
  272.1 9.6 %fusion.4 = bf16[1024,2048]{1,0:T(8,128)(2,1)} fusion(bf16[1,1152,2048]{2,1,0:T(8,128)(2,1)} %get-tuple-element.94.refs_0_, bf16[1,1152,1024]{2,1,0:T(8,128)(2,1)} %get-tuple-element.107.refs_0_), kind=kOutput, calls=%fused_computation.15 | convolution fusion | flops 4833935360 | bytes 11272192 | tf_op jit(solution)/shard_map/rf,rd->fd/dot_general | solution.py:1232
  281.8 21.1 %expert_forward.3 = (bf16[1,1152,2048]{2,1,0:T(8,128)(2,1)}, bf16[1,1152,2048]{2,1,0:T(8,128)(2,1)}, bf16[1,1152,1024]{2,1,0:T(8,128)(2,1)}, f32[1,1152,1024]{2,1,0:T(8,128)}, f32[1,1152,1024]{2,1,0:T(8,128)}) custom-call(bf16[8,256,2048]{2,1,0:T(8,128)(2,1)} %get-tuple-element.92.x_ref, bf16[8,256,2048]{2,1,0:T(8,128)(2,1)} %bitcast.143, ...), custom_call_target="tpu_custom_call" | custom-call | bytes 1024 | tf_op jit(solution)/shard_map/expert_forward/pallas_call | solution.py:1094
  302.9 9.6 %fusion.7 = bf16[1024,2048]{1,0:T(8,128)(2,1)} fusion(bf16[1,1152,2048]{2,1,0:T(8,128)(2,1)} %get-tuple-element.97.refs_1_, bf16[1,1152,1024]{2,1,0:T(8,128)(2,1)} %get-tuple-element.108.refs_1_), kind=kOutput, calls=%fused_computation.16 | convolution fusion | flops 4833935360 | bytes 11272192 | tf_op jit(solution)/shard_map/rf,rd->fd/dot_general | solution.py:1232
  312.6 48.9 %expert_back.1 = (bf16[2,1152,1024]{2,1,0:T(8,128)(2,1)}, bf16[2,1152,1024]{2,1,0:T(8,128)(2,1)}, bf16[8,256,2048]{2,1,0:T(8,128)(2,1)}) custom-call(bf16[1,1152,2048]{2,1,0:T(8,128)(2,1)} %get-tuple-element.94.refs_0_, bf16[1,1152,2048]{2,1,0:T(8,128)(2,1)} %get-tuple-element.97.refs_1_, f32[1,1152,1024]{2,1,0:T(8,128)} %get-tuple-element.98.refs_2_, ...), custom_call_target="tpu_custom_call" | custom-call | bytes 1024 | tf_op jit(solution)/shard_map/expert_back/pallas_call | solution.py:1188
  361.5 2.7 constant_dynamic-update-slice_fusion.1
  364.2 2.7 constant_dynamic-update-slice_fusion
  366.9 3.9 copy-done.11
  370.8 15.4 %convolution_convert_fusion.1 = bf16[2,2048,1024]{2,1,0:T(8,128)(2,1)} fusion(bf16[2,1152,2048]{2,1,0:T(8,128)(2,1)S(1)} %constant_dynamic-update-slice_fusion, bf16[2,1152,1024]{2,1,0:T(8,128)(2,1)} %get-tuple-element.106), kind=kOutput, calls=%fused_computation.5 | convolution fusion | flops 9667870720 | bytes 22544384 | tf_op jit(solution)/shard_map/jrd,jrf->jdf/dot_general | solution.py:1232
  388.0 2.0 copy.79.refs_4_
  390.1 0.7 fusion.38
  390.9 1.3 fusion.37.refs_2_
  392.2 23.4 %expert_combine.1 = (bf16[8,256,2048]{2,1,0:T(8,128)(2,1)}, f32[2,8,256,1]{3,2,1,0:T(8,128)}) custom-call(bf16[1,1152,1024]{2,1,0:T(8,128)(2,1)} %get-tuple-element.107.refs_0_, bf16[1,1152,1024]{2,1,0:T(8,128)(2,1)} %get-tuple-element.108.refs_1_, bf16[8,256,2048]{2,1,0:T(8,128)(2,1)} %bitcast.144, ...), custom_call_target="tpu_custom_call" | custom-call | bytes 1024 | tf_op jit(solution)/shard_map/expert_combine/pallas_call | solution.py:1137
  415.6 2.2 copy.80
  417.8 0.6 reshape.298.refs_1_
  418.4 43.9 %scatter_sum_3.1 = (f32[256,2048]{1,0:T(8,128)}, f32[8,4,128]{2,1,0:T(4,128)}, f32[8,128]{1,0:T(8,128)}) custom-call(bf16[8,256,2048]{2,1,0:T(8,128)(2,1)} %get-tuple-element.110.refs_0_, f32[8,4,128]{2,1,0:T(4,128)} %reshape.298.refs_1_, f32[8,128]{1,0:T(8,128)} %fusion.37.refs_2_), custom_call_target="tpu_custom_call" | custom-call | bytes 1024 | tf_op jit(solution)/shard_map/scatter_sum_3/pallas_call | solution.py:591
  462.4 1.3 slice.66
  463.6 0.7 reshape.300
  465.0 1.4 multiply_reduce_fusion.6
  466.6 3.3 multiply_reduce_fusion
  469.9 2.4 fusion.45
  472.3 40.3 %gather_rows_4.1.g_ref = bf16[8,256,2048]{2,1,0:T(8,128)(2,1)} custom-call(bf16[256,2048]{1,0:T(8,128)(2,1)} %get-tuple-element.117.refs_0_), custom_call_target="tpu_custom_call" | custom-call | bytes 1024 | tf_op jit(solution)/shard_map/gather_rows_4/pallas_call | solution.py:591
  512.7 46.5 %attend_back.1 = (bf16[8,256,2048]{2,1,0:T(8,128)(2,1)}, bf16[2048,1024]{1,0:T(8,128)(2,1)}, f32[8,128]{1,0:T(8,128)}) custom-call(s32[8]{0:T(128)} %slice_reduce_fusion.lengths_ref, bf16[8,256,2048]{2,1,0:T(8,128)(2,1)} %get-tuple-element.83.x_ref, bf16[8,256,2048]{2,1,0:T(8,128)(2,1)} %gather_rows_4.1.g_ref, ...), custom_call_target="tpu_custom_call" | custom-call | bytes 1024 | tf_op jit(solution)/shard_map/attend_back/pallas_call | solution.py:1013
  561.5 0.8 slice_reduce_fusion.1
  562.5 41.2 %scatter_sum_6.1 = f32[256,2048]{1,0:T(8,128)} custom-call(bf16[8,256,2048]{2,1,0:T(8,128)(2,1)} %get-tuple-element.121.refs_0_), custom_call_target="tpu_custom_call" | custom-call | bytes 1024 | tf_op jit(solution)/shard_map/scatter_sum_6/pallas_call | solution.py:591
  603.7 4.0 maximum_convert_fusion
  607.7 1.2 multiply_convert_fusion
  608.9 17.3 %convolution_convert_fusion.refs_1_ = bf16[2,2048,1024]{2,1,0:T(8,128)(2,1)} fusion(bf16[2,1152,2048]{2,1,0:T(8,128)(2,1)} %copy-done.11, bf16[2,1152,1024]{2,1,0:T(8,128)(2,1)} %get-tuple-element.123), kind=kOutput, calls=%fused_computation.4 | convolution fusion | flops 9667870720 | bytes 22544384 | tf_op jit(solution)/shard_map/jrd,jrf->jdf/dot_general | solution.py:1232
  626.2 42.2 %scatter_sum_5.1 = (f32[256,2048]{1,0:T(8,128)}, bf16[256,2048]{1,0:T(8,128)(2,1)}) custom-call(bf16[8,256,2048]{2,1,0:T(8,128)(2,1)} %get-tuple-element.125.refs_0_, bf16[4,64,2048]{2,1,0:T(8,128)(2,1)} %bitcast.148), custom_call_target="tpu_custom_call" | custom-call | bytes 1024 | tf_op jit(solution)/shard_map/scatter_sum_5/pallas_call | solution.py:591
  668.4 15.3 %reduce-scatter.11.cloned.1.call-done.refs_0_ = bf16[8,64,1024]{2,1,0:T(8,128)(2,1)} async-done(((bf16[8,256,1024]{2,1,0:T(8,128)(2,1)}), bf16[8,64,1024]{2,1,0:T(8,128)(2,1)}) %reduce-scatter.11.cloned.1.call-update) | async-done | bytes 1048592 | tf_op jit(solution)/shard_map/reduce_scatter | solution.py:1411
  683.6 2.1 fusion.23
  685.9 0.7 copy.106
  686.6 3.2 fusion.19
  689.8 202.0 %close.1 = (bf16[4,8,64,1024]{3,2,1,0:T(8,128)(2,1)}, f32[2,512,1024]{2,1,0:T(8,128)}, f32[40,128]{1,0:T(8,128)}, bf16[256,2048]{1,0:T(8,128)(2,1)}) custom-call(bf16[8,64,1024]{2,1,0:T(8,128)(2,1)} %reduce-scatter.11.cloned.1.call-done.refs_0_, bf16[2,2048,1024]{2,1,0:T(8,128)(2,1)} %convolution_convert_fusion.refs_1_, f32[8,40,128]{2,1,0:T(8,128)} %bitcast.157, ...), custom_call_target="tpu_custom_call" | custom-call | bytes 1024 | tf_op jit(solution)/shard_map/close/pallas_call | solution.py:591
  891.9 1.3 slice_bitcast_fusion
  893.2 0.7 slice.70
  893.9 1.6 gather_fusion.2
  896.2 1.4 fusion.46
  897.7 0.7 copy.84
  898.4 1.6 bitcast_convert_fusion
  900.0 2.5 convert_element_type.189
  902.5 5.9 assemble.1
  908.3 4.9 copy.113
  (121 shorter events, 12.1 us)
Async XLA Ops:
  7.2 7.1 copy-start
  7.2 8.7 copy-start.13
  7.2 243.4 %all-gather.3.cloned.1.call-start = ((), (), s32[]{:S(2)}) async-start(), calls=%async_computation.8 | async-start | bytes 9437184 | tf_op jit(solution)/shard_map/all_gather | solution.py:1316
  63.7 45.1 %copy-start.20 = (f32[256]{0:T(256)}, f32[256]{0:T(256)S(1)}, u32[]{:S(2)}) copy-start(f32[256]{0:T(256)S(1)} %add_rsqrt_fusion.1) | copy-start | bytes 3076
  63.7 45.0 %copy-start.17 = (f32[1,2,8,128]{3,1,2,0:T(2,128)}, f32[1,2,8,128]{3,1,2,0:T(2,128)S(1)}, u32[]{:S(2)}) copy-start(f32[1,2,8,128]{3,1,2,0:T(2,128)S(1)} %copy.93) | copy-start | bytes 24580
  108.7 2.6 copy-start.19
  111.2 361.1 %reduce-scatter.5.cloned.1.call-start = ((), (), s32[]{:S(2)}) async-start(), calls=%async_computation.4 | async-start | bytes 5242880 | tf_op jit(solution)/shard_map/reduce_scatter | solution.py:1361
  140.0 59.7 %copy-start.5 = (bf16[256,2048]{1,0:T(8,128)(2,1)S(1)}, bf16[256,2048]{1,0:T(8,128)(2,1)}, u32[]{:S(2)}) copy-start(bf16[256,2048]{1,0:T(8,128)(2,1)} %get-tuple-element.80) | copy-start | bytes 3145732
  201.7 1.3 copy-start.2
  202.0 1.4 copy-start.6
  281.7 190.6 %reduce-scatter.7.cloned.1.call-start = ((), (), s32[]{:S(2)}) async-start(), calls=%async_computation.5 | async-start | bytes 5242880 | tf_op jit(solution)/shard_map/reduce_scatter | solution.py:1361
  312.5 296.3 %reduce-scatter.9.cloned.1.call-start = ((), (), s32[]{:S(2)}) async-start(), calls=%async_computation.6 | async-start | bytes 10485760 | tf_op jit(solution)/shard_map/reduce_scatter | solution.py:1372
  366.9 3.9 copy-start.11
  386.2 0.9 copy-start.22
  386.2 1.7 copy-start.16
  386.3 297.4 %reduce-scatter.11.cloned.1.call-start = ((), (), s32[]{:S(2)}) async-start(), calls=%async_computation.7 | async-start | bytes 5242880 | tf_op jit(solution)/shard_map/reduce_scatter | solution.py:1411
  466.6 3.3 copy-start.3
  466.6 3.3 copy-start.10
  559.1 1.2 copy-start.7
  603.6 4.0 copy-start.4
  603.7 4.0 copy-start.9
  626.2 57.5 %copy-start.18 = (f32[1,2,8,128]{3,1,2,0:T(2,128)S(1)}, f32[1,2,8,128]{3,1,2,0:T(2,128)}, u32[]{:S(2)}) copy-start(f32[1,2,8,128]{3,1,2,0:T(2,128)} %copy-done.17) | copy-start | bytes 24580
  626.2 57.5 %copy-start.21 = (f32[256]{0:T(256)S(1)}, f32[256]{0:T(256)}, u32[]{:S(2)}) copy-start(f32[256]{0:T(256)} %copy-done.20) | copy-start | bytes 3076
  668.4 18.3 %copy-start.8 = (f32[256,2048]{1,0:T(8,128)S(1)}, f32[256,2048]{1,0:T(8,128)}, u32[]{:S(2)}) copy-start(f32[256,2048]{1,0:T(8,128)} %get-tuple-element.132) | copy-start | bytes 6291460
  689.8 204.1 %copy-start.14 = (bf16[256,2048]{1,0:T(8,128)(2,1)S(1)}, bf16[256,2048]{1,0:T(8,128)(2,1)}, u32[]{:S(2)}) copy-start(bf16[256,2048]{1,0:T(8,128)(2,1)} %get-tuple-element.127) | copy-start | bytes 3145732
  891.9 3.7 copy-start.15
  896.1 3.8 copy-start.12
  908.3 4.9 copy-start.1
Sparse Core Ops, SparseCore 0:
  111.4 72.0 all-gather.2
  281.8 76.8 reduce-scatter.4
  361.7 77.5 reduce-scatter.6
  441.5 144.9 reduce-scatter.8
  589.3 94.3 reduce-scatter.10

commit v5 on v4

--- a/solution.py
+++ b/solution.py
@@ -413,24 +413,26 @@
 
 
 class LineSum:
-    over_dp = True
-
-    def __init__(self, x, n, replicas, parts=4):
+    def __init__(self, values, n, replicas, parts=4):
         self.replicas, self.parts = replicas, parts
-        self.blocks, rows, columns = x.shape
+        self.blocks = len(values)
+        rows, columns = values[0].shape
         self.rows = rows // replicas
         self.size = self.rows // parts
         held = pltpu.VMEM((replicas, self.blocks, self.rows, columns), bf16)
-        self.ins = [(x, AWAY_SPEC)]
+        self.ins = [(x, AWAY_SPEC) for x in values]
         self.outs = [(jax.ShapeDtypeStruct((self.blocks, self.rows, columns), f32), VMEM_SPEC)]
         sems = DMA((2, replicas, parts))
-        self.scratch = [held, held, held, DMA((replicas, parts)), sems, sems]
-
-    def load(self, x, own, sem, c, p):
+        self.scratch = [held, held, held, DMA((self.blocks, replicas, parts)), sems, sems]
+
+    def loads(self, values, own, sem, c, p):
         rows = pl.ds(pl.multiple_of(c * self.rows + p * self.size, self.size), self.size)
-        return pltpu.make_async_copy(
-            x.at[:, rows], own.at[c, :, pl.ds(p * self.size, self.size)], sem.at[c, p]
-        )
+        return [
+            pltpu.make_async_copy(
+                x.at[rows], own.at[c, b, pl.ds(p * self.size, self.size)], sem.at[b, c, p]
+            )
+            for b, x in enumerate(values)
+        ]
 
     def hop(self, own, got, send, recv, way, c, p):
         here = lax.axis_index("dp")
@@ -458,12 +460,13 @@
                 else:
                     widen[b, rows] = widen[b, rows] + got[c, b, rows].astype(f32)
 
-    def start(self, me, x, out, own, up, down, loads, send, recv):
+    def start(self, values, own, sem):
         for t in range(self.replicas):
             for p in range(self.parts):
-                self.load(x, own, loads, t, p).start()
-
-    def steps(self, x, out, own, up, down, loads, send, recv):
+                for copy in self.loads(values, own, sem, t, p):
+                    copy.start()
+
+    def steps(self, values, out, own, up, down, sem, send, recv):
         here = lax.axis_index("dp")
         last = self.replicas - 1
         for t in range(last):
@@ -474,7 +477,8 @@
 
                     @pl.when(bound)
                     def _():
-                        self.load(x, own, loads, c, p).wait()
+                        for copy in self.loads(values, own, sem, c, p):
+                            copy.wait()
 
                         @pl.when(inner)
                         def _():
@@ -485,7 +489,8 @@
 
                 yield
         for p in range(self.parts):
-            self.load(x, own, loads, here, p).wait()
+            for copy in self.loads(values, own, sem, here, p):
+                copy.wait()
             self.add(own, None, here, p, out)
             for way, got, inner in ((0, up, here > 0), (1, down, here < last)):
 
@@ -503,14 +508,15 @@
                         self.hop(own, got, send, recv, way, c, p).wait_send()
 
 
-def close_kernel(exchange, gather, line, meet, share, x, full, out, rows, *refs):
+def close_kernel(exchange, gather, line, meet, share, *refs):
+    values, (full, out, rows), refs = refs[: line.blocks], refs[line.blocks :][:3], refs[line.blocks + 3 :]
     swap_refs, refs = refs[:2], refs[2:]
     gather_refs, line_refs = refs[: len(gather.scratch)], refs[len(gather.scratch) :]
     me = lax.axis_index("expert")
-    line.start(me, x, out, *line_refs)
+    line.start(values, line_refs[0], line_refs[3])
     meet(me)
     exchange.start(me, share, rows, *swap_refs)
-    running = [line.steps(x, out, *line_refs)]
+    running = [line.steps(values, out, *line_refs)]
     next(running[0])
     exchange.finish(me)
     gather.start(me, rows, full, *gather_refs)
@@ -1201,26 +1207,47 @@
     )(*grad_recv, *gate_in, *up_in, slot_of[:, :, None, :], w_gate, w_up, w_down)
 
 
-def assemble_kernel(x_ref, *outs):
+def assemble_kernel(
+    order_ref, x_ref, grad_ref, out_ref, last_ref, q_ref, k_ref, v_ref, o_ref, grad_input_ref, output_ref, up_ref
+):
     wide = x_ref.shape[3] // 4
-    for i, out in enumerate(outs):
+    for i, to in enumerate((q_ref, k_ref, v_ref, o_ref)):
         for s in range(x_ref.shape[1]):
-            out[:, s * wide : (s + 1) * wide] = x_ref[0, s, :, i * wide : (i + 1) * wide].astype(f32)
-
-
-def assemble(x):
+            to[:, s * wide : (s + 1) * wide] = x_ref[0, s, :, i * wide : (i + 1) * wide].astype(f32)
+    grad_input_ref[...] = grad_ref[0].astype(f32)
+    output_ref[...] = out_ref[0]
+    up_ref[...] = last_ref[...]
+
+
+def assemble(order_row, x, grad_home, out_home, last):
     shares, blocks, rows, columns = x.shape
-    width = blocks * columns // 4
+    _, dealt, width = grad_home.shape
+    local, up_rows, ff = last.shape
+    weight = jax.ShapeDtypeStruct((shares * rows, width), f32)
+    at = lambda p, order: (p, 0)
+    home = pl.BlockSpec((1, dealt, width), lambda p, order: (order[p], 0, 0))
+    part = up_rows // shares
     return pl.pallas_call(
         assemble_kernel,
-        out_shape=[jax.ShapeDtypeStruct((shares * rows, width), f32)] * 4,
-        grid=(shares,),
-        in_specs=[pl.BlockSpec((1, blocks, rows, columns), lambda p: (p, 0, 0, 0))],
-        out_specs=[pl.BlockSpec((rows, width), lambda p: (p, 0))] * 4,
+        out_shape=[weight] * 4
+        + [
+            jax.ShapeDtypeStruct((shares * dealt, width), f32),
+            jax.ShapeDtypeStruct((shares * dealt, width), bf16),
+            jax.ShapeDtypeStruct((local, up_rows, ff), f32),
+        ],
+        grid_spec=pltpu.PrefetchScalarGridSpec(
+            num_scalar_prefetch=1,
+            grid=(shares,),
+            in_specs=[pl.BlockSpec((1, blocks, rows, columns), lambda p, order: (p, 0, 0, 0)), home, home]
+            + [pl.BlockSpec((local, part, ff), lambda p, order: (0, p, 0))],
+            out_specs=[pl.BlockSpec((rows, width), at)] * 4
+            + [pl.BlockSpec((dealt, width), at)] * 2
+            + [pl.BlockSpec((local, part, ff), lambda p, order: (0, p, 0))],
+        ),
         compiler_params=pltpu.CompilerParams(vmem_limit_bytes=kernel_vmem),
         cost_estimate=small_cost,
         name="assemble",
-    )(x)
+    )(order_row, x, grad_home, out_home, last)
 
 
 def pad_rows(flat, tile):
@@ -1366,8 +1393,9 @@
     grad_gate_in, grad_up_in, grad_part = expert_back(
         grad_recv, gate_in, up_in, slot_of, w_gate, w_up, w_down, groups, tok_rows, capacity
     )
-    expert_in = jnp.concatenate(expert_in, axis=0)
-    grad_gate_w = einf("jrd,jrf->jdf", expert_in, grad_gate_in).astype(bf16)
+    grad_gate_w = jnp.stack(
+        [einf("rd,rf->df", expert_in[j][0], grad_gate_in[j]).astype(bf16) for j in range(local_experts)]
+    )
     grad_part, act_low, grad_gate_w = lax.optimization_barrier((grad_part, act_low, grad_gate_w))
     total_gate = lax.psum_scatter(grad_gate_w, "dp", scatter_dimension=1, tiled=True)
     sum_part, own_grad_gates = expert_combine(act_low, cot_all, slot_of, own_gates, w_down, capacity)
@@ -1418,15 +1446,16 @@
     def to_deal(values):
         return values.reshape(replicas, block_rows, width)
 
-    grad_up_in, grad_attn_part, out_seq, total_gate = lax.optimization_barrier(
-        (grad_up_in, grad_attn_part, out_seq, total_gate)
-    )
-    grad_up_w = einf("jrd,jrf->jdf", expert_in, grad_up_in).astype(bf16)
+    grad_up_in, out_seq, total_gate = lax.optimization_barrier((grad_up_in, out_seq, total_gate))
+    total_gate = total_gate.astype(f32)
+    total_gate, grad_attn_part = lax.optimization_barrier((total_gate, grad_attn_part))
+    grad_up_w = [
+        einf("rd,rf->df", expert_in[j][0], grad_up_in[j]).astype(bf16) for j in range(local_experts)
+    ]
     grad_up_w, grad_attn_part = lax.optimization_barrier((grad_up_w, grad_attn_part))
     grad_attn_in, out_home = scatter_sum(
         grad_attn_part, groups, replicas, 5, riders=[Deal(to_deal(out_seq), groups, replicas)]
     )
-    grad_attn_in, attn_share = lax.optimization_barrier((grad_attn_in, attn_share))
     grad_input_norm, grad_attn_g = norm_back(inputs, inv_first, attn_g, grad_attn_in, 0)
     grad_seq = (grad_hidden + grad_input_norm).astype(bf16)
 
@@ -1437,6 +1466,7 @@
     pad = -pieces.shape[1] % 1024
     pieces = jnp.pad(pieces, ((0, 0), (0, pad))).reshape(groups, -1, 128)
 
+    pieces, grad_seq, attn_share = lax.optimization_barrier((pieces, grad_seq, attn_share))
     attn_sum, total_up, sum_small, grad_home = close(
         attn_share,
         3 * local_width,
@@ -1446,14 +1476,13 @@
         7,
         [SmallSum(pieces, groups, replicas), Deal(to_deal(grad_seq), groups, replicas)],
     )
-    grad_input = to_deal(grad_home)[order_row].reshape(tok_rows, width).astype(f32)
-    output = to_deal(out_home)[order_row].reshape(tok_rows, width)
-    sum_q, sum_k, sum_v, sum_o = assemble(attn_sum)
+    sum_q, sum_k, sum_v, sum_o, grad_input, output, total_up = assemble(
+        order_row, attn_sum, to_deal(grad_home), to_deal(out_home), total_up
+    )
     sum_small = sum_small.reshape(-1)
     sum_r = sum_small[:n_router].reshape(shard_rows, experts)
     sum_ga, sum_gm, sum_gq, sum_gk = (sum_small[cuts[i] : cuts[i + 1]] for i in range(1, 5))
     total_down = jnp.stack(total_down).astype(f32)
-    total_gate = total_gate.astype(f32)
     return (
         output,
         balance_loss,

time: 926 us -> 922 us (level)
  local copies, waits for them, and re-layouts: 49 us -> 33 us
  Pallas kernels: 749 us -> 763 us
  waiting for transfers between devices: 15.4 us -> 4.03 us
    reduce_scatter x1, waiting for transfers between devices: 15.3 us -> 3.94 us  [body(): lax.psum_scatter(grad_attn_w.reshape(groups, shard_rows, 4 * local_width)...]
    unnamed x57 -> x51, local copies, waits for them, and re-layouts: 17 us -> 5.98 us
    dot_general x8 -> x10, matrix products: 56.3 us -> 60 us  [einf(): return jnp.einsum(spec, left, right, preferred_element_type=f32)]
  transfers between devices with their start and end apart: 5 -> 5, of which waited for: 1 -> 1; matrix products, arithmetic and copies ran while one was open for 9% -> 11% of each run, Pallas kernels for 47% -> 47%
where the time goes in v5:
time: 922 us; the launch traced here: 917 us
  Pallas kernels  763 us (83%)
  matrix products  60 us (7%)
  other arithmetic  38.6 us (4%)
  local copies, waits for them, and re-layouts  33 us (4%)
  between operations  18.7 us (2%)
    pallas_call x8, Pallas kernels, riding_call(): pl.pallas_call(functools.partial(riding_kernel, n, replicas, main, counts...  523 us
    dot_general x10, matrix products, einf(): return jnp.einsum(spec, left, right, preferred_element_type=f32)  60 us
    pallas_call x1, Pallas kernels, expert_back(): pl.pallas_call(functools.partial(expert_back_kernel, capacity), out_shape...  49.1 us
    pallas_call x1, Pallas kernels, attend_back(): pl.pallas_call(functools.partial(attend_back_kernel, wide // head_dim, he...  46.3 us
    pallas_call x1, Pallas kernels, front(): pl.pallas_call(functools.partial(front_kernel, n, replicas), out_shape=[j...  43.2 us
    pallas_call x2, Pallas kernels, expert_forward(): pl.pallas_call(functools.partial(expert_in_kernel, capacity), out_shape=[...  42.9 us
    pallas_call x1, Pallas kernels, attend(): pl.pallas_call(functools.partial(attend_kernel, wide // head_dim, head_di...  23.9 us
    pallas_call x1, Pallas kernels, expert_combine(): pl.pallas_call(functools.partial(expert_out_kernel, capacity), out_shape=...  23.4 us
  transfers between devices with their start and end apart: 5, of which 1 were waited for; matrix products, arithmetic and copies ran while one was open for 11% of the time, Pallas kernels for 47%

profile of v5, /device:TPU:0, one launch (start us, length us, event | category | flops | bytes accessed | tf_op | source)
XLA Modules:
  0.0 917.1 jit_solution(12084976698564054661)
XLA Ops:
  8.0 0.9 dynamic-slice_reduce_fusion.order_ref
  9.5 0.8 copy.65
  10.4 2.8 concatenate.18
  13.8 0.8 copy.66
  14.7 1.6 gather_fusion.1
  16.3 1.6 gather_fusion
  18.5 43.2 %front.1 = (bf16[8,48,128]{2,1,0:T(8,128)(2,1)}, s32[8,24,128]{2,1,0:T(8,128)}, bf16[256,2048]{1,0:T(8,128)(2,1)}, bf16[8,256,768]{2,1,0:T(8,128)(2,1)}) custom-call(bf16[48,128]{1,0:T(8,128)(2,1)} %pad_bitcast_fusion.1.small, s32[24,128]{1,0:T(8,128)} %select_bitcast_fusion.ints, bf16[4,64,2048]{2,1,0:T(8,128)(2,1)} %gather_fusion, bf16[256,2048]{1,0:T(8,128)(2,1)} %wq.1, ...), custom_call_target="tpu_custom_call" | custom-call | bytes 1024 | tf_op jit(solution)/shard_map/front/pallas_call | solution.py:191
  61.7 0.9 copy.97
  62.6 1.5 fusion.46
  64.2 2.5 fusion.40.refs_0_
  66.7 42.5 %gather_rows_1.1 = (bf16[8,256,2048]{2,1,0:T(8,128)(2,1)}, bf16[256,2048]{1,0:T(8,128)(2,1)}) custom-call(bf16[256,2048]{1,0:T(8,128)(2,1)} %fusion.40.refs_0_, bf16[4,64,2048]{2,1,0:T(8,128)(2,1)} %gather_fusion.1), custom_call_target="tpu_custom_call" | custom-call | bytes 1024 | tf_op jit(solution)/shard_map/gather_rows_1/pallas_call | solution.py:597
  109.2 2.4 fusion.50
  114.3 0.6 slice_reduce_fusion.lengths_ref
  115.5 0.8 pad_maximum_fusion.1
  116.3 23.9 %attend.1 = (bf16[8,256,256]{2,1,0:T(8,128)(2,1)}, bf16[8,256,2048]{2,1,0:T(8,128)(2,1)}) custom-call(s32[8]{0:T(128)} %slice_reduce_fusion.lengths_ref, bf16[8,256,2048]{2,1,0:T(8,128)(2,1)} %get-tuple-element.89.x_ref, bf16[2048,768]{1,0:T(8,128)(2,1)} %bitcast.167, bf16[256,2048]{1,0:T(8,128)(2,1)} %wo_ref.3, f32[1,128]{1,0:T(1,128)} %reshape.280.qg_ref, ...), custom_call_target="tpu_custom_call" | custom-call | bytes 1024 | tf_op jit(solution)/shard_map/attend/pallas_call | solution.py:909
  140.2 60.0 %scatter_sum_8.1 = f32[256,2048]{1,0:T(8,128)} custom-call(bf16[8,256,2048]{2,1,0:T(8,128)(2,1)} %get-tuple-element.91.refs_0_), custom_call_target="tpu_custom_call" | custom-call | bytes 1024 | tf_op jit(solution)/shard_map/scatter_sum_8/pallas_call | solution.py:597
  200.2 1.9 multiply_reduce_fusion.2
  202.9 0.6 copy-done.2
  204.0 0.7 reshape.263.refs_1_
  204.7 43.0 %gather_rows_2.1 = (bf16[8,256,2048]{2,1,0:T(8,128)(2,1)}, f32[8,32,128]{2,1,0:T(8,128)}) custom-call(bf16[256,2048]{1,0:T(8,128)(2,1)} %copy-done.6, f32[32,128]{1,0:T(8,128)} %reshape.263.refs_1_), custom_call_target="tpu_custom_call" | custom-call | bytes 1024 | tf_op jit(solution)/shard_map/gather_rows_2/pallas_call | solution.py:597
  247.7 1.2 reshape_reshape.3
  249.8 0.7 broadcast_in_dim.15.slot_ref.refs_6_.refs_3_
  250.4 0.6 broadcast_in_dim.16.gate_ref
  251.0 21.5 %expert_forward.2 = (bf16[1,1152,2048]{2,1,0:T(8,128)(2,1)}, bf16[1,1152,2048]{2,1,0:T(8,128)(2,1)}, bf16[1,1152,1024]{2,1,0:T(8,128)(2,1)}, f32[1,1152,1024]{2,1,0:T(8,128)}, f32[1,1152,1024]{2,1,0:T(8,128)}) custom-call(bf16[8,256,2048]{2,1,0:T(8,128)(2,1)} %get-tuple-element.98.x_ref, bf16[8,256,2048]{2,1,0:T(8,128)(2,1)} %bitcast.164, ...), custom_call_target="tpu_custom_call" | custom-call | bytes 1024 | tf_op jit(solution)/shard_map/expert_forward/pallas_call | solution.py:1100
  272.5 9.6 %fusion.12 = bf16[1024,2048]{1,0:T(8,128)(2,1)} fusion(bf16[1,1152,2048]{2,1,0:T(8,128)(2,1)} %get-tuple-element.97.refs_0_, bf16[1,1152,1024]{2,1,0:T(8,128)(2,1)} %get-tuple-element.113.refs_0_), kind=kOutput, calls=%fused_computation.22 | convolution fusion | flops 4833935360 | bytes 11272192 | tf_op jit(solution)/shard_map/rf,rd->fd/dot_general | solution.py:1259
  282.2 21.4 %expert_forward.3 = (bf16[1,1152,2048]{2,1,0:T(8,128)(2,1)}, bf16[1,1152,2048]{2,1,0:T(8,128)(2,1)}, bf16[1,1152,1024]{2,1,0:T(8,128)(2,1)}, f32[1,1152,1024]{2,1,0:T(8,128)}, f32[1,1152,1024]{2,1,0:T(8,128)}) custom-call(bf16[8,256,2048]{2,1,0:T(8,128)(2,1)} %get-tuple-element.98.x_ref, bf16[8,256,2048]{2,1,0:T(8,128)(2,1)} %bitcast.165, ...), custom_call_target="tpu_custom_call" | custom-call | bytes 1024 | tf_op jit(solution)/shard_map/expert_forward/pallas_call | solution.py:1100
  303.6 9.6 %fusion.15 = bf16[1024,2048]{1,0:T(8,128)(2,1)} fusion(bf16[1,1152,2048]{2,1,0:T(8,128)(2,1)} %get-tuple-element.101.refs_1_, bf16[1,1152,1024]{2,1,0:T(8,128)(2,1)} %get-tuple-element.114.refs_1_), kind=kOutput, calls=%fused_computation.23 | convolution fusion | flops 4833935360 | bytes 11272192 | tf_op jit(solution)/shard_map/rf,rd->fd/dot_general | solution.py:1259
  313.3 49.1 %expert_back.1 = (bf16[2,1152,1024]{2,1,0:T(8,128)(2,1)}, bf16[2,1152,1024]{2,1,0:T(8,128)(2,1)}, bf16[8,256,2048]{2,1,0:T(8,128)(2,1)}) custom-call(bf16[1,1152,2048]{2,1,0:T(8,128)(2,1)} %get-tuple-element.97.refs_0_, bf16[1,1152,2048]{2,1,0:T(8,128)(2,1)} %get-tuple-element.101.refs_1_, f32[1,1152,1024]{2,1,0:T(8,128)} %get-tuple-element.102.refs_2_, ...), custom_call_target="tpu_custom_call" | custom-call | bytes 1024 | tf_op jit(solution)/shard_map/expert_back/pallas_call | solution.py:1194
  362.3 8.7 convert_bitcast_fusion
  371.1 9.7 %convert_bitcast_fusion.1 = bf16[1,2048,1024]{2,1,0:T(8,128)(2,1)} fusion(bf16[1,1152,2048]{2,1,0:T(8,128)(2,1)} %get-tuple-element.109, bf16[2,1152,1024]{2,1,0:T(8,128)(2,1)S(1)} %copy-done.16), kind=kOutput, calls=%fused_computation.16 | convolution fusion | flops 4833935360 | bytes 11272192 | tf_op jit(solution)/shard_map/rd,rf->df/dot_general | solution.py:1259
  380.8 6.1 pad_maximum_fusion
  388.6 2.0 copy.72.refs_4_
  390.7 0.7 fusion.64
  391.5 1.3 fusion.63.refs_2_
  392.8 23.4 %expert_combine.1 = (bf16[8,256,2048]{2,1,0:T(8,128)(2,1)}, f32[2,8,256,1]{3,2,1,0:T(8,128)}) custom-call(bf16[1,1152,1024]{2,1,0:T(8,128)(2,1)} %get-tuple-element.113.refs_0_, bf16[1,1152,1024]{2,1,0:T(8,128)(2,1)} %get-tuple-element.114.refs_1_, bf16[8,256,2048]{2,1,0:T(8,128)(2,1)} %bitcast.166, ...), custom_call_target="tpu_custom_call" | custom-call | bytes 1024 | tf_op jit(solution)/shard_map/expert_combine/pallas_call | solution.py:1143
  416.2 2.2 copy.73
  418.4 0.6 reshape.264.refs_1_
  419.0 43.9 %scatter_sum_3.1 = (f32[256,2048]{1,0:T(8,128)}, f32[8,4,128]{2,1,0:T(4,128)}, f32[8,128]{1,0:T(8,128)}) custom-call(bf16[8,256,2048]{2,1,0:T(8,128)(2,1)} %get-tuple-element.112.refs_0_, f32[8,4,128]{2,1,0:T(4,128)} %reshape.264.refs_1_, f32[8,128]{1,0:T(8,128)} %fusion.63.refs_2_), custom_call_target="tpu_custom_call" | custom-call | bytes 1024 | tf_op jit(solution)/shard_map/scatter_sum_3/pallas_call | solution.py:597
  462.9 0.7 reshape.266
  463.7 1.3 slice.80
  465.6 1.4 multiply_reduce_fusion.6
  467.1 3.3 multiply_reduce_fusion
  470.5 2.5 fusion.70
  473.0 40.4 %gather_rows_4.1.g_ref = bf16[8,256,2048]{2,1,0:T(8,128)(2,1)} custom-call(bf16[256,2048]{1,0:T(8,128)(2,1)} %get-tuple-element.123.refs_0_), custom_call_target="tpu_custom_call" | custom-call | bytes 1024 | tf_op jit(solution)/shard_map/gather_rows_4/pallas_call | solution.py:597
  513.4 46.3 %attend_back.1 = (bf16[8,256,2048]{2,1,0:T(8,128)(2,1)}, bf16[2048,1024]{1,0:T(8,128)(2,1)}, f32[8,128]{1,0:T(8,128)}) custom-call(s32[8]{0:T(128)} %slice_reduce_fusion.lengths_ref, bf16[8,256,2048]{2,1,0:T(8,128)(2,1)} %get-tuple-element.89.x_ref, bf16[8,256,2048]{2,1,0:T(8,128)(2,1)} %gather_rows_4.1.g_ref, ...), custom_call_target="tpu_custom_call" | custom-call | bytes 1024 | tf_op jit(solution)/shard_map/attend_back/pallas_call | solution.py:1019
  561.4 0.6 reshape.268
  562.0 41.2 %scatter_sum_6.1 = f32[256,2048]{1,0:T(8,128)} custom-call(bf16[8,256,2048]{2,1,0:T(8,128)(2,1)} %get-tuple-element.126.refs_0_), custom_call_target="tpu_custom_call" | custom-call | bytes 1024 | tf_op jit(solution)/shard_map/scatter_sum_6/pallas_call | solution.py:597
  603.2 0.8 slice_reduce_fusion.1
  604.2 4.0 maximum_convert_fusion
  608.2 1.2 multiply_convert_fusion
  609.4 4.3 convert_element_type.188
  613.7 10.3 %fusion.25.refs_2_ = bf16[2048,1024]{1,0:T(8,128)(2,1)} fusion(bf16[1,1152,2048]{2,1,0:T(8,128)(2,1)} %get-tuple-element.111, bf16[2,1152,1024]{2,1,0:T(8,128)(2,1)} %get-tuple-element.128), kind=kOutput, calls=%fused_computation.25 | convolution fusion | flops 4833935360 | bytes 11272192 | tf_op jit(solution)/shard_map/rd,rf->df/dot_general | solution.py:1259
  624.1 7.5 fusion.20.refs_1_
  631.6 42.1 %scatter_sum_5.1 = (f32[256,2048]{1,0:T(8,128)}, bf16[256,2048]{1,0:T(8,128)(2,1)}) custom-call(bf16[8,256,2048]{2,1,0:T(8,128)(2,1)} %get-tuple-element.132.refs_0_, bf16[4,64,2048]{2,1,0:T(8,128)(2,1)} %bitcast.170), custom_call_target="tpu_custom_call" | custom-call | bytes 1024 | tf_op jit(solution)/shard_map/scatter_sum_5/pallas_call | solution.py:597
  673.8 2.3 fusion.49
  676.2 0.7 copy.96
  676.9 3.2 fusion.45
  680.1 3.9 reduce-scatter.11.cloned.1.call-done.refs_0_
  684.0 210.0 %close.1 = (bf16[4,8,64,1024]{3,2,1,0:T(8,128)(2,1)}, f32[2,512,1024]{2,1,0:T(8,128)}, f32[40,128]{1,0:T(8,128)}, bf16[256,2048]{1,0:T(8,128)(2,1)}) custom-call(bf16[8,64,1024]{2,1,0:T(8,128)(2,1)} %reduce-scatter.11.cloned.1.call-done.refs_0_, bf16[2048,1024]{1,0:T(8,128)(2,1)} %fusion.20.refs_1_, bf16[2048,1024]{1,0:T(8,128)(2,1)} %fusion.25.refs_2_, ...), custom_call_target="tpu_custom_call" | custom-call | bytes 1024 | tf_op jit(solution)/shard_map/close/pallas_call | solution.py:597
  894.1 1.3 slice_bitcast_fusion
  895.4 0.7 slice.86
  896.1 1.3 fusion.71
  897.6 0.7 copy.76
  898.2 10.8 %assemble.1 = (f32[256,2048]{1,0:T(8,128)}, f32[256,2048]{1,0:T(8,128)}, f32[256,2048]{1,0:T(8,128)}, f32[256,2048]{1,0:T(8,128)}, f32[256,2048]{1,0:T(8,128)}, ...) custom-call(s32[4]{0:T(128)} %copy-done.15, bf16[4,8,64,1024]{3,2,1,0:T(8,128)(2,1)} %get-tuple-element.142.x_ref, ...), custom_call_target="tpu_custom_call" | custom-call | bytes 1024 | tf_op jit(solution)/shard_map/assemble/pallas_call | solution.py:1230
  (115 shorter events, 9.9 us)
Async XLA Ops:
  7.2 7.6 copy-start
  7.2 9.1 copy-start.11
  7.2 243.8 %all-gather.3.cloned.1.call-start = ((), (), s32[]{:S(2)}) async-start(), calls=%async_computation.8 | async-start | bytes 9437184 | tf_op jit(solution)/shard_map/all_gather | solution.py:1343
  8.9 0.6 copy-start.15
  66.7 45.0 %copy-start.13 = (s32[8,24,128]{2,1,0:T(8,128)S(1)}, s32[8,24,128]{2,1,0:T(8,128)}, u32[]{:S(2)}) copy-start(s32[8,24,128]{2,1,0:T(8,128)} %get-tuple-element.87) | copy-start | bytes 294916
  111.6 361.3 %reduce-scatter.5.cloned.1.call-start = ((), (), s32[]{:S(2)}) async-start(), calls=%async_computation.4 | async-start | bytes 5242880 | tf_op jit(solution)/shard_map/reduce_scatter | solution.py:1388
  140.2 60.0 %copy-start.5 = (bf16[256,2048]{1,0:T(8,128)(2,1)S(1)}, bf16[256,2048]{1,0:T(8,128)(2,1)}, u32[]{:S(2)}) copy-start(bf16[256,2048]{1,0:T(8,128)(2,1)} %get-tuple-element.86) | copy-start | bytes 3145732
  202.2 1.3 copy-start.2
  202.5 1.4 copy-start.6
  282.1 190.8 %reduce-scatter.7.cloned.1.call-start = ((), (), s32[]{:S(2)}) async-start(), calls=%async_computation.5 | async-start | bytes 5242880 | tf_op jit(solution)/shard_map/reduce_scatter | solution.py:1388
  313.2 296.1 %reduce-scatter.9.cloned.1.call-start = ((), (), s32[]{:S(2)}) async-start(), calls=%async_computation.6 | async-start | bytes 10485760 | tf_op jit(solution)/shard_map/reduce_scatter | solution.py:1400
  362.3 8.8 copy-start.16
  387.0 0.8 copy-start.14
  387.0 1.5 copy-start.12
  387.0 297.0 %reduce-scatter.11.cloned.1.call-start = ((), (), s32[]{:S(2)}) async-start(), calls=%async_computation.7 | async-start | bytes 5242880 | tf_op jit(solution)/shard_map/reduce_scatter | solution.py:1439
  467.1 3.3 copy-start.3
  467.1 3.4 copy-start.10
  559.7 1.2 copy-start.7
  604.1 4.0 copy-start.4
  604.2 4.0 copy-start.9
  609.4 14.7 %slice-start = ((s8[4718592]{0:T(1024)(128)(4,1)}), s8[4194304]{0:T(1024)(128)(4,1)S(1)}, s32[]{:S(2)}) async-start(s8[4718592]{0:T(1024)(128)(4,1)} %bitcast.198), calls=%async_computation.9 | async-start | bytes 8388608
  609.4 14.7 %slice-start.2 = ((s8[4718592]{0:T(1024)(128)(4,1)}), s8[4194304]{0:T(1024)(128)(4,1)S(1)}, s32[]{:S(2)}) async-start(s8[4718592]{0:T(1024)(128)(4,1)} %bitcast.200), calls=%async_computation.11 | async-start | bytes 8388608
  613.7 10.3 %slice-start.1 = ((s8[4718592]{0:T(1024)(128)(4,1)}), s8[524288]{0:T(1024)(128)(4,1)S(1)}, s32[]{:S(2)}) async-start(s8[4718592]{0:T(1024)(128)(4,1)} %bitcast.198), calls=%async_computation.10 | async-start | bytes 1048576
  613.7 10.3 %slice-start.3 = ((s8[4718592]{0:T(1024)(128)(4,1)}), s8[524288]{0:T(1024)(128)(4,1)S(1)}, s32[]{:S(2)}) async-start(s8[4718592]{0:T(1024)(128)(4,1)} %bitcast.200), calls=%async_computation.12 | async-start | bytes 1048576
  673.8 3.1 copy-start.8
  898.2 10.8 %copy-start.1 = (bf16[256,2048]{1,0:T(8,128)(2,1)S(1)}, bf16[256,2048]{1,0:T(8,128)(2,1)}, u32[]{:S(2)}) copy-start(bf16[256,2048]{1,0:T(8,128)(2,1)} %param.19) | copy-start | bytes 3145732
Sparse Core Ops, SparseCore 0:
  111.8 72.0 all-gather.2
  282.2 76.8 reduce-scatter.4
  362.2 77.5 reduce-scatter.6
  441.9 144.9 reduce-scatter.8
  589.7 94.3 reduce-scatter.10

commit v6 on v5

--- a/solution.py
+++ b/solution.py
@@ -413,7 +413,7 @@
 
 
 class LineSum:
-    def __init__(self, values, n, replicas, parts=4):
+    def __init__(self, values, n, replicas, parts=8):
         self.replicas, self.parts = replicas, parts
         self.blocks = len(values)
         rows, columns = values[0].shape
@@ -521,8 +521,10 @@
     exchange.finish(me)
     gather.start(me, rows, full, *gather_refs)
     running.append(gather.steps(rows, full, *gather_refs))
+    turn = 0
     while running:
-        running = [r for r in running if next(r, True) is None]
+        turn += 1
+        running = [r for i, r in enumerate(running) if (i and turn % 2) or next(r, True) is None]
 
 
 def close(attn_share, columns, grad_up_w, n, replicas, collective_id, riders):

time: 922 us -> 930 us (level)
  no operation moved by 1% of the time
where the time goes in v6:
time: 930 us; the launch traced here: 925 us
  Pallas kernels  771 us (83%)
  matrix products  60 us (6%)
  other arithmetic  38.6 us (4%)
  local copies, waits for them, and re-layouts  33 us (4%)
  between operations  18.7 us (2%)
    pallas_call x8, Pallas kernels, riding_call(): pl.pallas_call(functools.partial(riding_kernel, n, replicas, main, counts...  531 us
    dot_general x10, matrix products, einf(): return jnp.einsum(spec, left, right, preferred_element_type=f32)  60 us
    pallas_call x1, Pallas kernels, expert_back(): pl.pallas_call(functools.partial(expert_back_kernel, capacity), out_shape...  49.1 us
    pallas_call x1, Pallas kernels, attend_back(): pl.pallas_call(functools.partial(attend_back_kernel, wide // head_dim, he...  46.3 us
    pallas_call x1, Pallas kernels, front(): pl.pallas_call(functools.partial(front_kernel, n, replicas), out_shape=[j...  43.2 us
    pallas_call x2, Pallas kernels, expert_forward(): pl.pallas_call(functools.partial(expert_in_kernel, capacity), out_shape=[...  42.9 us
    pallas_call x1, Pallas kernels, attend(): pl.pallas_call(functools.partial(attend_kernel, wide // head_dim, head_di...  23.9 us
    pallas_call x1, Pallas kernels, expert_combine(): pl.pallas_call(functools.partial(expert_out_kernel, capacity), out_shape=...  23.4 us
  transfers between devices with their start and end apart: 5, of which 1 were waited for; matrix products, arithmetic and copies ran while one was open for 11% of the time, Pallas kernels for 47%

profile of v6, /device:TPU:0, one launch (start us, length us, event | category | flops | bytes accessed | tf_op | source)
XLA Modules:
  0.0 925.3 jit_solution(3683426143709419198)
XLA Ops:
  8.0 0.9 dynamic-slice_reduce_fusion.order_ref
  9.5 0.8 copy.65
  10.4 2.8 concatenate.18
  13.8 0.8 copy.66
  14.7 1.6 gather_fusion.1
  16.3 1.6 gather_fusion
  18.5 43.2 %front.1 = (bf16[8,48,128]{2,1,0:T(8,128)(2,1)}, s32[8,24,128]{2,1,0:T(8,128)}, bf16[256,2048]{1,0:T(8,128)(2,1)}, bf16[8,256,768]{2,1,0:T(8,128)(2,1)}) custom-call(bf16[48,128]{1,0:T(8,128)(2,1)} %pad_bitcast_fusion.1.small, s32[24,128]{1,0:T(8,128)} %select_bitcast_fusion.ints, bf16[4,64,2048]{2,1,0:T(8,128)(2,1)} %gather_fusion, bf16[256,2048]{1,0:T(8,128)(2,1)} %wq.1, ...), custom_call_target="tpu_custom_call" | custom-call | bytes 1024 | tf_op jit(solution)/shard_map/front/pallas_call | solution.py:191
  61.7 0.9 copy.97
  62.6 1.5 fusion.46
  64.2 2.5 fusion.40.refs_0_
  66.7 42.5 %gather_rows_1.1 = (bf16[8,256,2048]{2,1,0:T(8,128)(2,1)}, bf16[256,2048]{1,0:T(8,128)(2,1)}) custom-call(bf16[256,2048]{1,0:T(8,128)(2,1)} %fusion.40.refs_0_, bf16[4,64,2048]{2,1,0:T(8,128)(2,1)} %gather_fusion.1), custom_call_target="tpu_custom_call" | custom-call | bytes 1024 | tf_op jit(solution)/shard_map/gather_rows_1/pallas_call | solution.py:599
  109.2 2.4 fusion.50
  114.3 0.6 slice_reduce_fusion.lengths_ref
  115.5 0.8 pad_maximum_fusion.1
  116.3 23.9 %attend.1 = (bf16[8,256,256]{2,1,0:T(8,128)(2,1)}, bf16[8,256,2048]{2,1,0:T(8,128)(2,1)}) custom-call(s32[8]{0:T(128)} %slice_reduce_fusion.lengths_ref, bf16[8,256,2048]{2,1,0:T(8,128)(2,1)} %get-tuple-element.89.x_ref, bf16[2048,768]{1,0:T(8,128)(2,1)} %bitcast.167, bf16[256,2048]{1,0:T(8,128)(2,1)} %wo_ref.3, f32[1,128]{1,0:T(1,128)} %reshape.280.qg_ref, ...), custom_call_target="tpu_custom_call" | custom-call | bytes 1024 | tf_op jit(solution)/shard_map/attend/pallas_call | solution.py:911
  140.2 60.0 %scatter_sum_8.1 = f32[256,2048]{1,0:T(8,128)} custom-call(bf16[8,256,2048]{2,1,0:T(8,128)(2,1)} %get-tuple-element.91.refs_0_), custom_call_target="tpu_custom_call" | custom-call | bytes 1024 | tf_op jit(solution)/shard_map/scatter_sum_8/pallas_call | solution.py:599
  200.2 1.9 multiply_reduce_fusion.2
  202.9 0.6 copy-done.2
  204.0 0.7 reshape.263.refs_1_
  204.7 43.0 %gather_rows_2.1 = (bf16[8,256,2048]{2,1,0:T(8,128)(2,1)}, f32[8,32,128]{2,1,0:T(8,128)}) custom-call(bf16[256,2048]{1,0:T(8,128)(2,1)} %copy-done.6, f32[32,128]{1,0:T(8,128)} %reshape.263.refs_1_), custom_call_target="tpu_custom_call" | custom-call | bytes 1024 | tf_op jit(solution)/shard_map/gather_rows_2/pallas_call | solution.py:599
  247.7 1.2 reshape_reshape.3
  249.8 0.7 broadcast_in_dim.15.slot_ref.refs_6_.refs_3_
  250.4 0.6 broadcast_in_dim.16.gate_ref
  251.0 21.5 %expert_forward.2 = (bf16[1,1152,2048]{2,1,0:T(8,128)(2,1)}, bf16[1,1152,2048]{2,1,0:T(8,128)(2,1)}, bf16[1,1152,1024]{2,1,0:T(8,128)(2,1)}, f32[1,1152,1024]{2,1,0:T(8,128)}, f32[1,1152,1024]{2,1,0:T(8,128)}) custom-call(bf16[8,256,2048]{2,1,0:T(8,128)(2,1)} %get-tuple-element.98.x_ref, bf16[8,256,2048]{2,1,0:T(8,128)(2,1)} %bitcast.164, ...), custom_call_target="tpu_custom_call" | custom-call | bytes 1024 | tf_op jit(solution)/shard_map/expert_forward/pallas_call | solution.py:1102
  272.5 9.6 %fusion.12 = bf16[1024,2048]{1,0:T(8,128)(2,1)} fusion(bf16[1,1152,2048]{2,1,0:T(8,128)(2,1)} %get-tuple-element.97.refs_0_, bf16[1,1152,1024]{2,1,0:T(8,128)(2,1)} %get-tuple-element.113.refs_0_), kind=kOutput, calls=%fused_computation.22 | convolution fusion | flops 4833935360 | bytes 11272192 | tf_op jit(solution)/shard_map/rf,rd->fd/dot_general | solution.py:1261
  282.2 21.4 %expert_forward.3 = (bf16[1,1152,2048]{2,1,0:T(8,128)(2,1)}, bf16[1,1152,2048]{2,1,0:T(8,128)(2,1)}, bf16[1,1152,1024]{2,1,0:T(8,128)(2,1)}, f32[1,1152,1024]{2,1,0:T(8,128)}, f32[1,1152,1024]{2,1,0:T(8,128)}) custom-call(bf16[8,256,2048]{2,1,0:T(8,128)(2,1)} %get-tuple-element.98.x_ref, bf16[8,256,2048]{2,1,0:T(8,128)(2,1)} %bitcast.165, ...), custom_call_target="tpu_custom_call" | custom-call | bytes 1024 | tf_op jit(solution)/shard_map/expert_forward/pallas_call | solution.py:1102
  303.6 9.6 %fusion.15 = bf16[1024,2048]{1,0:T(8,128)(2,1)} fusion(bf16[1,1152,2048]{2,1,0:T(8,128)(2,1)} %get-tuple-element.101.refs_1_, bf16[1,1152,1024]{2,1,0:T(8,128)(2,1)} %get-tuple-element.114.refs_1_), kind=kOutput, calls=%fused_computation.23 | convolution fusion | flops 4833935360 | bytes 11272192 | tf_op jit(solution)/shard_map/rf,rd->fd/dot_general | solution.py:1261
  313.3 49.1 %expert_back.1 = (bf16[2,1152,1024]{2,1,0:T(8,128)(2,1)}, bf16[2,1152,1024]{2,1,0:T(8,128)(2,1)}, bf16[8,256,2048]{2,1,0:T(8,128)(2,1)}) custom-call(bf16[1,1152,2048]{2,1,0:T(8,128)(2,1)} %get-tuple-element.97.refs_0_, bf16[1,1152,2048]{2,1,0:T(8,128)(2,1)} %get-tuple-element.101.refs_1_, f32[1,1152,1024]{2,1,0:T(8,128)} %get-tuple-element.102.refs_2_, ...), custom_call_target="tpu_custom_call" | custom-call | bytes 1024 | tf_op jit(solution)/shard_map/expert_back/pallas_call | solution.py:1196
  362.3 8.7 convert_bitcast_fusion
  371.1 9.7 %convert_bitcast_fusion.1 = bf16[1,2048,1024]{2,1,0:T(8,128)(2,1)} fusion(bf16[1,1152,2048]{2,1,0:T(8,128)(2,1)} %get-tuple-element.109, bf16[2,1152,1024]{2,1,0:T(8,128)(2,1)S(1)} %copy-done.16), kind=kOutput, calls=%fused_computation.16 | convolution fusion | flops 4833935360 | bytes 11272192 | tf_op jit(solution)/shard_map/rd,rf->df/dot_general | solution.py:1261
  380.8 6.1 pad_maximum_fusion
  388.6 2.0 copy.72.refs_4_
  390.7 0.7 fusion.64
  391.5 1.3 fusion.63.refs_2_
  392.8 23.4 %expert_combine.1 = (bf16[8,256,2048]{2,1,0:T(8,128)(2,1)}, f32[2,8,256,1]{3,2,1,0:T(8,128)}) custom-call(bf16[1,1152,1024]{2,1,0:T(8,128)(2,1)} %get-tuple-element.113.refs_0_, bf16[1,1152,1024]{2,1,0:T(8,128)(2,1)} %get-tuple-element.114.refs_1_, bf16[8,256,2048]{2,1,0:T(8,128)(2,1)} %bitcast.166, ...), custom_call_target="tpu_custom_call" | custom-call | bytes 1024 | tf_op jit(solution)/shard_map/expert_combine/pallas_call | solution.py:1145
  416.2 2.2 copy.73
  418.4 0.6 reshape.264.refs_1_
  419.0 43.9 %scatter_sum_3.1 = (f32[256,2048]{1,0:T(8,128)}, f32[8,4,128]{2,1,0:T(4,128)}, f32[8,128]{1,0:T(8,128)}) custom-call(bf16[8,256,2048]{2,1,0:T(8,128)(2,1)} %get-tuple-element.112.refs_0_, f32[8,4,128]{2,1,0:T(4,128)} %reshape.264.refs_1_, f32[8,128]{1,0:T(8,128)} %fusion.63.refs_2_), custom_call_target="tpu_custom_call" | custom-call | bytes 1024 | tf_op jit(solution)/shard_map/scatter_sum_3/pallas_call | solution.py:599
  462.9 0.7 reshape.266
  463.7 1.3 slice.80
  465.6 1.4 multiply_reduce_fusion.6
  467.1 3.3 multiply_reduce_fusion
  470.5 2.5 fusion.70
  473.0 40.4 %gather_rows_4.1.g_ref = bf16[8,256,2048]{2,1,0:T(8,128)(2,1)} custom-call(bf16[256,2048]{1,0:T(8,128)(2,1)} %get-tuple-element.123.refs_0_), custom_call_target="tpu_custom_call" | custom-call | bytes 1024 | tf_op jit(solution)/shard_map/gather_rows_4/pallas_call | solution.py:599
  513.4 46.3 %attend_back.1 = (bf16[8,256,2048]{2,1,0:T(8,128)(2,1)}, bf16[2048,1024]{1,0:T(8,128)(2,1)}, f32[8,128]{1,0:T(8,128)}) custom-call(s32[8]{0:T(128)} %slice_reduce_fusion.lengths_ref, bf16[8,256,2048]{2,1,0:T(8,128)(2,1)} %get-tuple-element.89.x_ref, bf16[8,256,2048]{2,1,0:T(8,128)(2,1)} %gather_rows_4.1.g_ref, ...), custom_call_target="tpu_custom_call" | custom-call | bytes 1024 | tf_op jit(solution)/shard_map/attend_back/pallas_call | solution.py:1021
  561.4 0.6 reshape.268
  562.0 41.2 %scatter_sum_6.1 = f32[256,2048]{1,0:T(8,128)} custom-call(bf16[8,256,2048]{2,1,0:T(8,128)(2,1)} %get-tuple-element.126.refs_0_), custom_call_target="tpu_custom_call" | custom-call | bytes 1024 | tf_op jit(solution)/shard_map/scatter_sum_6/pallas_call | solution.py:599
  603.2 0.8 slice_reduce_fusion.1
  604.2 4.0 maximum_convert_fusion
  608.2 1.2 multiply_convert_fusion
  609.4 4.3 convert_element_type.188
  613.7 10.3 %fusion.25.refs_2_ = bf16[2048,1024]{1,0:T(8,128)(2,1)} fusion(bf16[1,1152,2048]{2,1,0:T(8,128)(2,1)} %get-tuple-element.111, bf16[2,1152,1024]{2,1,0:T(8,128)(2,1)} %get-tuple-element.128), kind=kOutput, calls=%fused_computation.25 | convolution fusion | flops 4833935360 | bytes 11272192 | tf_op jit(solution)/shard_map/rd,rf->df/dot_general | solution.py:1261
  624.1 7.5 fusion.20.refs_1_
  631.6 42.1 %scatter_sum_5.1 = (f32[256,2048]{1,0:T(8,128)}, bf16[256,2048]{1,0:T(8,128)(2,1)}) custom-call(bf16[8,256,2048]{2,1,0:T(8,128)(2,1)} %get-tuple-element.132.refs_0_, bf16[4,64,2048]{2,1,0:T(8,128)(2,1)} %bitcast.170), custom_call_target="tpu_custom_call" | custom-call | bytes 1024 | tf_op jit(solution)/shard_map/scatter_sum_5/pallas_call | solution.py:599
  673.8 2.3 fusion.49
  676.2 0.7 copy.96
  676.9 3.2 fusion.45
  680.1 3.9 reduce-scatter.11.cloned.1.call-done.refs_0_
  684.0 218.2 %close.1 = (bf16[4,8,64,1024]{3,2,1,0:T(8,128)(2,1)}, f32[2,512,1024]{2,1,0:T(8,128)}, f32[40,128]{1,0:T(8,128)}, bf16[256,2048]{1,0:T(8,128)(2,1)}) custom-call(bf16[8,64,1024]{2,1,0:T(8,128)(2,1)} %reduce-scatter.11.cloned.1.call-done.refs_0_, bf16[2048,1024]{1,0:T(8,128)(2,1)} %fusion.20.refs_1_, bf16[2048,1024]{1,0:T(8,128)(2,1)} %fusion.25.refs_2_, ...), custom_call_target="tpu_custom_call" | custom-call | bytes 1024 | tf_op jit(solution)/shard_map/close/pallas_call | solution.py:599
  902.2 1.3 slice_bitcast_fusion
  903.6 0.7 slice.86
  904.3 1.3 fusion.71
  905.7 0.7 copy.76
  906.4 10.8 %assemble.1 = (f32[256,2048]{1,0:T(8,128)}, f32[256,2048]{1,0:T(8,128)}, f32[256,2048]{1,0:T(8,128)}, f32[256,2048]{1,0:T(8,128)}, f32[256,2048]{1,0:T(8,128)}, ...) custom-call(s32[4]{0:T(128)} %copy-done.15, bf16[4,8,64,1024]{3,2,1,0:T(8,128)(2,1)} %get-tuple-element.142.x_ref, ...), custom_call_target="tpu_custom_call" | custom-call | bytes 1024 | tf_op jit(solution)/shard_map/assemble/pallas_call | solution.py:1232
  (115 shorter events, 9.9 us)
Async XLA Ops:
  7.2 7.6 copy-start
  7.2 9.1 copy-start.11
  7.2 243.8 %all-gather.3.cloned.1.call-start = ((), (), s32[]{:S(2)}) async-start(), calls=%async_computation.8 | async-start | bytes 9437184 | tf_op jit(solution)/shard_map/all_gather | solution.py:1345
  8.9 0.6 copy-start.15
  66.7 45.0 %copy-start.13 = (s32[8,24,128]{2,1,0:T(8,128)S(1)}, s32[8,24,128]{2,1,0:T(8,128)}, u32[]{:S(2)}) copy-start(s32[8,24,128]{2,1,0:T(8,128)} %get-tuple-element.87) | copy-start | bytes 294916
  111.6 361.3 %reduce-scatter.5.cloned.1.call-start = ((), (), s32[]{:S(2)}) async-start(), calls=%async_computation.4 | async-start | bytes 5242880 | tf_op jit(solution)/shard_map/reduce_scatter | solution.py:1390
  140.2 60.0 %copy-start.5 = (bf16[256,2048]{1,0:T(8,128)(2,1)S(1)}, bf16[256,2048]{1,0:T(8,128)(2,1)}, u32[]{:S(2)}) copy-start(bf16[256,2048]{1,0:T(8,128)(2,1)} %get-tuple-element.86) | copy-start | bytes 3145732
  202.2 1.3 copy-start.2
  202.5 1.4 copy-start.6
  282.1 190.8 %reduce-scatter.7.cloned.1.call-start = ((), (), s32[]{:S(2)}) async-start(), calls=%async_computation.5 | async-start | bytes 5242880 | tf_op jit(solution)/shard_map/reduce_scatter | solution.py:1390
  313.2 296.1 %reduce-scatter.9.cloned.1.call-start = ((), (), s32[]{:S(2)}) async-start(), calls=%async_computation.6 | async-start | bytes 10485760 | tf_op jit(solution)/shard_map/reduce_scatter | solution.py:1402
  362.3 8.8 copy-start.16
  387.0 0.8 copy-start.14
  387.0 1.5 copy-start.12
  387.0 297.0 %reduce-scatter.11.cloned.1.call-start = ((), (), s32[]{:S(2)}) async-start(), calls=%async_computation.7 | async-start | bytes 5242880 | tf_op jit(solution)/shard_map/reduce_scatter | solution.py:1441
  467.1 3.3 copy-start.3
  467.1 3.4 copy-start.10
  559.7 1.2 copy-start.7
  604.1 4.0 copy-start.4
  604.2 4.0 copy-start.9
  609.4 14.7 %slice-start = ((s8[4718592]{0:T(1024)(128)(4,1)}), s8[4194304]{0:T(1024)(128)(4,1)S(1)}, s32[]{:S(2)}) async-start(s8[4718592]{0:T(1024)(128)(4,1)} %bitcast.198), calls=%async_computation.9 | async-start | bytes 8388608
  609.4 14.7 %slice-start.2 = ((s8[4718592]{0:T(1024)(128)(4,1)}), s8[4194304]{0:T(1024)(128)(4,1)S(1)}, s32[]{:S(2)}) async-start(s8[4718592]{0:T(1024)(128)(4,1)} %bitcast.200), calls=%async_computation.11 | async-start | bytes 8388608
  613.7 10.3 %slice-start.1 = ((s8[4718592]{0:T(1024)(128)(4,1)}), s8[524288]{0:T(1024)(128)(4,1)S(1)}, s32[]{:S(2)}) async-start(s8[4718592]{0:T(1024)(128)(4,1)} %bitcast.198), calls=%async_computation.10 | async-start | bytes 1048576
  613.7 10.3 %slice-start.3 = ((s8[4718592]{0:T(1024)(128)(4,1)}), s8[524288]{0:T(1024)(128)(4,1)S(1)}, s32[]{:S(2)}) async-start(s8[4718592]{0:T(1024)(128)(4,1)} %bitcast.200), calls=%async_computation.12 | async-start | bytes 1048576
  673.8 3.1 copy-start.8
  906.4 10.8 %copy-start.1 = (bf16[256,2048]{1,0:T(8,128)(2,1)S(1)}, bf16[256,2048]{1,0:T(8,128)(2,1)}, u32[]{:S(2)}) copy-start(bf16[256,2048]{1,0:T(8,128)(2,1)} %param.19) | copy-start | bytes 3145732
Sparse Core Ops, SparseCore 0:
  111.8 72.0 all-gather.2
  282.2 76.8 reduce-scatter.4
  362.2 77.5 reduce-scatter.6
  441.9 144.9 reduce-scatter.8
  589.7 94.3 reduce-scatter.10
